TPU v7x, 1024 devices: a whole 4x4x32 slice. The times are simulated.
1024 devices in a mesh: gx: 64 (over z, x_hi), gy: 16 (over y, x_lo, core).
Axes of the slice: x: 4 (x_hi: 2, x_lo: 2; x = x_hi * 2 + x_lo), y: 4, z: 32, core: 2. Of those that a mesh axis runs over, the one named last changes fastest.
Arguments:
- right_side: float32 [512, 256, 256], P('gx', 'gy'), may hold values from -8 to 8
- shift: float32 [512, 256, 256], P('gx', 'gy'), may hold values from 0.05 to 0.5
- coef_x: float32 [512, 256, 256], P('gx', 'gy'), may hold values from 0.5 to 2
- coef_y: float32 [512, 256, 256], P('gx', 'gy'), may hold values from 0.5 to 2
- coef_z: float32 [512, 256, 256], P('gx', 'gy'), may hold values from 0.5 to 2
- low_frac: float32 [2], replicated, may hold values from 0.01 to 0.05
- high_frac: float32 [2], replicated, may hold values from 1 to 1.3
Outputs:
- pressure: float32 [512, 256, 256], P('gx', 'gy')
- residual: float32 [512, 256, 256], P('gx', 'gy')
All inputs are finite; a program needn't handle non-finite values.
Results may differ from a plain program's by a relative error of at most 0.000065.
Values sent between devices are 32-bit elements; how exact they have to be, the bound alone decides.
No kernel may reach another device: no remote copies, remote signals or barrier semaphores. Data moves between devices by JAX's collectives and lax.ppermute only.
A program may use at most 32 MiB of HBM per device.

v0:
```python
import jax
import jax.numpy as jnp
from jax import lax
from jax.sharding import Mesh
from jax.sharding import PartitionSpec as P

ITERS = 8
GX_GY = ("gx_0", "gx_1", "gy_0", "gy_1", "gy_2")
GX = ("gx_0", "gx_1")
GY = ("gy_0", "gy_1", "gy_2")


def extended(array, sides, width):
    edges = {}
    for axis, dim in sides:
        size, length = (lax.axis_size(axis), array.shape[dim])
        up = [(i, (i + 1) % size) for i in range(size - 1)]
        last = lax.slice_in_dim(array, length - width, length, axis=dim)
        initial = lax.slice_in_dim(array, 0, width, axis=dim)
        edges[dim] = (
            lax.ppermute(last, axis, up),
            lax.ppermute(initial, axis, [(b, a) for a, b in up]),
        )
    done = []
    for _, dim in sides:
        low, high = edges[dim]
        around = [(width, width) if d in done else (0, 0) for d in range(array.ndim)]
        array = jnp.concatenate([jnp.pad(low, around), array, jnp.pad(high, around)], axis=dim)
        done.append(dim)
    return array


def passed_along(array, axis, by):
    length = lax.axis_size(axis)
    pairs = [(i, i + by) for i in range(length) if 0 <= i + by < length]
    return lax.ppermute(array, axis, pairs)


def one_axis_at_a_time(array, axes):
    for axis in axes:
        array = lax.pmax(array, axis)
    return array


def lower_local(a, axis):
    width = [(0, 0)] * a.ndim
    width[axis] = (1, 0)
    return jnp.pad(a, width)[
        tuple((slice(0, -1) if k == axis else slice(None) for k in range(a.ndim)))
    ]


def upper_local(a, axis):
    width = [(0, 0)] * a.ndim
    width[axis] = (0, 1)
    return jnp.pad(a, width)[
        tuple((slice(1, None) if k == axis else slice(None) for k in range(a.ndim)))
    ]


def operate(field, shift, coef_x, coef_y, coef_z, low_x, low_y, low_z):
    padded = extended(field, ((GX, 1), (GY, 2)), 1)
    total = shift * field
    total = total + coef_x * (field - padded[:, 2:, 1:-1]) + low_x * (field - padded[:, :-2, 1:-1])
    total = total + coef_y * (field - padded[:, 1:-1, 2:]) + low_y * (field - padded[:, 1:-1, :-2])
    total = (
        total + coef_z * (field - upper_local(field, 3)) + low_z * (field - lower_local(field, 3))
    )
    return total


def shards(right_side, shift, coef_x, coef_y, coef_z, low_frac, high_frac):
    before_x = passed_along(coef_x[-1:], GX, 1)
    before_y = passed_along(coef_y[:, -1:], GY, 1)
    low_x = jnp.concatenate([before_x, coef_x[:-1]], 0)
    low_y = jnp.concatenate([before_y, coef_y[:, :-1]], 1)
    low_z = lower_local(coef_z, 2)
    bound = one_axis_at_a_time(
        jnp.max(shift + 2.0 * (coef_x + low_x + coef_y + low_y + coef_z + low_z)), GX_GY
    )
    columns = lax.all_to_all(right_side, GX, split_axis=2, concat_axis=0, tiled=True)
    mirrored = lax.all_to_all(jnp.flip(columns, 0), GX, split_axis=0, concat_axis=2, tiled=True)
    fields = jnp.stack([(right_side + mirrored) / 2.0, (right_side - mirrored) / 2.0])
    lmin = (low_frac * bound)[:, None, None, None]
    lmax = (high_frac * bound)[:, None, None, None]
    theta = (lmax + lmin) / 2.0
    delta = (lmax - lmin) / 2.0
    sigma = theta / delta
    rho = 1.0 / sigma
    solution = jnp.zeros_like(fields)
    resid = fields
    direction = resid / theta
    for step in range(ITERS):
        solution = solution + direction
        resid = resid - operate(direction, shift, coef_x, coef_y, coef_z, low_x, low_y, low_z)
        rho_new = 1.0 / (2.0 * sigma - rho)
        direction = rho_new * rho * direction + 2.0 * rho_new / delta * resid
        rho = rho_new
    return (solution[0] + solution[1], resid[0] + resid[1])


def solution(mesh):
    torus = Mesh(mesh.devices.reshape(32, 2, 4, 2, 2), ("gx_0", "gx_1", "gy_0", "gy_1", "gy_2"))
    in_specs = (
        P(GX, GY, None),
        P(GX, GY, None),
        P(GX, GY, None),
        P(GX, GY, None),
        P(GX, GY, None),
        P(),
        P(),
    )
    out_specs = (P(GX, GY, None), P(GX, GY, None))
    return jax.shard_map(
        shards, mesh=torus, in_specs=in_specs, out_specs=out_specs, check_vma=False
    )
```

profile of v0, /device:TPU:102, one launch (start us, length us, event | category | flops | bytes accessed | tf_op | source)
XLA Modules:
  0.0 321.0 jit_solution(17458201406174822139)
XLA Ops:
  0.6 1.3 copy.211
  2.4 58.5 %all_to_all.36 = f32[64,1,512]{2,1,0:T(1,128)S(1)} all-to-all(f32[64,1,512]{2,1,0:T(1,128)S(1)} %reshape.71), channel_id=1, replica_groups=mesh['gx_0'=32,'gx_1'=2,'gy_0'=4,'gy_1'=2,'gy_2'=2] {'gx_0','gx_1'}, dimensions={0} | all-to-all | bytes 262144 | tf_op jit(solution)/shard_map/all_to_all | solution.py:81
  60.9 0.5 broadcast.297
  61.4 0.9 reduce
  62.8 0.5 rev.4
  63.3 0.7 copy.255
  64.0 1.5 reshape.73
  65.4 9.4 %all-to-all-start.1 = ((f32[64,1,512]{2,1,0:T(1,128)}), f32[64,1,512]{2,1,0:T(1,128)S(1)}, u32[]{:S(2)}, u32[]{:S(2)}) async-start(f32[64,1,512]{2,1,0:T(1,128)} %reshape.73), calls=%async_computation.1 | async-start | bytes 262144 | tf_op jit(solution)/shard_map/all_to_all | solution.py:82
  74.9 4.7 %collective-permute-start = (f32[1,16,256]{2,1,0:T(8,128)S(1)}, f32[1,16,256]{2,1,0:T(8,128)S(1)}, u32[]{:S(2)}, u32[]{:S(2)}) collective-permute-start(f32[1,16,256]{2,1,0:T(8,128)S(1)} %slice.299), channel_id=1, source_target_pairs={{0,16},{16,32},{32,48},{48,64},{64,80},{80,96},{96,112},{112,128},... | collective-permute-start | bytes 49160 | tf_op jit(solution)/shard_map/ppermute | solution.py:36
  79.6 2.1 collective-permute-start.1
  81.7 3.0 collective-permute-done.1
  84.8 0.7 add_reduce_fusion
  85.5 56.1 %pmax.35 = f32[]{:T(128)} all-reduce(f32[]{:T(128)} %get-tuple-element.35), channel_id=1, replica_groups=mesh['gx_0'=32,'gx_1'=2,'gy_0'=4,'gy_1'=2,'gy_2'=2] {'gx_0'}, use_global_device_ids=true, to_apply=%region_1.2 | all-reduce | flops 1 | bytes 8 | tf_op jit(solution)/shard_map/pmax | solution.py:41
  141.6 7.9 %pmax.36 = f32[]{:T(128)} all-reduce(f32[]{:T(128)} %pmax.35), channel_id=1, replica_groups=mesh['gx_0'=32,'gx_1'=2,'gy_0'=4,'gy_1'=2,'gy_2'=2] {'gx_1'}, use_global_device_ids=true, to_apply=%region_2.3 | all-reduce | flops 1 | bytes 8 | tf_op jit(solution)/shard_map/pmax | solution.py:41
  149.4 11.4 %pmax.37 = f32[]{:T(128)} all-reduce(f32[]{:T(128)} %pmax.36), channel_id=1, replica_groups=mesh['gx_0'=32,'gx_1'=2,'gy_0'=4,'gy_1'=2,'gy_2'=2] {'gy_0'}, use_global_device_ids=true, to_apply=%region_3.4 | all-reduce | flops 1 | bytes 8 | tf_op jit(solution)/shard_map/pmax | solution.py:41
  160.9 5.6 %pmax.38 = f32[]{:T(128)} all-reduce(f32[]{:T(128)} %pmax.37), channel_id=1, replica_groups=mesh['gx_0'=32,'gx_1'=2,'gy_0'=4,'gy_1'=2,'gy_2'=2] {'gy_1'}, use_global_device_ids=true, to_apply=%region_4.5 | all-reduce | flops 1 | bytes 8 | tf_op jit(solution)/shard_map/pmax | solution.py:41
  166.5 3.1 pmax.39
  169.6 0.6 divide_multiply_fusion
  170.3 1.0 reduce.1
  171.3 0.7 reshape.74
  172.6 0.5 copy-done.4
  173.3 2.1 collective-permute-start.5
  175.4 3.5 %collective-permute-start.4 = (f32[2,8,1,256]{3,1,2,0:T(8,128)S(1)}, f32[2,8,1,256]{3,1,2,0:T(8,128)S(1)}, u32[]{:S(2)}, u32[]{:S(2)}) collective-permute-start(f32[2,8,1,256]{3,1,2,0:T(8,128)S(1)} %copy.218), channel_id=1, source_target_pairs={{1,0},{2,1},{3,2},{4,3},{5,4},{6,5},{7,6},{8,7},{9,8},{10,9},{11,1... | collective-permute-start | bytes 49160 | tf_op jit(solution)/shard_map/ppermute | solution.py:22
  178.9 7.6 %collective-permute-start.3 = (f32[2,1,16,256]{3,2,1,0:T(8,128)S(1)}, f32[2,1,16,256]{3,2,1,0:T(8,128)S(1)}, u32[]{:S(2)}, u32[]{:S(2)}) collective-permute-start(f32[2,1,16,256]{3,2,1,0:T(8,128)S(1)} %get-tuple-element.67), channel_id=1, source_target_pairs={{0,16},{16,32},{32,48},{48,64},{64,80},{80,96},{96,112},{112,128},... | collective-permute-start | bytes 98312 | tf_op jit(solution)/shard_map/ppermute | solution.py:21
  186.5 1.9 collective-permute-start.2
  188.6 7.4 %collective-permute-done.2 = f32[2,1,16,256]{3,2,1,0:T(8,128)S(1)} collective-permute-done((f32[2,1,16,256]{3,2,1,0:T(8,128)S(1)}, f32[2,1,16,256]{3,2,1,0:T(8,128)S(1)}, u32[]{:S(2)}, u32[]{:S(2)}) %collective-permute-start.2) | collective-permute-done | bytes 32800 | tf_op jit(solution)/shard_map/ppermute | solution.py:22
  196.3 1.9 collective-permute-start.7
  198.2 5.4 %collective-permute-start.6 = (f32[2,1,16,256]{3,2,1,0:T(8,128)S(1)}, f32[2,1,16,256]{3,2,1,0:T(8,128)S(1)}, u32[]{:S(2)}, u32[]{:S(2)}) collective-permute-start(f32[2,1,16,256]{3,2,1,0:T(8,128)S(1)} %get-tuple-element.64), channel_id=1, source_target_pairs={{16,0},{32,16},{48,32},{64,48},{80,64},{96,80},{112,96},{128,112},... | collective-permute-start | bytes 98312 | tf_op jit(solution)/shard_map/ppermute | solution.py:22
  203.7 1.9 collective-permute-start.9
  205.6 3.6 %collective-permute-start.8 = (f32[2,8,1,256]{3,1,2,0:T(8,128)S(1)}, f32[2,8,1,256]{3,1,2,0:T(8,128)S(1)}, u32[]{:S(2)}, u32[]{:S(2)}) collective-permute-start(f32[2,8,1,256]{3,1,2,0:T(8,128)S(1)} %copy.222), channel_id=1, source_target_pairs={{1,0},{2,1},{3,2},{4,3},{5,4},{6,5},{7,6},{8,7},{9,8},{10,9},{11,1... | collective-permute-start | bytes 49160 | tf_op jit(solution)/shard_map/ppermute | solution.py:22
  209.3 1.4 collective-permute-done.8
  211.1 4.0 %collective-permute-start.11 = (f32[2,1,16,256]{3,2,1,0:T(8,128)S(1)}, f32[2,1,16,256]{3,2,1,0:T(8,128)S(1)}, u32[]{:S(2)}, u32[]{:S(2)}) collective-permute-start(f32[2,1,16,256]{3,2,1,0:T(8,128)S(1)} %get-tuple-element.59), channel_id=1, source_target_pairs={{0,16},{16,32},{32,48},{48,64},{64,80},{80,96},{96,112},{112,128},... | collective-permute-start | bytes 98312 | tf_op jit(solution)/shard_map/ppermute | solution.py:21
  215.2 3.3 %collective-permute-start.10 = (f32[2,1,16,256]{3,2,1,0:T(8,128)S(1)}, f32[2,1,16,256]{3,2,1,0:T(8,128)S(1)}, u32[]{:S(2)}, u32[]{:S(2)}) collective-permute-start(f32[2,1,16,256]{3,2,1,0:T(8,128)S(1)} %get-tuple-element.60), channel_id=1, source_target_pairs={{16,0},{32,16},{48,32},{64,48},{80,64},{96,80},{112,96},{128,112},... | collective-permute-start | bytes 98312 | tf_op jit(solution)/shard_map/ppermute | solution.py:22
  218.5 3.0 collective-permute-start.13
  221.6 2.5 collective-permute-start.12
  224.2 1.4 collective-permute-done.12
  225.9 6.1 %collective-permute-start.15 = (f32[2,1,16,256]{3,2,1,0:T(8,128)S(1)}, f32[2,1,16,256]{3,2,1,0:T(8,128)S(1)}, u32[]{:S(2)}, u32[]{:S(2)}) collective-permute-start(f32[2,1,16,256]{3,2,1,0:T(8,128)S(1)} %get-tuple-element.55), channel_id=1, source_target_pairs={{0,16},{16,32},{32,48},{48,64},{64,80},{80,96},{96,112},{112,128},... | collective-permute-start | bytes 98312 | tf_op jit(solution)/shard_map/ppermute | solution.py:21
  232.1 1.9 collective-permute-start.14
  234.1 4.8 %collective-permute-start.17 = (f32[2,8,1,256]{3,1,2,0:T(8,128)S(1)}, f32[2,8,1,256]{3,1,2,0:T(8,128)S(1)}, u32[]{:S(2)}, u32[]{:S(2)}) collective-permute-start(f32[2,8,1,256]{3,1,2,0:T(8,128)S(1)} %copy.232), channel_id=1, source_target_pairs={{0,1},{1,2},{2,3},{3,4},{4,5},{5,6},{6,7},{7,8},{8,9},{9,10},{10,1... | collective-permute-start | bytes 49160 | tf_op jit(solution)/shard_map/ppermute | solution.py:21
  238.9 1.9 collective-permute-start.16
  240.8 1.4 collective-permute-done.16
  242.6 7.3 %collective-permute-start.19 = (f32[2,1,16,256]{3,2,1,0:T(8,128)S(1)}, f32[2,1,16,256]{3,2,1,0:T(8,128)S(1)}, u32[]{:S(2)}, u32[]{:S(2)}) collective-permute-start(f32[2,1,16,256]{3,2,1,0:T(8,128)S(1)} %get-tuple-element.51), channel_id=1, source_target_pairs={{0,16},{16,32},{32,48},{48,64},{64,80},{80,96},{96,112},{112,128},... | collective-permute-start | bytes 98312 | tf_op jit(solution)/shard_map/ppermute | solution.py:21
  249.9 1.9 collective-permute-start.18
  251.9 4.8 %collective-permute-start.21 = (f32[2,8,1,256]{3,1,2,0:T(8,128)S(1)}, f32[2,8,1,256]{3,1,2,0:T(8,128)S(1)}, u32[]{:S(2)}, u32[]{:S(2)}) collective-permute-start(f32[2,8,1,256]{3,1,2,0:T(8,128)S(1)} %copy.236), channel_id=1, source_target_pairs={{0,1},{1,2},{2,3},{3,4},{4,5},{5,6},{6,7},{7,8},{8,9},{9,10},{10,1... | collective-permute-start | bytes 49160 | tf_op jit(solution)/shard_map/ppermute | solution.py:21
  256.7 1.9 collective-permute-start.20
  258.7 1.4 collective-permute-done.20
  260.5 7.3 %collective-permute-start.23 = (f32[2,1,16,256]{3,2,1,0:T(8,128)S(1)}, f32[2,1,16,256]{3,2,1,0:T(8,128)S(1)}, u32[]{:S(2)}, u32[]{:S(2)}) collective-permute-start(f32[2,1,16,256]{3,2,1,0:T(8,128)S(1)} %get-tuple-element.47), channel_id=1, source_target_pairs={{0,16},{16,32},{32,48},{48,64},{64,80},{80,96},{96,112},{112,128},... | collective-permute-start | bytes 98312 | tf_op jit(solution)/shard_map/ppermute | solution.py:21
  267.7 1.9 collective-permute-start.22
  269.7 4.8 %collective-permute-start.25 = (f32[2,8,1,256]{3,1,2,0:T(8,128)S(1)}, f32[2,8,1,256]{3,1,2,0:T(8,128)S(1)}, u32[]{:S(2)}, u32[]{:S(2)}) collective-permute-start(f32[2,8,1,256]{3,1,2,0:T(8,128)S(1)} %copy.240), channel_id=1, source_target_pairs={{0,1},{1,2},{2,3},{3,4},{4,5},{5,6},{6,7},{7,8},{8,9},{9,10},{10,1... | collective-permute-start | bytes 49160 | tf_op jit(solution)/shard_map/ppermute | solution.py:21
  274.5 1.9 collective-permute-start.24
  276.5 1.4 collective-permute-done.24
  278.3 7.3 %collective-permute-start.27 = (f32[2,1,16,256]{3,2,1,0:T(8,128)S(1)}, f32[2,1,16,256]{3,2,1,0:T(8,128)S(1)}, u32[]{:S(2)}, u32[]{:S(2)}) collective-permute-start(f32[2,1,16,256]{3,2,1,0:T(8,128)S(1)} %get-tuple-element.43), channel_id=1, source_target_pairs={{0,16},{16,32},{32,48},{48,64},{64,80},{80,96},{96,112},{112,128},... | collective-permute-start | bytes 98312 | tf_op jit(solution)/shard_map/ppermute | solution.py:21
  285.5 1.9 collective-permute-start.26
  287.5 4.8 %collective-permute-start.29 = (f32[2,8,1,256]{3,1,2,0:T(8,128)S(1)}, f32[2,8,1,256]{3,1,2,0:T(8,128)S(1)}, u32[]{:S(2)}, u32[]{:S(2)}) collective-permute-start(f32[2,8,1,256]{3,1,2,0:T(8,128)S(1)} %copy.244), channel_id=1, source_target_pairs={{0,1},{1,2},{2,3},{3,4},{4,5},{5,6},{6,7},{7,8},{8,9},{9,10},{10,1... | collective-permute-start | bytes 49160 | tf_op jit(solution)/shard_map/ppermute | solution.py:21
  292.4 1.9 collective-permute-start.28
  294.3 1.4 collective-permute-done.28
  295.7 0.5 add_add_fusion
  296.3 4.5 %collective-permute-start.33 = (f32[2,8,1,256]{3,1,2,0:T(8,128)S(1)}, f32[2,8,1,256]{3,1,2,0:T(8,128)S(1)}, u32[]{:S(2)}, u32[]{:S(2)}) collective-permute-start(f32[2,8,1,256]{3,1,2,0:T(8,128)S(1)} %copy.248), channel_id=1, source_target_pairs={{0,1},{1,2},{2,3},{3,4},{4,5},{5,6},{6,7},{7,8},{8,9},{9,10},{10,1... | collective-permute-start | bytes 49160 | tf_op jit(solution)/shard_map/ppermute | solution.py:21
  300.9 1.9 collective-permute-start.32
  302.8 7.8 %collective-permute-start.31 = (f32[2,1,16,256]{3,2,1,0:T(8,128)S(1)}, f32[2,1,16,256]{3,2,1,0:T(8,128)S(1)}, u32[]{:S(2)}, u32[]{:S(2)}) collective-permute-start(f32[2,1,16,256]{3,2,1,0:T(8,128)S(1)} %get-tuple-element.39), channel_id=1, source_target_pairs={{0,16},{16,32},{32,48},{48,64},{64,80},{80,96},{96,112},{112,128},... | collective-permute-start | bytes 98312 | tf_op jit(solution)/shard_map/ppermute | solution.py:21
  310.6 1.9 collective-permute-start.30
  312.6 0.7 fusion.170
  313.3 6.7 %collective-permute-done.30 = f32[2,1,16,256]{3,2,1,0:T(8,128)S(1)} collective-permute-done((f32[2,1,16,256]{3,2,1,0:T(8,128)S(1)}, f32[2,1,16,256]{3,2,1,0:T(8,128)S(1)}, u32[]{:S(2)}, u32[]{:S(2)}) %collective-permute-start.30) | collective-permute-done | bytes 32800 | tf_op jit(solution)/shard_map/ppermute | solution.py:22
  320.4 0.7 fusion.169
  (108 shorter events, 4.6 us)
Async XLA Ops:
  64.0 20.8 %copy-start.3 = (f32[8,16,256]{2,1,0:T(8,128)S(1)}, f32[8,16,256]{2,1,0:T(8,128)}, u32[]{:S(2)}) copy-start(f32[8,16,256]{2,1,0:T(8,128)} %param.11) | copy-start | bytes 393220
  65.4 9.4 %copy-start.1 = (f32[8,16,256]{2,1,0:T(8,128)S(1)}, f32[8,16,256]{2,1,0:T(8,128)}, u32[]{:S(2)}) copy-start(f32[8,16,256]{2,1,0:T(8,128)} %param.9) | copy-start | bytes 393220
  65.4 14.2 %copy-start = (f32[8,16,256]{2,1,0:T(8,128)S(1)}, f32[8,16,256]{2,1,0:T(8,128)}, u32[]{:S(2)}) copy-start(f32[8,16,256]{2,1,0:T(8,128)} %param.10) | copy-start | bytes 393220
  65.4 104.8 %all-to-all-start.1 = ((f32[64,1,512]{2,1,0:T(1,128)}), f32[64,1,512]{2,1,0:T(1,128)S(1)}, u32[]{:S(2)}, u32[]{:S(2)}) async-start(f32[64,1,512]{2,1,0:T(1,128)} %reshape.73), calls=%async_computation.1 | async-start | bytes 262144 | tf_op jit(solution)/shard_map/all_to_all | solution.py:82
  74.9 9.9 %copy-start.2 = (f32[8,16,256]{2,1,0:T(8,128)S(1)}, f32[8,16,256]{2,1,0:T(8,128)}, u32[]{:S(2)}) copy-start(f32[8,16,256]{2,1,0:T(8,128)} %param.8) | copy-start | bytes 393220
  74.9 9.9 %collective-permute-start = (f32[1,16,256]{2,1,0:T(8,128)S(1)}, f32[1,16,256]{2,1,0:T(8,128)S(1)}, u32[]{:S(2)}, u32[]{:S(2)}) collective-permute-start(f32[1,16,256]{2,1,0:T(8,128)S(1)} %slice.299), channel_id=1, source_target_pairs={{0,16},{16,32},{32,48},{48,64},{64,80},{80,96},{96,112},{112,128},... | collective-permute-start | bytes 49160 | tf_op jit(solution)/shard_map/ppermute | solution.py:36
  79.6 5.1 %slice-start = ((f32[8,16,256]{2,1,0:T(8,128)}), f32[7,16,256]{2,1,0:T(8,128)S(1)}, s32[]{:S(2)}) async-start(f32[8,16,256]{2,1,0:T(8,128)} %param.9), calls=%async_computation.2 | async-start | bytes 229376 | tf_op jit(solution)/shard_map/slice | solution.py:75
  79.6 5.1 %collective-permute-start.1 = (f32[8,1,256]{2,1,0:T(1,128)S(1)}, f32[8,1,256]{2,1,0:T(1,128)S(1)}, u32[]{:S(2)}, u32[]{:S(2)}) collective-permute-start(f32[8,1,256]{2,1,0:T(1,128)S(1)} %slice.301), channel_id=1, source_target_pairs={{0,1},{1,2},{2,3},{3,4},{4,5},{5,6},{6,7},{7,8},{8,9},{9,10},{10,1... | collective-permute-start | bytes 24584 | tf_op jit(solution)/shard_map/ppermute | solution.py:36
  166.5 3.1 copy-start.5
  166.5 3.1 copy-start.6
  172.2 0.9 copy-start.4
  173.3 15.1 %collective-permute-start.5 = (f32[2,8,1,256]{3,1,2,0:T(8,128)S(1)}, f32[2,8,1,256]{3,1,2,0:T(8,128)S(1)}, u32[]{:S(2)}, u32[]{:S(2)}) collective-permute-start(f32[2,8,1,256]{3,1,2,0:T(8,128)S(1)} %copy.220), channel_id=1, source_target_pairs={{0,1},{1,2},{2,3},{3,4},{4,5},{5,6},{6,7},{7,8},{8,9},{9,10},{10,1... | collective-permute-start | bytes 49160 | tf_op jit(solution)/shard_map/ppermute | solution.py:21
  175.4 13.1 %collective-permute-start.4 = (f32[2,8,1,256]{3,1,2,0:T(8,128)S(1)}, f32[2,8,1,256]{3,1,2,0:T(8,128)S(1)}, u32[]{:S(2)}, u32[]{:S(2)}) collective-permute-start(f32[2,8,1,256]{3,1,2,0:T(8,128)S(1)} %copy.218), channel_id=1, source_target_pairs={{1,0},{2,1},{3,2},{4,3},{5,4},{6,5},{7,6},{8,7},{9,8},{10,9},{11,1... | collective-permute-start | bytes 49160 | tf_op jit(solution)/shard_map/ppermute | solution.py:22
  178.9 9.6 %collective-permute-start.3 = (f32[2,1,16,256]{3,2,1,0:T(8,128)S(1)}, f32[2,1,16,256]{3,2,1,0:T(8,128)S(1)}, u32[]{:S(2)}, u32[]{:S(2)}) collective-permute-start(f32[2,1,16,256]{3,2,1,0:T(8,128)S(1)} %get-tuple-element.67), channel_id=1, source_target_pairs={{0,16},{16,32},{32,48},{48,64},{64,80},{80,96},{96,112},{112,128},... | collective-permute-start | bytes 98312 | tf_op jit(solution)/shard_map/ppermute | solution.py:21
  186.5 9.4 %collective-permute-start.2 = (f32[2,1,16,256]{3,2,1,0:T(8,128)S(1)}, f32[2,1,16,256]{3,2,1,0:T(8,128)S(1)}, u32[]{:S(2)}, u32[]{:S(2)}) collective-permute-start(f32[2,1,16,256]{3,2,1,0:T(8,128)S(1)} %get-tuple-element.68), channel_id=1, source_target_pairs={{16,0},{32,16},{48,32},{64,48},{80,64},{96,80},{112,96},{128,112},... | collective-permute-start | bytes 98312 | tf_op jit(solution)/shard_map/ppermute | solution.py:22
  196.3 14.4 %collective-permute-start.7 = (f32[2,1,16,256]{3,2,1,0:T(8,128)S(1)}, f32[2,1,16,256]{3,2,1,0:T(8,128)S(1)}, u32[]{:S(2)}, u32[]{:S(2)}) collective-permute-start(f32[2,1,16,256]{3,2,1,0:T(8,128)S(1)} %get-tuple-element.63), channel_id=1, source_target_pairs={{0,16},{16,32},{32,48},{48,64},{64,80},{80,96},{96,112},{112,128},... | collective-permute-start | bytes 98312 | tf_op jit(solution)/shard_map/ppermute | solution.py:21
  198.2 12.5 %collective-permute-start.6 = (f32[2,1,16,256]{3,2,1,0:T(8,128)S(1)}, f32[2,1,16,256]{3,2,1,0:T(8,128)S(1)}, u32[]{:S(2)}, u32[]{:S(2)}) collective-permute-start(f32[2,1,16,256]{3,2,1,0:T(8,128)S(1)} %get-tuple-element.64), channel_id=1, source_target_pairs={{16,0},{32,16},{48,32},{64,48},{80,64},{96,80},{112,96},{128,112},... | collective-permute-start | bytes 98312 | tf_op jit(solution)/shard_map/ppermute | solution.py:22
  203.7 5.6 %collective-permute-start.9 = (f32[2,8,1,256]{3,1,2,0:T(8,128)S(1)}, f32[2,8,1,256]{3,1,2,0:T(8,128)S(1)}, u32[]{:S(2)}, u32[]{:S(2)}) collective-permute-start(f32[2,8,1,256]{3,1,2,0:T(8,128)S(1)} %copy.224), channel_id=1, source_target_pairs={{0,1},{1,2},{2,3},{3,4},{4,5},{5,6},{6,7},{7,8},{8,9},{9,10},{10,1... | collective-permute-start | bytes 49160 | tf_op jit(solution)/shard_map/ppermute | solution.py:21
  205.6 5.1 %collective-permute-start.8 = (f32[2,8,1,256]{3,1,2,0:T(8,128)S(1)}, f32[2,8,1,256]{3,1,2,0:T(8,128)S(1)}, u32[]{:S(2)}, u32[]{:S(2)}) collective-permute-start(f32[2,8,1,256]{3,1,2,0:T(8,128)S(1)} %copy.222), channel_id=1, source_target_pairs={{1,0},{2,1},{3,2},{4,3},{5,4},{6,5},{7,6},{8,7},{9,8},{10,9},{11,1... | collective-permute-start | bytes 49160 | tf_op jit(solution)/shard_map/ppermute | solution.py:22
  211.1 14.4 %collective-permute-start.11 = (f32[2,1,16,256]{3,2,1,0:T(8,128)S(1)}, f32[2,1,16,256]{3,2,1,0:T(8,128)S(1)}, u32[]{:S(2)}, u32[]{:S(2)}) collective-permute-start(f32[2,1,16,256]{3,2,1,0:T(8,128)S(1)} %get-tuple-element.59), channel_id=1, source_target_pairs={{0,16},{16,32},{32,48},{48,64},{64,80},{80,96},{96,112},{112,128},... | collective-permute-start | bytes 98312 | tf_op jit(solution)/shard_map/ppermute | solution.py:21
  215.2 10.4 %collective-permute-start.10 = (f32[2,1,16,256]{3,2,1,0:T(8,128)S(1)}, f32[2,1,16,256]{3,2,1,0:T(8,128)S(1)}, u32[]{:S(2)}, u32[]{:S(2)}) collective-permute-start(f32[2,1,16,256]{3,2,1,0:T(8,128)S(1)} %get-tuple-element.60), channel_id=1, source_target_pairs={{16,0},{32,16},{48,32},{64,48},{80,64},{96,80},{112,96},{128,112},... | collective-permute-start | bytes 98312 | tf_op jit(solution)/shard_map/ppermute | solution.py:22
  218.5 5.6 %collective-permute-start.13 = (f32[2,8,1,256]{3,1,2,0:T(8,128)S(1)}, f32[2,8,1,256]{3,1,2,0:T(8,128)S(1)}, u32[]{:S(2)}, u32[]{:S(2)}) collective-permute-start(f32[2,8,1,256]{3,1,2,0:T(8,128)S(1)} %copy.228), channel_id=1, source_target_pairs={{0,1},{1,2},{2,3},{3,4},{4,5},{5,6},{6,7},{7,8},{8,9},{9,10},{10,1... | collective-permute-start | bytes 49160 | tf_op jit(solution)/shard_map/ppermute | solution.py:21
  221.6 4.0 %collective-permute-start.12 = (f32[2,8,1,256]{3,1,2,0:T(8,128)S(1)}, f32[2,8,1,256]{3,1,2,0:T(8,128)S(1)}, u32[]{:S(2)}, u32[]{:S(2)}) collective-permute-start(f32[2,8,1,256]{3,1,2,0:T(8,128)S(1)} %copy.226), channel_id=1, source_target_pairs={{1,0},{2,1},{3,2},{4,3},{5,4},{6,5},{7,6},{8,7},{9,8},{10,9},{11,1... | collective-permute-start | bytes 49160 | tf_op jit(solution)/shard_map/ppermute | solution.py:22
  225.9 16.3 %collective-permute-start.15 = (f32[2,1,16,256]{3,2,1,0:T(8,128)S(1)}, f32[2,1,16,256]{3,2,1,0:T(8,128)S(1)}, u32[]{:S(2)}, u32[]{:S(2)}) collective-permute-start(f32[2,1,16,256]{3,2,1,0:T(8,128)S(1)} %get-tuple-element.55), channel_id=1, source_target_pairs={{0,16},{16,32},{32,48},{48,64},{64,80},{80,96},{96,112},{112,128},... | collective-permute-start | bytes 98312 | tf_op jit(solution)/shard_map/ppermute | solution.py:21
  232.1 10.2 %collective-permute-start.14 = (f32[2,1,16,256]{3,2,1,0:T(8,128)S(1)}, f32[2,1,16,256]{3,2,1,0:T(8,128)S(1)}, u32[]{:S(2)}, u32[]{:S(2)}) collective-permute-start(f32[2,1,16,256]{3,2,1,0:T(8,128)S(1)} %get-tuple-element.56), channel_id=1, source_target_pairs={{16,0},{32,16},{48,32},{64,48},{80,64},{96,80},{112,96},{128,112},... | collective-permute-start | bytes 98312 | tf_op jit(solution)/shard_map/ppermute | solution.py:22
  234.1 6.8 %collective-permute-start.17 = (f32[2,8,1,256]{3,1,2,0:T(8,128)S(1)}, f32[2,8,1,256]{3,1,2,0:T(8,128)S(1)}, u32[]{:S(2)}, u32[]{:S(2)}) collective-permute-start(f32[2,8,1,256]{3,1,2,0:T(8,128)S(1)} %copy.232), channel_id=1, source_target_pairs={{0,1},{1,2},{2,3},{3,4},{4,5},{5,6},{6,7},{7,8},{8,9},{9,10},{10,1... | collective-permute-start | bytes 49160 | tf_op jit(solution)/shard_map/ppermute | solution.py:21
  238.9 3.4 %collective-permute-start.16 = (f32[2,8,1,256]{3,1,2,0:T(8,128)S(1)}, f32[2,8,1,256]{3,1,2,0:T(8,128)S(1)}, u32[]{:S(2)}, u32[]{:S(2)}) collective-permute-start(f32[2,8,1,256]{3,1,2,0:T(8,128)S(1)} %copy.230), channel_id=1, source_target_pairs={{1,0},{2,1},{3,2},{4,3},{5,4},{6,5},{7,6},{8,7},{9,8},{10,9},{11,1... | collective-permute-start | bytes 49160 | tf_op jit(solution)/shard_map/ppermute | solution.py:22
  242.6 17.4 %collective-permute-start.19 = (f32[2,1,16,256]{3,2,1,0:T(8,128)S(1)}, f32[2,1,16,256]{3,2,1,0:T(8,128)S(1)}, u32[]{:S(2)}, u32[]{:S(2)}) collective-permute-start(f32[2,1,16,256]{3,2,1,0:T(8,128)S(1)} %get-tuple-element.51), channel_id=1, source_target_pairs={{0,16},{16,32},{32,48},{48,64},{64,80},{80,96},{96,112},{112,128},... | collective-permute-start | bytes 98312 | tf_op jit(solution)/shard_map/ppermute | solution.py:21
  249.9 10.2 %collective-permute-start.18 = (f32[2,1,16,256]{3,2,1,0:T(8,128)S(1)}, f32[2,1,16,256]{3,2,1,0:T(8,128)S(1)}, u32[]{:S(2)}, u32[]{:S(2)}) collective-permute-start(f32[2,1,16,256]{3,2,1,0:T(8,128)S(1)} %get-tuple-element.52), channel_id=1, source_target_pairs={{16,0},{32,16},{48,32},{64,48},{80,64},{96,80},{112,96},{128,112},... | collective-permute-start | bytes 98312 | tf_op jit(solution)/shard_map/ppermute | solution.py:22
  251.9 6.8 %collective-permute-start.21 = (f32[2,8,1,256]{3,1,2,0:T(8,128)S(1)}, f32[2,8,1,256]{3,1,2,0:T(8,128)S(1)}, u32[]{:S(2)}, u32[]{:S(2)}) collective-permute-start(f32[2,8,1,256]{3,1,2,0:T(8,128)S(1)} %copy.236), channel_id=1, source_target_pairs={{0,1},{1,2},{2,3},{3,4},{4,5},{5,6},{6,7},{7,8},{8,9},{9,10},{10,1... | collective-permute-start | bytes 49160 | tf_op jit(solution)/shard_map/ppermute | solution.py:21
  256.7 3.4 %collective-permute-start.20 = (f32[2,8,1,256]{3,1,2,0:T(8,128)S(1)}, f32[2,8,1,256]{3,1,2,0:T(8,128)S(1)}, u32[]{:S(2)}, u32[]{:S(2)}) collective-permute-start(f32[2,8,1,256]{3,1,2,0:T(8,128)S(1)} %copy.234), channel_id=1, source_target_pairs={{1,0},{2,1},{3,2},{4,3},{5,4},{6,5},{7,6},{8,7},{9,8},{10,9},{11,1... | collective-permute-start | bytes 49160 | tf_op jit(solution)/shard_map/ppermute | solution.py:22
  260.5 17.4 %collective-permute-start.23 = (f32[2,1,16,256]{3,2,1,0:T(8,128)S(1)}, f32[2,1,16,256]{3,2,1,0:T(8,128)S(1)}, u32[]{:S(2)}, u32[]{:S(2)}) collective-permute-start(f32[2,1,16,256]{3,2,1,0:T(8,128)S(1)} %get-tuple-element.47), channel_id=1, source_target_pairs={{0,16},{16,32},{32,48},{48,64},{64,80},{80,96},{96,112},{112,128},... | collective-permute-start | bytes 98312 | tf_op jit(solution)/shard_map/ppermute | solution.py:21
  267.7 10.2 %collective-permute-start.22 = (f32[2,1,16,256]{3,2,1,0:T(8,128)S(1)}, f32[2,1,16,256]{3,2,1,0:T(8,128)S(1)}, u32[]{:S(2)}, u32[]{:S(2)}) collective-permute-start(f32[2,1,16,256]{3,2,1,0:T(8,128)S(1)} %get-tuple-element.48), channel_id=1, source_target_pairs={{16,0},{32,16},{48,32},{64,48},{80,64},{96,80},{112,96},{128,112},... | collective-permute-start | bytes 98312 | tf_op jit(solution)/shard_map/ppermute | solution.py:22
  269.7 6.8 %collective-permute-start.25 = (f32[2,8,1,256]{3,1,2,0:T(8,128)S(1)}, f32[2,8,1,256]{3,1,2,0:T(8,128)S(1)}, u32[]{:S(2)}, u32[]{:S(2)}) collective-permute-start(f32[2,8,1,256]{3,1,2,0:T(8,128)S(1)} %copy.240), channel_id=1, source_target_pairs={{0,1},{1,2},{2,3},{3,4},{4,5},{5,6},{6,7},{7,8},{8,9},{9,10},{10,1... | collective-permute-start | bytes 49160 | tf_op jit(solution)/shard_map/ppermute | solution.py:21
  274.5 3.4 %collective-permute-start.24 = (f32[2,8,1,256]{3,1,2,0:T(8,128)S(1)}, f32[2,8,1,256]{3,1,2,0:T(8,128)S(1)}, u32[]{:S(2)}, u32[]{:S(2)}) collective-permute-start(f32[2,8,1,256]{3,1,2,0:T(8,128)S(1)} %copy.238), channel_id=1, source_target_pairs={{1,0},{2,1},{3,2},{4,3},{5,4},{6,5},{7,6},{8,7},{9,8},{10,9},{11,1... | collective-permute-start | bytes 49160 | tf_op jit(solution)/shard_map/ppermute | solution.py:22
  278.3 17.4 %collective-permute-start.27 = (f32[2,1,16,256]{3,2,1,0:T(8,128)S(1)}, f32[2,1,16,256]{3,2,1,0:T(8,128)S(1)}, u32[]{:S(2)}, u32[]{:S(2)}) collective-permute-start(f32[2,1,16,256]{3,2,1,0:T(8,128)S(1)} %get-tuple-element.43), channel_id=1, source_target_pairs={{0,16},{16,32},{32,48},{48,64},{64,80},{80,96},{96,112},{112,128},... | collective-permute-start | bytes 98312 | tf_op jit(solution)/shard_map/ppermute | solution.py:21
  285.5 10.2 %collective-permute-start.26 = (f32[2,1,16,256]{3,2,1,0:T(8,128)S(1)}, f32[2,1,16,256]{3,2,1,0:T(8,128)S(1)}, u32[]{:S(2)}, u32[]{:S(2)}) collective-permute-start(f32[2,1,16,256]{3,2,1,0:T(8,128)S(1)} %get-tuple-element.44), channel_id=1, source_target_pairs={{16,0},{32,16},{48,32},{64,48},{80,64},{96,80},{112,96},{128,112},... | collective-permute-start | bytes 98312 | tf_op jit(solution)/shard_map/ppermute | solution.py:22
  287.5 6.8 %collective-permute-start.29 = (f32[2,8,1,256]{3,1,2,0:T(8,128)S(1)}, f32[2,8,1,256]{3,1,2,0:T(8,128)S(1)}, u32[]{:S(2)}, u32[]{:S(2)}) collective-permute-start(f32[2,8,1,256]{3,1,2,0:T(8,128)S(1)} %copy.244), channel_id=1, source_target_pairs={{0,1},{1,2},{2,3},{3,4},{4,5},{5,6},{6,7},{7,8},{8,9},{9,10},{10,1... | collective-permute-start | bytes 49160 | tf_op jit(solution)/shard_map/ppermute | solution.py:21
  292.4 3.4 %collective-permute-start.28 = (f32[2,8,1,256]{3,1,2,0:T(8,128)S(1)}, f32[2,8,1,256]{3,1,2,0:T(8,128)S(1)}, u32[]{:S(2)}, u32[]{:S(2)}) collective-permute-start(f32[2,8,1,256]{3,1,2,0:T(8,128)S(1)} %copy.242), channel_id=1, source_target_pairs={{1,0},{2,1},{3,2},{4,3},{5,4},{6,5},{7,6},{8,7},{9,8},{10,9},{11,1... | collective-permute-start | bytes 49160 | tf_op jit(solution)/shard_map/ppermute | solution.py:22
  296.3 16.9 %collective-permute-start.33 = (f32[2,8,1,256]{3,1,2,0:T(8,128)S(1)}, f32[2,8,1,256]{3,1,2,0:T(8,128)S(1)}, u32[]{:S(2)}, u32[]{:S(2)}) collective-permute-start(f32[2,8,1,256]{3,1,2,0:T(8,128)S(1)} %copy.248), channel_id=1, source_target_pairs={{0,1},{1,2},{2,3},{3,4},{4,5},{5,6},{6,7},{7,8},{8,9},{9,10},{10,1... | collective-permute-start | bytes 49160 | tf_op jit(solution)/shard_map/ppermute | solution.py:21
  300.9 12.4 %collective-permute-start.32 = (f32[2,8,1,256]{3,1,2,0:T(8,128)S(1)}, f32[2,8,1,256]{3,1,2,0:T(8,128)S(1)}, u32[]{:S(2)}, u32[]{:S(2)}) collective-permute-start(f32[2,8,1,256]{3,1,2,0:T(8,128)S(1)} %copy.246), channel_id=1, source_target_pairs={{1,0},{2,1},{3,2},{4,3},{5,4},{6,5},{7,6},{8,7},{9,8},{10,9},{11,1... | collective-permute-start | bytes 49160 | tf_op jit(solution)/shard_map/ppermute | solution.py:22
  302.8 10.5 %collective-permute-start.31 = (f32[2,1,16,256]{3,2,1,0:T(8,128)S(1)}, f32[2,1,16,256]{3,2,1,0:T(8,128)S(1)}, u32[]{:S(2)}, u32[]{:S(2)}) collective-permute-start(f32[2,1,16,256]{3,2,1,0:T(8,128)S(1)} %get-tuple-element.39), channel_id=1, source_target_pairs={{0,16},{16,32},{32,48},{48,64},{64,80},{80,96},{96,112},{112,128},... | collective-permute-start | bytes 98312 | tf_op jit(solution)/shard_map/ppermute | solution.py:21
  310.6 9.4 %collective-permute-start.30 = (f32[2,1,16,256]{3,2,1,0:T(8,128)S(1)}, f32[2,1,16,256]{3,2,1,0:T(8,128)S(1)}, u32[]{:S(2)}, u32[]{:S(2)}) collective-permute-start(f32[2,1,16,256]{3,2,1,0:T(8,128)S(1)} %get-tuple-element.40), channel_id=1, source_target_pairs={{16,0},{32,16},{48,32},{64,48},{80,64},{96,80},{112,96},{128,112},... | collective-permute-start | bytes 98312 | tf_op jit(solution)/shard_map/ppermute | solution.py:22
where the time goes:
time: 322 us; the launch traced here: 321 us
  blocking collectives  143 us (44%)
  starting transfers between devices  136 us (42%)
  waiting for transfers between devices  25.6 us (8%)
  local copies, waits for them, and re-layouts  7.75 us (2%)
  other arithmetic  7.63 us (2%)
    pmax x5, blocking collectives, one_axis_at_a_time(): array = lax.pmax(array, axis)  84.1 us
    ppermute x16, starting transfers between devices, extended(): lax.ppermute(last, axis, up)  80.1 us
    all_to_all x1, blocking collectives, shards(): lax.all_to_all(right_side, GX, split_axis=2, concat_axis=0, tiled=True)  58.5 us
    ppermute x16, starting transfers between devices, extended(): lax.ppermute(initial, axis, [(b, a) for a, b in up])  39.5 us
    ppermute x16, waiting for transfers between devices, extended(): lax.ppermute(initial, axis, [(b, a) for a, b in up])  22.5 us
    all_to_all x1, starting transfers between devices, shards(): lax.all_to_all(jnp.flip(columns, 0), GX, split_axis=0, concat_axis=2, til...  9.38 us
    ppermute x2, starting transfers between devices, passed_along(): return lax.ppermute(array, axis, pairs)  6.77 us
  transfers between devices with their start and end apart: 35, of which 9 were waited for; matrix products, arithmetic and copies ran while one was open for 1% of the time, Pallas kernels for 0%

commit v1 on v0

v1 whole, which is shorter than its diff:
```python
import jax
import jax.numpy as jnp
from jax import lax
from jax.experimental import pallas as pl
from jax.experimental.pallas import tpu as pltpu
from jax.sharding import Mesh
from jax.sharding import PartitionSpec as P

ITERS = 8
GX = ("gx_0", "gx_1")
GY = ("gy_0", "gy_1", "gy_2")
BX, BY, NZ = 8, 16, 256
H = 8
EX, EY = BX + 2 * H, BY + 2 * H
VMEM = pl.BlockSpec(memory_space=pltpu.VMEM)
SMEM = pl.BlockSpec(memory_space=pltpu.SMEM)


def shift_pairs(n):
    up = [(i, i + 1) for i in range(n - 1)]
    return up, [(b, a) for a, b in up]


def both_ways(array_up, array_down, axes):
    up, down = shift_pairs(lax.axis_size(axes))
    return lax.ppermute(array_up, axes, up), lax.ppermute(array_down, axes, down)


def max_over(value, axes):
    n = lax.axis_size(axes)
    sent = jnp.broadcast_to(value[None], (n, 1, 128))
    return jnp.max(lax.all_to_all(sent, axes, 0, 0, tiled=True), axis=0)


def roll(x, by, axis):
    return pltpu.roll(x, by % x.shape[axis], axis)


def basis(first, second, d, cx, cy, cz, out):
    out[0] = first[H : H + BX, H : H + BY, :]
    bufs = (first, second)
    for k in range(1, ITERS + 1):
        now, nxt = bufs[(k - 1) % 2], bufs[k % 2]

        def row(r, carry, k=k, now=now, nxt=nxt):
            v = now[r]
            y = cy[r]
            z = cz[r]
            a = d[r] * v - cx[r] * now[r + 1] - cx[r - 1] * now[r - 1]
            a = a - y * roll(v, -1, 0) - roll(y * v, 1, 0)
            a = a - z * roll(v, -1, 1) - roll(z * v, 1, 1)
            nxt[r] = 0.5 * a if k == 1 else a - nxt[r]
            return carry

        lax.fori_loop(k, EX - k, row, 0)
        out[k] = nxt[H : H + BX, H : H + BY, :]


def prepare_kernel(keep, own, x_low, x_high, y_low, y_high, d, cx, cy, cz, top, out, shift, first, second):
    for i, ref in enumerate((shift, cx, cy, cz, first)):
        ref[0:H, H : H + BY, :] = x_low[i]
        ref[H : H + BX, H : H + BY, :] = own[i]
        ref[H + BX : EX, H : H + BY, :] = x_high[i]
        ref[:, 0:H, :] = y_low[i]
        ref[:, H + BY : EY, :] = y_high[i]
    lane = lax.broadcasted_iota(jnp.int32, (EY, NZ), 1)
    line = lax.broadcasted_iota(jnp.int32, (EY, NZ), 0)

    def diagonal(r, most):
        y = cy[r]
        z = cz[r]
        total = cx[r] + cx[r - 1] + y + roll(y, 1, 0) + z + jnp.where(lane > 0, roll(z, 1, 1), 0.0)
        diag = shift[r] + total
        d[r] = diag
        return jnp.maximum(most, jnp.where(line > 0, diag + total, 0.0))

    most = lax.fori_loop(1, EX, diagonal, jnp.zeros((EY, NZ), jnp.float32))
    bound = jnp.max(jnp.max(most, axis=0, keepdims=True), axis=1, keepdims=True)
    top[...] = jnp.broadcast_to(bound, top.shape)
    scale = jnp.broadcast_to(4.0 / bound, (1, NZ))
    keep_y = jnp.where(line == H + BY - 1, keep[1], 1.0) * scale
    keep_z = jnp.where(lane == NZ - 1, 0.0, 1.0) * scale

    def rescale(r, carry):
        d[r] = d[r] * scale - 2.0
        cx[r] = cx[r] * (scale * jnp.where(r == H + BX - 1, keep[0], 1.0))
        cy[r] = cy[r] * keep_y
        cz[r] = cz[r] * keep_z
        return carry

    lax.fori_loop(0, EX, rescale, 0)
    basis(first, second, d, cx, cy, cz, out)


def mirror_kernel(own, x_low, x_high, y_low, y_high, d, cx, cy, cz, out, first, second):
    for b, block in enumerate((x_low, own, x_high)):
        for i in range(BX):
            first[b * BX + i, H : H + BY, :] = block[BX - 1 - i]
            first[b * BX + i, 0:H, :] = y_low[b, BX - 1 - i]
            first[b * BX + i, H + BY : EY, :] = y_high[b, BX - 1 - i]
    basis(first, second, d, cx, cy, cz, out)


def polynomials(low, high, bound, top):
    lmin = low * bound
    lmax = high * bound
    theta = (lmax + lmin) / 2.0
    delta = (lmax - lmin) / 2.0
    sigma = theta / delta
    rho = 1.0 / sigma
    half = 0.5 * top
    zero = jnp.zeros_like(bound)
    n = ITERS + 1
    x = [zero] * n
    r = [zero + 1.0] + [zero] * ITERS
    d = [r[0] / theta] + [zero] * ITERS
    for _ in range(ITERS):
        x = [a + b for a, b in zip(x, d)]
        at = d + [zero]
        moved = [0.5 * at[1], at[0] + 0.5 * at[2]] + [0.5 * (at[k - 1] + at[k + 1]) for k in range(2, n)]
        r = [a - half * (b + c) for a, b, c in zip(r, d, moved)]
        rho_new = 1.0 / (2.0 * sigma - rho)
        by, of = rho_new * rho, 2.0 * rho_new / delta
        d = [by * a + of * b for a, b in zip(d, r)]
        rho = rho_new
    return x, r


def combine_kernel(low, high, bound, top, plain, mirrored, pressure, residual):
    found = [polynomials(low[f], high[f], bound[...], top[...]) for f in range(2)]
    sums, gaps = [], []
    for part in range(2):
        sums.append([0.5 * (a + b) for a, b in zip(found[0][part], found[1][part])])
        gaps.append([0.5 * (a - b) for a, b in zip(found[0][part], found[1][part])])
    tiles = [(i, j) for i in range(0, BY, 8) for j in range(0, NZ, 128)]

    def row(r, carry):
        for i, j in tiles:
            p = q = None
            for k in range(ITERS + 1):
                a = plain[k, r, i : i + 8, j : j + 128]
                b = mirrored[k, r, i : i + 8, j : j + 128]
                if k < ITERS:
                    t = sums[0][k] * a + gaps[0][k] * b
                    p = t if p is None else p + t
                t = sums[1][k] * a + gaps[1][k] * b
                q = t if q is None else q + t
            pressure[r, i : i + 8, j : j + 128] = p
            residual[r, i : i + 8, j : j + 128] = q
        return carry

    lax.fori_loop(0, BX, row, 0)


def f32(*shape):
    return jax.ShapeDtypeStruct(shape, jnp.float32)


def shards(right_side, shift, coef_x, coef_y, coef_z, low_frac, high_frac):
    nx, ny = lax.axis_size(GX), lax.axis_size(GY)
    me_x, me_y = lax.axis_index(GX), lax.axis_index(GY)
    up_x, up_y = shift_pairs(nx)[0], shift_pairs(ny)[0]

    before_x = lax.ppermute(coef_x[-1], GX, up_x)
    before_y = lax.ppermute(coef_y[:, -1], GY, up_y)
    own = jnp.stack([shift, coef_x, coef_y, coef_z, right_side])
    x_low, x_high = both_ways(own, own, GX)
    mirror = lax.ppermute(right_side, GX, [(i, nx - 1 - i) for i in range(nx)])

    low_x = jnp.concatenate([before_x[None], coef_x[:-1]], 0)
    low_y = jnp.concatenate([before_y[:, None], coef_y[:, :-1]], 1)
    low_z = jnp.pad(coef_z, ((0, 0), (0, 0), (1, 0)))[:, :, :-1]
    most = jnp.max(shift + 2.0 * (coef_x + low_x + coef_y + low_y + coef_z + low_z))
    bound = max_over(max_over(jnp.full((1, 128), most), GY), GX)
    bound = jnp.broadcast_to(bound, (8, 128))

    sides = jnp.concatenate([x_low, own, x_high], 1)
    y_low, y_high = both_ways(sides[:, :, BY - H :], sides[:, :, :H], GY)
    keep = jnp.stack([me_x < nx - 1, me_y < ny - 1]).astype(jnp.float32)
    wide = f32(EX, EY, NZ)
    scratch = pltpu.VMEM((EX, EY, NZ), jnp.float32)
    basis_out = f32(ITERS + 1, BX, BY, NZ)
    *operator, top, plain = pl.pallas_call(
        prepare_kernel,
        out_shape=(wide, wide, wide, wide, f32(8, 128), basis_out),
        in_specs=[SMEM] + [VMEM] * 5,
        out_specs=(VMEM,) * 6,
        scratch_shapes=[scratch] * 3,
        compiler_params=pltpu.CompilerParams(vmem_limit_bytes=16 << 20),
        cost_estimate=pl.CostEstimate(flops=30_000_000, bytes_accessed=8_000_000, transcendentals=0),
    )(keep, own, x_low, x_high, y_low, y_high)

    m_low, m_high = both_ways(mirror, mirror, GX)
    n_low, n_high = both_ways(
        jnp.stack([a[:, BY - H :] for a in (m_low, mirror, m_high)]),
        jnp.stack([a[:, :H] for a in (m_low, mirror, m_high)]),
        GY,
    )
    mirrored = pl.pallas_call(
        mirror_kernel,
        out_shape=basis_out,
        in_specs=[VMEM] * 9,
        out_specs=VMEM,
        scratch_shapes=[scratch] * 2,
        compiler_params=pltpu.CompilerParams(vmem_limit_bytes=16 << 20),
        cost_estimate=pl.CostEstimate(flops=20_000_000, bytes_accessed=6_000_000, transcendentals=0),
    )(mirror, m_low, m_high, n_low, n_high, *operator)

    return pl.pallas_call(
        combine_kernel,
        out_shape=(f32(BX, BY, NZ), f32(BX, BY, NZ)),
        in_specs=[SMEM, SMEM] + [VMEM] * 4,
        out_specs=(VMEM, VMEM),
        compiler_params=pltpu.CompilerParams(vmem_limit_bytes=8 << 20),
        cost_estimate=pl.CostEstimate(flops=3_000_000, bytes_accessed=3_000_000, transcendentals=0),
    )(low_frac, high_frac, bound, top, plain, mirrored)


def solution(mesh):
    torus = Mesh(mesh.devices.reshape(32, 2, 4, 2, 2), GX + GY)
    block = P(GX, GY, None)
    return jax.shard_map(
        shards,
        mesh=torus,
        in_specs=(block,) * 5 + (P(), P()),
        out_specs=(block, block),
        check_vma=False,
    )
```

time: 322 us -> 155 us (0.48)
  the two profiles are of different devices: /device:TPU:102 before, /device:TPU:33 now
where the time goes in v1:
time: 155 us; the launch traced here: 154 us
  starting transfers between devices  84.2 us (54%)
  Pallas kernels  28.2 us (18%)
  waiting for transfers between devices  16.5 us (11%)
  blocking collectives  10.2 us (7%)
  local copies, waits for them, and re-layouts  9.91 us (6%)
  other arithmetic  4.38 us (3%)
    all_to_all x1, starting transfers between devices, max_over(): return jnp.max(lax.all_to_all(sent, axes, 0, 0, tiled=True), axis=0)  29.6 us
    ppermute x1, starting transfers between devices, shards(): mirror = lax.ppermute(right_side, GX, [(i, nx - 1 - i) for i in range(nx)])  21.2 us
    ppermute x4, starting transfers between devices, both_ways(): lax.ppermute(array_up, axes, up)  16.1 us
    ppermute x4, waiting for transfers between devices, both_ways(): lax.ppermute(array_down, axes, down)  14.8 us
    pallas_call x1, Pallas kernels, shards(): pl.pallas_call(prepare_kernel, out_shape=(wide, wide, wide, wide, f32(8,...  14.5 us
    pallas_call x1, Pallas kernels, shards(): pl.pallas_call(mirror_kernel, out_shape=basis_out, in_specs=[VMEM] * 9, o...  11.8 us
    all_to_all x1, blocking collectives, max_over(): return jnp.max(lax.all_to_all(sent, axes, 0, 0, tiled=True), axis=0)  10.2 us
    ppermute x4, starting transfers between devices, both_ways(): lax.ppermute(array_down, axes, down)  9.95 us
  transfers between devices with their start and end apart: 12, of which 3 were waited for; matrix products, arithmetic and copies ran while one was open for 6% of the time, Pallas kernels for 9%

profile of v1, /device:TPU:33, one launch (start us, length us, event | category | flops | bytes accessed | tf_op | source)
XLA Modules:
  0.0 154.3 jit_solution(4762641978085358018)
XLA Ops:
  0.6 0.9 bitcast_dynamic-update-slice_fusion.4
  1.5 0.9 bitcast_dynamic-update-slice_fusion.3
  2.5 0.9 bitcast_dynamic-update-slice_fusion.2
  3.4 0.9 bitcast_dynamic-update-slice_fusion.1
  4.3 0.9 bitcast_dynamic-update-slice_fusion.own
  5.2 4.7 %collective-permute-start.2 = (f32[5,8,16,256]{3,2,1,0:T(8,128)S(1)}, f32[5,8,16,256]{3,2,1,0:T(8,128)S(1)}, u32[]{:S(2)}, u32[]{:S(2)}) collective-permute-start(f32[5,8,16,256]{3,2,1,0:T(8,128)S(1)} %bitcast_dynamic-update-slice_fusion.own), channel_id=1, source_target_pairs={{0,16},{16,32},{32,48},{48,64},{64,80},{80,96},{96,112},{112,128},... | collective-permute-start | bytes 1966088 | tf_op jit(solution)/shard_map/ppermute | solution.py:26
  9.9 3.0 %collective-permute-start.3 = (f32[5,8,16,256]{3,2,1,0:T(8,128)S(1)}, f32[5,8,16,256]{3,2,1,0:T(8,128)S(1)}, u32[]{:S(2)}, u32[]{:S(2)}) collective-permute-start(f32[5,8,16,256]{3,2,1,0:T(8,128)S(1)} %bitcast_dynamic-update-slice_fusion.own), channel_id=1, source_target_pairs={{16,0},{32,16},{48,32},{64,48},{80,64},{96,80},{112,96},{128,112},... | collective-permute-start | bytes 1966088 | tf_op jit(solution)/shard_map/ppermute | solution.py:26
  12.9 0.7 slice_bitcast_fusion.6
  13.7 3.7 %collective-permute-start = (f32[16,256]{1,0:T(8,128)S(1)}, f32[16,256]{1,0:T(8,128)S(1)}, u32[]{:S(2)}, u32[]{:S(2)}) collective-permute-start(f32[16,256]{1,0:T(8,128)S(1)} %slice_bitcast_fusion.6), channel_id=1, source_target_pairs={{0,16},{16,32},{32,48},{48,64},{64,80},{80,96},{96,112},{112,128},... | collective-permute-start | bytes 49160 | tf_op jit(solution)/shard_map/ppermute | solution.py:164
  17.4 0.9 slice.41
  18.3 3.6 %collective-permute-start.1 = (f32[8,256]{1,0:T(8,128)S(1)}, f32[8,256]{1,0:T(8,128)S(1)}, u32[]{:S(2)}, u32[]{:S(2)}) collective-permute-start(f32[8,256]{1,0:T(8,128)S(1)} %bitcast.37), channel_id=1, source_target_pairs={{0,1},{1,2},{2,3},{3,4},{4,5},{5,6},{6,7},{7,8},{8,9},{9,10},{10,1... | collective-permute-start | bytes 24584 | tf_op jit(solution)/shard_map/ppermute | solution.py:165
  21.9 21.2 %collective-permute-start.6 = (f32[8,16,256]{2,1,0:T(8,128)}, f32[8,16,256]{2,1,0:T(8,128)S(1)}, u32[]{:S(2)}, u32[]{:S(2)}) collective-permute-start(f32[8,16,256]{2,1,0:T(8,128)} %param.7), channel_id=1, source_target_pairs={{0,1008},{16,992},{32,976},{48,960},{64,944},{80,928},{96,912},{11... | collective-permute-start | bytes 393224 | tf_op jit(solution)/shard_map/ppermute | solution.py:168
  43.1 0.9 slice.40
  44.0 0.0 collective-permute-done.1
  44.0 0.0 collective-permute-done
  44.0 1.9 %fusion.3 = f32[]{:T(128)} fusion(f32[8,16,256]{2,1,0:T(8,128)} %param.8, f32[8,16,256]{2,1,0:T(8,128)} %param.11, f32[8,16,256]{2,1,0:T(8,128)} %param.10, f32[8,16,256]{2,1,0:T(8,128)} %param.9, f32[7,16,256]{2,1,0:T(8,128)S(1)} %slice.40, f32[1,16,256]{2,1,0:T(8,128)S(1)} %bitcast.36, f32[8,15,256]{2,1,0:T(8,128)} %bitcast.34, f32[8,1,256]{2,1,0:T(1,128)S(1)} %copy.15), kind=kLoop, calls=%fused_computation.7 | loop fusion | flops 327679 | bytes 786436 | tf_op jit(solution)/shard_map/reduce_max | solution.py:173
  46.0 0.6 broadcast_in_dim_broadcast_in_dim_broadcast_in_dim.3
  46.6 10.2 %all_to_all.10 = f32[16,1,128]{2,1,0:T(1,128)S(1)} all-to-all(f32[16,1,128]{2,1,0:T(1,128)S(1)} %broadcast_in_dim_broadcast_in_dim_broadcast_in_dim.3), channel_id=1, replica_groups=mesh['gx_0'=32,'gx_1'=2,'gy_0'=4,'gy_1'=2,'gy_2'=2] {'gy_0','gy_1','gy_2'}, dimensions={0} | all-to-all | bytes 16384 | tf_op jit(solution)/shard_map/all_to_all | solution.py:32
  56.8 0.6 broadcast_in_dim.19
  57.5 29.6 %all-to-all-start.1 = ((f32[64,1,128]{2,1,0:T(1,128)}), f32[64,1,128]{2,1,0:T(1,128)}, u32[]{:S(2)}, u32[]{:S(2)}) async-start(f32[64,1,128]{2,1,0:T(1,128)} %broadcast_in_dim.19), calls=%async_computation.1 | async-start | bytes 65536 | tf_op jit(solution)/shard_map/all_to_all | solution.py:32
  87.0 0.0 collective-permute-done.6.own
  87.0 4.6 %collective-permute-start.7 = (f32[8,16,256]{2,1,0:T(8,128)S(1)}, f32[8,16,256]{2,1,0:T(8,128)S(1)}, u32[]{:S(2)}, u32[]{:S(2)}) collective-permute-start(f32[8,16,256]{2,1,0:T(8,128)S(1)} %collective-permute-done.6.own), channel_id=1, source_target_pairs={{0,16},{16,32},{32,48},{48,64},{64,80},{80,96},{96,112},{112,128},... | collective-permute-start | bytes 393224 | tf_op jit(solution)/shard_map/ppermute | solution.py:26
  91.6 3.1 %collective-permute-start.8 = (f32[8,16,256]{2,1,0:T(8,128)S(1)}, f32[8,16,256]{2,1,0:T(8,128)S(1)}, u32[]{:S(2)}, u32[]{:S(2)}) collective-permute-start(f32[8,16,256]{2,1,0:T(8,128)S(1)} %collective-permute-done.6.own), channel_id=1, source_target_pairs={{16,0},{32,16},{48,32},{64,48},{80,64},{96,80},{112,96},{128,112},... | collective-permute-start | bytes 393224 | tf_op jit(solution)/shard_map/ppermute | solution.py:26
  94.7 0.0 collective-permute-done.2.x_low
  94.8 0.0 collective-permute-done.3.x_high
  94.8 0.2 pad_maximum_fusion
  95.0 1.5 fusion.7
  96.5 3.3 %collective-permute-start.4 = (f32[5,24,8,256]{3,2,1,0:T(8,128)}, f32[5,24,8,256]{3,2,1,0:T(8,128)S(1)}, u32[]{:S(2)}, u32[]{:S(2)}) collective-permute-start(f32[5,24,8,256]{3,2,1,0:T(8,128)} %get-tuple-element.15), channel_id=1, source_target_pairs={{0,1},{1,2},{2,3},{3,4},{4,5},{5,6},{6,7},{7,8},{8,9},{9,10},{10,1... | collective-permute-start | bytes 2949128 | tf_op jit(solution)/shard_map/ppermute | solution.py:26
  99.7 1.9 %collective-permute-start.5 = (f32[5,24,8,256]{3,2,1,0:T(8,128)}, f32[5,24,8,256]{3,2,1,0:T(8,128)}, u32[]{:S(2)}, u32[]{:S(2)}) collective-permute-start(f32[5,24,8,256]{3,2,1,0:T(8,128)} %get-tuple-element.14), channel_id=1, source_target_pairs={{1,0},{2,1},{3,2},{4,3},{5,4},{6,5},{7,6},{8,7},{9,8},{10,9},{11,1... | collective-permute-start | bytes 2949128 | tf_op jit(solution)/shard_map/ppermute | solution.py:26
  101.7 0.0 collective-permute-done.7.x_low
  101.7 0.0 collective-permute-done.8.x_high
  101.7 0.7 pad_maximum_fusion.2
  102.4 1.9 %collective-permute-start.10 = (f32[3,8,8,256]{3,2,1,0:T(8,128)}, f32[3,8,8,256]{3,2,1,0:T(8,128)S(1)}, u32[]{:S(2)}, u32[]{:S(2)}) collective-permute-start(f32[3,8,8,256]{3,2,1,0:T(8,128)} %pad_maximum_fusion.2), channel_id=1, source_target_pairs={{1,0},{2,1},{3,2},{4,3},{5,4},{6,5},{7,6},{8,7},{9,8},{10,9},{11,1... | collective-permute-start | bytes 589832 | tf_op jit(solution)/shard_map/ppermute | solution.py:26
  104.3 0.7 pad_maximum_fusion.1
  105.0 3.6 %collective-permute-start.9 = (f32[3,8,8,256]{3,2,1,0:T(8,128)}, f32[3,8,8,256]{3,2,1,0:T(8,128)}, u32[]{:S(2)}, u32[]{:S(2)}) collective-permute-start(f32[3,8,8,256]{3,2,1,0:T(8,128)} %pad_maximum_fusion.1), channel_id=1, source_target_pairs={{0,1},{1,2},{2,3},{3,4},{4,5},{5,6},{6,7},{7,8},{8,9},{9,10},{10,1... | collective-permute-start | bytes 589832 | tf_op jit(solution)/shard_map/ppermute | solution.py:26
  108.7 0.1 add_convert_fusion.keep
  108.8 1.2 all-to-all-done.1
  110.0 0.8 reduce_max.29
  110.8 0.4 collective-permute-done.4.y_low
  111.2 14.8 %collective-permute-done.5.y_high = f32[5,24,8,256]{3,2,1,0:T(8,128)} collective-permute-done((f32[5,24,8,256]{3,2,1,0:T(8,128)}, f32[5,24,8,256]{3,2,1,0:T(8,128)}, u32[]{:S(2)}, u32[]{:S(2)}) %collective-permute-start.5) | collective-permute-done | bytes 983072 | tf_op jit(solution)/shard_map/ppermute | solution.py:26
  126.0 14.5 %shard_map.86 = (f32[24,32,256]{2,1,0:T(8,128)S(1)}, f32[24,32,256]{2,1,0:T(8,128)S(1)}, f32[24,32,256]{2,1,0:T(8,128)S(1)}, f32[24,32,256]{2,1,0:T(8,128)S(1)},...) custom-call(f32[2]{0:T(128)S(1)} %add_convert_fusion.keep, ...), custom_call_target="tpu_custom_call" | custom-call | flops 30000000 | bytes 8000000 | tf_op jit(solution)/shard_map/pallas_call | solution.py:183
  140.6 0.0 collective-permute-done.10.y_high
  140.6 0.0 collective-permute-done.9.y_low
  140.6 0.0 copy-start
  140.6 0.0 copy-start.1
  140.6 11.8 %shard_map.87.mirrored = f32[9,8,16,256]{3,2,1,0:T(8,128)S(1)} custom-call(f32[8,16,256]{2,1,0:T(8,128)S(1)} %collective-permute-done.6.own, f32[8,16,256]{2,1,0:T(8,128)S(1)} %collective-permute-done.7.x_low, f32[8,16,256]{2,1,0:T(8,128)S(1)} %collective-permute-done.8.x_high, f32[3,8,8,256]{3,2,1,0:T(8,128)} %collective-permute-done.9.y_low, ...), custom_call_target="tpu_custom_call" | custom-call | flops 20000000 | bytes 6000000 | tf_op jit(solution)/shard_map/pallas_call | solution.py:199
  152.4 0.0 copy-done
  152.5 0.0 copy-done.1
  152.5 1.9 %shard_map.88 = (f32[8,16,256]{2,1,0:T(8,128)}, f32[8,16,256]{2,1,0:T(8,128)}) custom-call(f32[2]{0:T(128)S(1)} %copy-done, f32[2]{0:T(128)S(1)} %copy-done.1, f32[8,128]{1,0:T(8,128)S(1)} %broadcast_in_dim.20.bound, f32[8,128]{1,0:T(8,128)S(1)} %get-tuple-element.8.top, f32[9,8,16,256]{3,2,1,0:T(8,128)S(1)} %get-tuple-element.9.plain, ...), custom_call_target="tpu_custom_call" | custom-call | flops 3000000 | bytes 3000000 | tf_op jit(solution)/shard_map/pallas_call | solution.py:209
  (7 shorter events, 0.1 us)
Async XLA Ops:
  5.2 89.5 %collective-permute-start.2 = (f32[5,8,16,256]{3,2,1,0:T(8,128)S(1)}, f32[5,8,16,256]{3,2,1,0:T(8,128)S(1)}, u32[]{:S(2)}, u32[]{:S(2)}) collective-permute-start(f32[5,8,16,256]{3,2,1,0:T(8,128)S(1)} %bitcast_dynamic-update-slice_fusion.own), channel_id=1, source_target_pairs={{0,16},{16,32},{32,48},{48,64},{64,80},{80,96},{96,112},{112,128},... | collective-permute-start | bytes 1966088 | tf_op jit(solution)/shard_map/ppermute | solution.py:26
  9.9 84.9 %collective-permute-start.3 = (f32[5,8,16,256]{3,2,1,0:T(8,128)S(1)}, f32[5,8,16,256]{3,2,1,0:T(8,128)S(1)}, u32[]{:S(2)}, u32[]{:S(2)}) collective-permute-start(f32[5,8,16,256]{3,2,1,0:T(8,128)S(1)} %bitcast_dynamic-update-slice_fusion.own), channel_id=1, source_target_pairs={{16,0},{32,16},{48,32},{64,48},{80,64},{96,80},{112,96},{128,112},... | collective-permute-start | bytes 1966088 | tf_op jit(solution)/shard_map/ppermute | solution.py:26
  13.7 30.4 %collective-permute-start = (f32[16,256]{1,0:T(8,128)S(1)}, f32[16,256]{1,0:T(8,128)S(1)}, u32[]{:S(2)}, u32[]{:S(2)}) collective-permute-start(f32[16,256]{1,0:T(8,128)S(1)} %slice_bitcast_fusion.6), channel_id=1, source_target_pairs={{0,16},{16,32},{32,48},{48,64},{64,80},{80,96},{96,112},{112,128},... | collective-permute-start | bytes 49160 | tf_op jit(solution)/shard_map/ppermute | solution.py:164
  18.3 25.7 %collective-permute-start.1 = (f32[8,256]{1,0:T(8,128)S(1)}, f32[8,256]{1,0:T(8,128)S(1)}, u32[]{:S(2)}, u32[]{:S(2)}) collective-permute-start(f32[8,256]{1,0:T(8,128)S(1)} %bitcast.37), channel_id=1, source_target_pairs={{0,1},{1,2},{2,3},{3,4},{4,5},{5,6},{6,7},{7,8},{8,9},{9,10},{10,1... | collective-permute-start | bytes 24584 | tf_op jit(solution)/shard_map/ppermute | solution.py:165
  21.9 65.1 %collective-permute-start.6 = (f32[8,16,256]{2,1,0:T(8,128)}, f32[8,16,256]{2,1,0:T(8,128)S(1)}, u32[]{:S(2)}, u32[]{:S(2)}) collective-permute-start(f32[8,16,256]{2,1,0:T(8,128)} %param.7), channel_id=1, source_target_pairs={{0,1008},{16,992},{32,976},{48,960},{64,944},{80,928},{96,912},{11... | collective-permute-start | bytes 393224 | tf_op jit(solution)/shard_map/ppermute | solution.py:168
  57.5 52.5 %all-to-all-start.1 = ((f32[64,1,128]{2,1,0:T(1,128)}), f32[64,1,128]{2,1,0:T(1,128)}, u32[]{:S(2)}, u32[]{:S(2)}) async-start(f32[64,1,128]{2,1,0:T(1,128)} %broadcast_in_dim.19), calls=%async_computation.1 | async-start | bytes 65536 | tf_op jit(solution)/shard_map/all_to_all | solution.py:32
  87.0 14.7 %collective-permute-start.7 = (f32[8,16,256]{2,1,0:T(8,128)S(1)}, f32[8,16,256]{2,1,0:T(8,128)S(1)}, u32[]{:S(2)}, u32[]{:S(2)}) collective-permute-start(f32[8,16,256]{2,1,0:T(8,128)S(1)} %collective-permute-done.6.own), channel_id=1, source_target_pairs={{0,16},{16,32},{32,48},{48,64},{64,80},{80,96},{96,112},{112,128},... | collective-permute-start | bytes 393224 | tf_op jit(solution)/shard_map/ppermute | solution.py:26
  91.6 10.1 %collective-permute-start.8 = (f32[8,16,256]{2,1,0:T(8,128)S(1)}, f32[8,16,256]{2,1,0:T(8,128)S(1)}, u32[]{:S(2)}, u32[]{:S(2)}) collective-permute-start(f32[8,16,256]{2,1,0:T(8,128)S(1)} %collective-permute-done.6.own), channel_id=1, source_target_pairs={{16,0},{32,16},{48,32},{64,48},{80,64},{96,80},{112,96},{128,112},... | collective-permute-start | bytes 393224 | tf_op jit(solution)/shard_map/ppermute | solution.py:26
  96.5 14.7 %collective-permute-start.4 = (f32[5,24,8,256]{3,2,1,0:T(8,128)}, f32[5,24,8,256]{3,2,1,0:T(8,128)S(1)}, u32[]{:S(2)}, u32[]{:S(2)}) collective-permute-start(f32[5,24,8,256]{3,2,1,0:T(8,128)} %get-tuple-element.15), channel_id=1, source_target_pairs={{0,1},{1,2},{2,3},{3,4},{4,5},{5,6},{6,7},{7,8},{8,9},{9,10},{10,1... | collective-permute-start | bytes 2949128 | tf_op jit(solution)/shard_map/ppermute | solution.py:26
  99.7 26.3 %collective-permute-start.5 = (f32[5,24,8,256]{3,2,1,0:T(8,128)}, f32[5,24,8,256]{3,2,1,0:T(8,128)}, u32[]{:S(2)}, u32[]{:S(2)}) collective-permute-start(f32[5,24,8,256]{3,2,1,0:T(8,128)} %get-tuple-element.14), channel_id=1, source_target_pairs={{1,0},{2,1},{3,2},{4,3},{5,4},{6,5},{7,6},{8,7},{9,8},{10,9},{11,1... | collective-permute-start | bytes 2949128 | tf_op jit(solution)/shard_map/ppermute | solution.py:26
  102.4 38.1 %collective-permute-start.10 = (f32[3,8,8,256]{3,2,1,0:T(8,128)}, f32[3,8,8,256]{3,2,1,0:T(8,128)S(1)}, u32[]{:S(2)}, u32[]{:S(2)}) collective-permute-start(f32[3,8,8,256]{3,2,1,0:T(8,128)} %pad_maximum_fusion.2), channel_id=1, source_target_pairs={{1,0},{2,1},{3,2},{4,3},{5,4},{6,5},{7,6},{8,7},{9,8},{10,9},{11,1... | collective-permute-start | bytes 589832 | tf_op jit(solution)/shard_map/ppermute | solution.py:26
  105.0 35.5 %collective-permute-start.9 = (f32[3,8,8,256]{3,2,1,0:T(8,128)}, f32[3,8,8,256]{3,2,1,0:T(8,128)}, u32[]{:S(2)}, u32[]{:S(2)}) collective-permute-start(f32[3,8,8,256]{3,2,1,0:T(8,128)} %pad_maximum_fusion.1), channel_id=1, source_target_pairs={{0,1},{1,2},{2,3},{3,4},{4,5},{5,6},{6,7},{7,8},{8,9},{9,10},{10,1... | collective-permute-start | bytes 589832 | tf_op jit(solution)/shard_map/ppermute | solution.py:26
  140.6 11.9 %copy-start = (f32[2]{0:T(128)S(1)}, f32[2]{0:T(128)}, u32[]{:S(2)}) copy-start(f32[2]{0:T(128)} %low.1) | copy-start | bytes 28
  140.6 11.9 %copy-start.1 = (f32[2]{0:T(128)S(1)}, f32[2]{0:T(128)}, u32[]{:S(2)}) copy-start(f32[2]{0:T(128)} %high.1) | copy-start | bytes 28

commit v2 on v1

v2 whole, which is shorter than its diff:
```python
import jax
import jax.numpy as jnp
from jax import lax
from jax.experimental import pallas as pl
from jax.experimental.pallas import tpu as pltpu
from jax.sharding import Mesh
from jax.sharding import PartitionSpec as P


ITERS = 8
GX = ("gx_0", "gx_1")
GY = ("gy_0", "gy_1", "gy_2")
BX, BY, NZ = 8, 16, 256
H = 8
PAD = 8
EX, EY = BX + 2 * H, BY + 2 * H
NEAR = ("gx_1",) + GY
VMEM = pl.BlockSpec(memory_space=pltpu.VMEM)
SMEM = pl.BlockSpec(memory_space=pltpu.SMEM)


def shift_pairs(n):
    up = [(i, i + 1) for i in range(n - 1)]
    return up, [(b, a) for a, b in up]


def both_ways(array_up, array_down, axes):
    up, down = shift_pairs(lax.axis_size(axes))
    return lax.ppermute(array_up, axes, up), lax.ppermute(array_down, axes, down)


def turn(x, by):
    return pltpu.roll(x, by % 128, 1)


def basis(first, second, d, cx, cy, ly, cz, lz, out):
    lane = lax.broadcasted_iota(jnp.int32, (8, 128), 1)
    at_start, at_end = lane == 0, lane == 127
    bufs = (first, second)
    for k in range(1, ITERS + 1):
        now, nxt = bufs[(k - 1) % 2], bufs[k % 2]
        for tile in range(EY // 8):
            inner = H <= 8 * tile < H + BY
            start = k if inner else k + 1
            y = PAD + 8 * tile
            if start >= EX - start or (k == ITERS and not inner):
                continue
            below = [now[start - 1, h, y : y + 8, :] for h in range(2)]
            here = [now[start, h, y : y + 8, :] for h in range(2)]
            face = [cx[start - 1, h, y : y + 8, :] for h in range(2)]
            for r in range(start, EX - start):
                above = [now[r + 1, h, y : y + 8, :] for h in range(2)]
                face_up = [cx[r, h, y : y + 8, :] for h in range(2)]
                ahead = [turn(v, -1) for v in here]
                behind = [turn(v, 1) for v in here]
                ahead[0] = jnp.where(at_end, ahead[1], ahead[0])
                behind[1] = jnp.where(at_start, behind[0], behind[1])
                for h in range(2):
                    a = d[r, h, y : y + 8, :] * here[h] - (face_up[h] * above[h] + face[h] * below[h])
                    side = cy[r, h, y : y + 8, :] * now[r, h, y + 1 : y + 9, :]
                    side = side + ly[r, h, y : y + 8, :] * now[r, h, y - 1 : y + 7, :]
                    wall = cz[r, h, y : y + 8, :] * ahead[h] + lz[r, h, y : y + 8, :] * behind[h]
                    a = a - (side + wall)
                    a = 0.5 * a if k == 1 else a - nxt[r, h, y : y + 8, :]
                    nxt[r, h, y : y + 8, :] = a
                    if inner and H <= r < H + BX:
                        out[k, r - H, h, y - PAD - H : y - PAD - H + 8, :] = a
                below, here, face = here, above, face_up
    return out


def place(ref, r, y, value):
    for h in range(2):
        ref[r, h, PAD + y : PAD + y + value.shape[0], :] = value[:, 128 * h : 128 * h + 128]


def prepare_kernel(
    keep, own, x_low, x_high, y_low, y_high, d, cx, cy, ly, cz, lz, top, out, shift, first, second
):
    lane = lax.broadcasted_iota(jnp.int32, (8, 128), 1)
    line = lax.broadcasted_iota(jnp.int32, (8, 128), 0)
    fields = (shift, cx, cy, cz, first)
    for b, block in enumerate((x_low, own, x_high)):

        def assemble(i, carry, b=b, block=block):
            for n, ref in enumerate(fields):
                r = b * BX + i
                place(ref, r, 0, y_low[n, r])
                place(ref, r, H, block[n, i])
                place(ref, r, H + BY, y_high[n, r])
            return carry

        lax.fori_loop(0, BX, assemble, 0)
    for i in range(BX):
        for h in range(2):
            out[0, i, h] = own[4, i, :, 128 * h : 128 * h + 128]

    tiles = [PAD + 8 * t for t in range(EY // 8)]

    def diagonal(r, most):
        for y in tiles:
            z = [cz[r, h, y : y + 8, :] for h in range(2)]
            behind = [turn(v, 1) for v in z]
            behind[1] = jnp.where(lane == 0, behind[0], behind[1])
            behind[0] = jnp.where(lane == 0, 0.0, behind[0])
            for h in range(2):
                lower = cy[r, h, y - 1 : y + 7, :]
                total = cx[r, h, y : y + 8, :] + cx[r - 1, h, y : y + 8, :]
                total = total + cy[r, h, y : y + 8, :] + lower + z[h] + behind[h]
                diag = shift[r, h, y : y + 8, :] + total
                d[r, h, y : y + 8, :] = diag
                ly[r, h, y : y + 8, :] = lower
                lz[r, h, y : y + 8, :] = behind[h]
                row_bound = diag + total
                if y == PAD:
                    row_bound = jnp.where(line > 0, row_bound, 0.0)
                most = jnp.maximum(most, row_bound)
        return most

    most = lax.fori_loop(1, EX, diagonal, jnp.zeros((8, 128), jnp.float32))
    bound = jnp.max(jnp.max(most, axis=0, keepdims=True), axis=1, keepdims=True)
    top[...] = jnp.broadcast_to(bound, top.shape)
    scale = jnp.broadcast_to(4.0 / bound, (8, 128))
    inside = scale * keep[1]

    def rescale(r, carry):
        scale_x = jnp.where(r == H + BX - 1, scale * keep[0], scale)
        for y in tiles:
            last = y - PAD + 8 == H + BY
            after = y - PAD == H + BY
            for h in range(2):
                at = (r, h, slice(y, y + 8), slice(None))
                d[at] = d[at] * scale - 2.0
                cx[at] = cx[at] * scale_x
                cy[at] = cy[at] * (jnp.where(line == 7, inside, scale) if last else scale)
                ly[at] = ly[at] * (jnp.where(line == 0, inside, scale) if after else scale)
                cz[at] = cz[at] * (scale if h == 0 else jnp.where(lane == 127, 0.0, scale))
                lz[at] = lz[at] * scale
        return carry

    lax.fori_loop(0, EX, rescale, 0)
    basis(first, second, d, cx, cy, ly, cz, lz, out)


def mirror_kernel(own, x_low, x_high, y_low, y_high, d, cx, cy, ly, cz, lz, out, first, second):
    for b, block in enumerate((x_low, own, x_high)):
        for i in range(BX):
            r = b * BX + i
            place(first, r, 0, y_low[b * BX + BX - 1 - i])
            place(first, r, H, block[BX - 1 - i])
            place(first, r, H + BY, y_high[b * BX + BX - 1 - i])
    for i in range(BX):
        for h in range(2):
            out[0, i, h] = own[BX - 1 - i, :, 128 * h : 128 * h + 128]
    basis(first, second, d, cx, cy, ly, cz, lz, out)


def pack_kernel(shift, cx, cy, cz, right_side, own, plane_x, plane_y, sems):
    copies = [pltpu.make_async_copy(a, own.at[n], sems.at[n]) for n, a in enumerate((shift, cx, cy, cz, right_side))]
    for copy in copies:
        copy.start()
    copies[1].wait()
    plane_x[...] = own[1, BX - 1]
    copies[2].wait()
    for i in range(BX):
        plane_y[i : i + 1, :] = own[2, i, BY - 1 : BY, :]
    for n in (0, 3, 4):
        copies[n].wait()


def edge_kernel(x_low, own, x_high, first_lines, last_lines):
    for b, block in enumerate((x_low, own, x_high)):
        rows = pl.ds(b * BX, BX)
        if len(block.shape) == 3:
            first_lines[rows] = block[:, :H, :]
            last_lines[rows] = block[:, BY - H :, :]
        else:
            for n in range(block.shape[0]):
                first_lines[n, rows] = block[n, :, :H, :]
                last_lines[n, rows] = block[n, :, BY - H :, :]


def bound_kernel(own, before_x, before_y, out):
    lane = lax.broadcasted_iota(jnp.int32, (BY, NZ), 1)
    line = lax.broadcasted_iota(jnp.int32, (BY, NZ), 0)
    most = jnp.zeros((BY, NZ), jnp.float32)
    for r in range(BX):
        x, y, z = own[1, r], own[2, r], own[3, r]
        low_x = before_x[...] if r == 0 else own[1, r - 1]
        low_y = jnp.where(line == 0, before_y[r : r + 1, :], pltpu.roll(y, 1, 0))
        low_z = jnp.where(lane == 0, 0.0, pltpu.roll(z, 1, 1))
        most = jnp.maximum(most, own[0, r] + 2.0 * (x + low_x + y + low_y + z + low_z))
    most = jnp.max(jnp.max(most, axis=0, keepdims=True), axis=1, keepdims=True)
    out[...] = jnp.broadcast_to(most[None], out.shape)


def spread_kernel(values, out):
    most = values[0]
    for i in range(1, values.shape[0]):
        most = jnp.maximum(most, values[i])
    out[...] = jnp.broadcast_to(most[None], out.shape)


def polynomials(low, high, bound, top):
    lmin = low * bound
    lmax = high * bound
    theta = (lmax + lmin) / 2.0
    delta = (lmax - lmin) / 2.0
    sigma = theta / delta
    rho = 1.0 / sigma
    half = 0.5 * top
    zero = jnp.zeros_like(bound)
    n = ITERS + 1
    x = [zero] * n
    r = [zero + 1.0] + [zero] * ITERS
    d = [r[0] / theta] + [zero] * ITERS
    for _ in range(ITERS):
        x = [a + b for a, b in zip(x, d)]
        at = d + [zero]
        moved = [0.5 * at[1], at[0] + 0.5 * at[2]] + [0.5 * (at[k - 1] + at[k + 1]) for k in range(2, n)]
        r = [a - half * (b + c) for a, b, c in zip(r, d, moved)]
        rho_new = 1.0 / (2.0 * sigma - rho)
        by, of = rho_new * rho, 2.0 * rho_new / delta
        d = [by * a + of * b for a, b in zip(d, r)]
        rho = rho_new
    return x, r


def combine_kernel(low, high, bounds, top, plain, mirrored, pressure, residual):
    bound = bounds[0]
    for i in range(1, bounds.shape[0]):
        bound = jnp.maximum(bound, bounds[i])
    bound = jnp.broadcast_to(bound, (8, 128))
    found = [polynomials(low[f], high[f], bound, top[...]) for f in range(2)]
    sums, gaps = [], []
    for part in range(2):
        sums.append([0.5 * (a + b) for a, b in zip(found[0][part], found[1][part])])
        gaps.append([0.5 * (a - b) for a, b in zip(found[0][part], found[1][part])])

    def row(r, carry):
        for i in range(0, BY, 8):
            for h in range(2):
                p = q = None
                for k in range(ITERS + 1):
                    a = plain[k, r, h, i : i + 8, :]
                    b = mirrored[k, r, h, i : i + 8, :]
                    if k < ITERS:
                        t = sums[0][k] * a + gaps[0][k] * b
                        p = t if p is None else p + t
                    t = sums[1][k] * a + gaps[1][k] * b
                    q = t if q is None else q + t
                pressure[r, i : i + 8, 128 * h : 128 * h + 128] = p
                residual[r, i : i + 8, 128 * h : 128 * h + 128] = q
        return carry

    lax.fori_loop(0, BX, row, 0)


def f32(*shape):
    return jax.ShapeDtypeStruct(shape, jnp.float32)


def kernel(body, out, operands, smem=0, scratch=(), mib=16, flops=1_000_000, where=VMEM):
    nbytes = sum(a.size * 4 for a in operands)
    return pl.pallas_call(
        body,
        out_shape=out,
        in_specs=[SMEM] * smem + [where] * (len(operands) - smem),
        out_specs=jax.tree.map(lambda _: VMEM, out),
        scratch_shapes=scratch,
        compiler_params=pltpu.CompilerParams(vmem_limit_bytes=mib << 20),
        cost_estimate=pl.CostEstimate(flops=flops, bytes_accessed=nbytes, transcendentals=0),
    )(*operands)


def shards(right_side, shift, coef_x, coef_y, coef_z, low_frac, high_frac):
    nx, ny = lax.axis_size(GX), lax.axis_size(GY)
    me_x, me_y = lax.axis_index(GX), lax.axis_index(GY)
    up_x, up_y = shift_pairs(nx)[0], shift_pairs(ny)[0]
    nz_chips, near = lax.axis_size("gx_0"), lax.axis_size(NEAR)

    own, plane_x, plane_y = kernel(
        pack_kernel,
        (f32(5, BX, BY, NZ), f32(BY, NZ), f32(BX, NZ)),
        (shift, coef_x, coef_y, coef_z, right_side),
        scratch=[pltpu.SemaphoreType.DMA((5,))],
        where=pl.BlockSpec(memory_space=pl.ANY),
        mib=56,
    )
    before_x = lax.ppermute(plane_x, GX, up_x)
    before_y = lax.ppermute(plane_y, GY, up_y)
    x_low, x_high = both_ways(own, own, GX)
    mirror = lax.ppermute(right_side, GX, [(i, nx - 1 - i) for i in range(nx)])

    most = kernel(bound_kernel, f32(near, 1, 128), (own, before_x, before_y), mib=4)
    most = lax.all_to_all(most, NEAR, 0, 0, tiled=True)
    most = kernel(spread_kernel, f32(nz_chips, 1, 128), (most,), mib=4)
    bounds = lax.all_to_all(most, "gx_0", 0, 0, tiled=True)

    edge = f32(5, EX, H, NZ)
    first_lines, last_lines = kernel(edge_kernel, (edge, edge), (x_low, own, x_high))
    y_low, y_high = both_ways(last_lines, first_lines, GY)
    keep = jnp.stack([me_x < nx - 1, me_y < ny - 1]).astype(jnp.float32)
    wide = f32(EX, 2, EY + 2 * PAD, 128)
    scratch = pltpu.VMEM(wide.shape, jnp.float32)
    basis_out = f32(ITERS + 1, BX, 2, BY, 128)
    *operator, top, plain = kernel(
        prepare_kernel,
        (wide,) * 6 + (f32(8, 128), basis_out),
        (keep, own, x_low, x_high, y_low, y_high),
        smem=1,
        scratch=[scratch] * 3,
        flops=30_000_000,
    )

    m_low, m_high = both_ways(mirror, mirror, GX)
    edge = f32(EX, H, NZ)
    first_lines, last_lines = kernel(edge_kernel, (edge, edge), (m_low, mirror, m_high), mib=8)
    n_low, n_high = both_ways(last_lines, first_lines, GY)
    mirrored = kernel(
        mirror_kernel,
        basis_out,
        (mirror, m_low, m_high, n_low, n_high, *operator),
        scratch=[scratch] * 2,
        flops=20_000_000,
    )
    return kernel(
        combine_kernel,
        (f32(BX, BY, NZ), f32(BX, BY, NZ)),
        (low_frac, high_frac, bounds, top, plain, mirrored),
        smem=2,
        mib=8,
        flops=3_000_000,
    )


def solution(mesh):
    torus = Mesh(mesh.devices.reshape(32, 2, 4, 2, 2), GX + GY)
    block = P(GX, GY, None)
    return jax.shard_map(
        shards,
        mesh=torus,
        in_specs=(block,) * 5 + (P(), P()),
        out_specs=(block, block),
        check_vma=False,
    )
```

time: 155 us -> 180 us (1.16)
  the two profiles are of different devices: /device:TPU:33 before, /device:TPU:1 now
where the time goes in v2:
time: 180 us; the launch traced here: 179 us
  starting transfers between devices  76.8 us (43%)
  waiting for transfers between devices  59.9 us (33%)
  Pallas kernels  18.8 us (10%)
  blocking collectives  18.2 us (10%)
  local copies, waits for them, and re-layouts  4.52 us (3%)
    ppermute x4, waiting for transfers between devices, both_ways(): lax.ppermute(array_up, axes, up)  24.4 us
    ppermute x4, starting transfers between devices, both_ways(): lax.ppermute(array_up, axes, up)  23.2 us
    ppermute x1, waiting for transfers between devices, shards(): mirror = lax.ppermute(right_side, GX, [(i, nx - 1 - i) for i in range(nx)])  22 us
    ppermute x1, starting transfers between devices, shards(): mirror = lax.ppermute(right_side, GX, [(i, nx - 1 - i) for i in range(nx)])  20.7 us
    all_to_all x1, starting transfers between devices, shards(): bounds = lax.all_to_all(most, 'gx_0', 0, 0, tiled=True)  19.7 us
    pallas_call x8, Pallas kernels, kernel(): pl.pallas_call(body, out_shape=out, in_specs=[SMEM] * smem + [where] * (l...  18.8 us
    all_to_all x1, blocking collectives, shards(): most = lax.all_to_all(most, NEAR, 0, 0, tiled=True)  18.2 us
    all_to_all x1, waiting for transfers between devices, shards(): bounds = lax.all_to_all(most, 'gx_0', 0, 0, tiled=True)  6.44 us
  transfers between devices with their start and end apart: 12, of which 7 were waited for; matrix products, arithmetic and copies ran while one was open for 0% of the time, Pallas kernels for 8%

profile of v2, /device:TPU:1, one launch (start us, length us, event | category | flops | bytes accessed | tf_op | source)
XLA Modules:
  0.0 179.1 jit_solution(4031114879136010445)
XLA Ops:
  0.6 0.0 copy-start.8
  0.6 2.1 %shard_map.86 = (f32[5,8,16,256]{3,2,1,0:T(8,128)}, f32[16,256]{1,0:T(8,128)}, f32[8,256]{1,0:T(8,128)}) custom-call(f32[8,16,256]{2,1,0:T(8,128)} %shift.1, f32[8,16,256]{2,1,0:T(8,128)} %cx.1, f32[8,16,256]{2,1,0:T(8,128)} %cy.1, f32[8,16,256]{2,1,0:T(8,128)} %cz.1, f32[8,16,256]{2,1,0:T(8,128)} %right_side.1), custom_call_target="tpu_custom_call" | custom-call | flops 1000000 | bytes 655360 | tf_op jit(solution)/shard_map/pallas_call | solution.py:265
  2.7 5.5 %collective-permute-start.2 = (f32[5,8,16,256]{3,2,1,0:T(8,128)}, f32[5,8,16,256]{3,2,1,0:T(8,128)S(1)}, u32[]{:S(2)}, u32[]{:S(2)}) collective-permute-start(f32[5,8,16,256]{3,2,1,0:T(8,128)} %get-tuple-element.17.own), channel_id=1, source_target_pairs={{0,16},{16,32},{32,48},{48,64},{64,80},{80,96},{96,112},{112,128},... | collective-permute-start | bytes 1966088 | tf_op jit(solution)/shard_map/ppermute | solution.py:29
  8.2 1.3 collective-permute-start.3
  9.5 23.1 %collective-permute-done.2.x_low = f32[5,8,16,256]{3,2,1,0:T(8,128)S(1)} collective-permute-done((f32[5,8,16,256]{3,2,1,0:T(8,128)}, f32[5,8,16,256]{3,2,1,0:T(8,128)S(1)}, u32[]{:S(2)}, u32[]{:S(2)}) %collective-permute-start.2) | collective-permute-done | bytes 655392 | tf_op jit(solution)/shard_map/ppermute | solution.py:29
  32.6 0.0 collective-permute-done.3.x_high
  32.6 0.0 copy-start
  32.6 1.1 copy-done
  33.7 0.0 copy-start.10
  33.7 0.0 copy-start.9
  33.7 0.0 copy-start.1
  33.7 1.4 shard_map.89
  35.1 7.0 %collective-permute-start.4 = (f32[5,24,8,256]{3,2,1,0:T(8,128)}, f32[5,24,8,256]{3,2,1,0:T(8,128)S(1)}, u32[]{:S(2)}, u32[]{:S(2)}) collective-permute-start(f32[5,24,8,256]{3,2,1,0:T(8,128)} %get-tuple-element.20), channel_id=1, source_target_pairs={{0,1},{1,2},{2,3},{3,4},{4,5},{5,6},{6,7},{7,8},{8,9},{9,10},{10,1... | collective-permute-start | bytes 2949128 | tf_op jit(solution)/shard_map/ppermute | solution.py:29
  42.1 1.9 %collective-permute-start.5 = (f32[5,24,8,256]{3,2,1,0:T(8,128)}, f32[5,24,8,256]{3,2,1,0:T(8,128)}, u32[]{:S(2)}, u32[]{:S(2)}) collective-permute-start(f32[5,24,8,256]{3,2,1,0:T(8,128)} %get-tuple-element.21), channel_id=1, source_target_pairs={{1,0},{2,1},{3,2},{4,3},{5,4},{6,5},{7,6},{8,7},{9,8},{10,9},{11,1... | collective-permute-start | bytes 2949128 | tf_op jit(solution)/shard_map/ppermute | solution.py:29
  44.0 0.0 copy-done.8
  44.0 20.7 %collective-permute-start.6 = (f32[8,16,256]{2,1,0:T(8,128)S(1)}, f32[8,16,256]{2,1,0:T(8,128)S(1)}, u32[]{:S(2)}, u32[]{:S(2)}) collective-permute-start(f32[8,16,256]{2,1,0:T(8,128)S(1)} %copy-done.8), channel_id=1, source_target_pairs={{0,1008},{16,992},{32,976},{48,960},{64,944},{80,928},{96,912},{11... | collective-permute-start | bytes 393224 | tf_op jit(solution)/shard_map/ppermute | solution.py:293
  64.8 22.0 %collective-permute-done.6.own = f32[8,16,256]{2,1,0:T(8,128)S(1)} collective-permute-done((f32[8,16,256]{2,1,0:T(8,128)S(1)}, f32[8,16,256]{2,1,0:T(8,128)S(1)}, u32[]{:S(2)}, u32[]{:S(2)}) %collective-permute-start.6) | collective-permute-done | bytes 131104 | tf_op jit(solution)/shard_map/ppermute | solution.py:293
  86.8 4.8 %collective-permute-start.7 = (f32[8,16,256]{2,1,0:T(8,128)S(1)}, f32[8,16,256]{2,1,0:T(8,128)S(1)}, u32[]{:S(2)}, u32[]{:S(2)}) collective-permute-start(f32[8,16,256]{2,1,0:T(8,128)S(1)} %collective-permute-done.6.own), channel_id=1, source_target_pairs={{0,16},{16,32},{32,48},{48,64},{64,80},{80,96},{96,112},{112,128},... | collective-permute-start | bytes 393224 | tf_op jit(solution)/shard_map/ppermute | solution.py:29
  91.6 1.3 collective-permute-start.8
  92.9 1.4 collective-permute-done.7.x_low
  94.3 5.3 %collective-permute-done.8.x_high = f32[8,16,256]{2,1,0:T(8,128)S(1)} collective-permute-done((f32[8,16,256]{2,1,0:T(8,128)S(1)}, f32[8,16,256]{2,1,0:T(8,128)S(1)}, u32[]{:S(2)}, u32[]{:S(2)}) %collective-permute-start.8) | collective-permute-done | bytes 131104 | tf_op jit(solution)/shard_map/ppermute | solution.py:29
  99.6 0.8 shard_map.91
  100.4 5.8 %collective-permute-start.9 = (f32[24,8,256]{2,1,0:T(8,128)}, f32[24,8,256]{2,1,0:T(8,128)}, u32[]{:S(2)}, u32[]{:S(2)}) collective-permute-start(f32[24,8,256]{2,1,0:T(8,128)} %get-tuple-element.24), channel_id=1, source_target_pairs={{0,1},{1,2},{2,3},{3,4},{4,5},{5,6},{6,7},{7,8},{8,9},{9,10},{10,1... | collective-permute-start | bytes 589832 | tf_op jit(solution)/shard_map/ppermute | solution.py:29
  106.2 1.9 %collective-permute-start.10 = (f32[24,8,256]{2,1,0:T(8,128)}, f32[24,8,256]{2,1,0:T(8,128)}, u32[]{:S(2)}, u32[]{:S(2)}) collective-permute-start(f32[24,8,256]{2,1,0:T(8,128)} %get-tuple-element.25), channel_id=1, source_target_pairs={{1,0},{2,1},{3,2},{4,3},{5,4},{6,5},{7,6},{8,7},{9,8},{10,9},{11,1... | collective-permute-start | bytes 589832 | tf_op jit(solution)/shard_map/ppermute | solution.py:29
  108.2 0.0 copy-done.10
  108.2 3.6 %collective-permute-start.1 = (f32[8,256]{1,0:T(8,128)S(1)}, f32[8,256]{1,0:T(8,128)S(1)}, u32[]{:S(2)}, u32[]{:S(2)}) collective-permute-start(f32[8,256]{1,0:T(8,128)S(1)} %copy-done.10), channel_id=1, source_target_pairs={{0,1},{1,2},{2,3},{3,4},{4,5},{5,6},{6,7},{7,8},{8,9},{9,10},{10,1... | collective-permute-start | bytes 24584 | tf_op jit(solution)/shard_map/ppermute | solution.py:291
  111.8 0.8 collective-permute-done.1.before_y
  112.6 0.0 copy-done.9
  112.6 3.2 %collective-permute-start = (f32[16,256]{1,0:T(8,128)S(1)}, f32[16,256]{1,0:T(8,128)S(1)}, u32[]{:S(2)}, u32[]{:S(2)}) collective-permute-start(f32[16,256]{1,0:T(8,128)S(1)} %copy-done.9), channel_id=1, source_target_pairs={{0,16},{16,32},{32,48},{48,64},{64,80},{80,96},{96,112},{112,128},... | collective-permute-start | bytes 49160 | tf_op jit(solution)/shard_map/ppermute | solution.py:290
  115.8 0.9 collective-permute-done.before_x
  116.6 0.2 shard_map.87
  116.8 18.2 %all_to_all.10.values = f32[32,1,128]{2,1,0:T(1,128)S(1)} all-to-all(f32[32,1,128]{2,1,0:T(1,128)S(1)} %shard_map.87), channel_id=1, replica_groups=mesh['gx_0'=32,'gx_1'=2,'gy_0'=4,'gy_1'=2,'gy_2'=2] {'gx_1','gy_0','gy_1..., dimensions={0} | all-to-all | bytes 32768 | tf_op jit(solution)/shard_map/all_to_all | solution.py:296
  135.0 0.6 shard_map.88
  135.6 19.7 %all-to-all-start.1 = ((f32[32,1,128]{2,1,0:T(1,128)}), f32[32,1,128]{2,1,0:T(1,128)S(1)}, u32[]{:S(2)}, u32[]{:S(2)}) async-start(f32[32,1,128]{2,1,0:T(1,128)} %shard_map.88), calls=%async_computation.1 | async-start | bytes 32768 | tf_op jit(solution)/shard_map/all_to_all | solution.py:298
  155.4 0.1 add_convert_fusion.keep
  155.4 0.0 collective-permute-done.4.y_low
  155.4 0.0 copy-start.2
  155.4 0.9 copy-done.2
  156.4 0.0 collective-permute-done.5.y_high
  156.4 0.0 copy-done.1
  156.4 0.0 copy-start.3
  156.4 1.2 copy-done.3
  157.6 7.4 %shard_map.90 = (f32[24,2,48,128]{3,2,1,0:T(8,128)S(1)}, f32[24,2,48,128]{3,2,1,0:T(8,128)S(1)}, f32[24,2,48,128]{3,2,1,0:T(8,128)S(1)}, f32[24,2,48,128]{3,2,1,...) custom-call(f32[2]{0:T(128)S(1)} %add_convert_fusion.keep, ...), custom_call_target="tpu_custom_call" | custom-call | flops 30000000 | bytes 3932168 | tf_op jit(solution)/shard_map/pallas_call | solution.py:265
  165.0 0.0 copy-start.4
  165.0 0.0 collective-permute-done.9.y_low
  165.0 0.0 collective-permute-done.10.y_high
  165.1 0.6 copy-done.4
  165.6 0.0 copy-start.6
  165.6 0.0 copy-start.7
  165.6 4.5 %shard_map.92.mirrored = f32[9,8,2,16,128]{4,3,2,1,0:T(8,128)S(1)} custom-call(f32[8,16,256]{2,1,0:T(8,128)S(1)} %collective-permute-done.6.own, f32[8,16,256]{2,1,0:T(8,128)S(1)} %collective-permute-done.7.x_low, f32[8,16,256]{2,1,0:T(8,128)S(1)} %collective-permute-done.8.x_high, f32[24,8,256]{2,1,0:T(8,128)} %collective-permute-done.9.y_low, ...), custom_call_target="tpu_custom_call" | custom-call | flops 20000000 | bytes 7864320 | tf_op jit(solution)/shard_map/pallas_call | solution.py:265
  170.1 6.4 %all-to-all-done.1.bounds = f32[32,1,128]{2,1,0:T(1,128)S(1)} async-done(((f32[32,1,128]{2,1,0:T(1,128)}), f32[32,1,128]{2,1,0:T(1,128)S(1)}, u32[]{:S(2)}, u32[]{:S(2)}) %all-to-all-start.1) | async-done | bytes 16416 | tf_op jit(solution)/shard_map/all_to_all | solution.py:298
  176.5 0.0 copy-done.6
  176.5 0.0 copy-done.7
  176.5 0.0 copy-start.5
  176.5 0.7 copy-done.5
  177.2 1.9 %shard_map.93 = (f32[8,16,256]{2,1,0:T(8,128)}, f32[8,16,256]{2,1,0:T(8,128)}) custom-call(f32[2]{0:T(128)S(1)} %copy-done.6, f32[2]{0:T(128)S(1)} %copy-done.7, f32[32,1,128]{2,1,0:T(1,128)S(1)} %all-to-all-done.1.bounds, f32[8,128]{1,0:T(8,128)S(1)} %copy-done.5, f32[9,8,2,16,128]{4,3,2,1,0:T(8,128)S(1)} %get-tuple-element.23.plain, ...), custom_call_target="tpu_custom_call" | custom-call | flops 3000000 | bytes 2379792 | tf_op jit(solution)/shard_map/pallas_call | solution.py:265
Async XLA Ops:
  0.6 43.4 %copy-start.8 = (f32[8,16,256]{2,1,0:T(8,128)S(1)}, f32[8,16,256]{2,1,0:T(8,128)}, u32[]{:S(2)}) copy-start(f32[8,16,256]{2,1,0:T(8,128)} %right_side.1) | copy-start | bytes 393220
  2.7 29.9 %collective-permute-start.2 = (f32[5,8,16,256]{3,2,1,0:T(8,128)}, f32[5,8,16,256]{3,2,1,0:T(8,128)S(1)}, u32[]{:S(2)}, u32[]{:S(2)}) collective-permute-start(f32[5,8,16,256]{3,2,1,0:T(8,128)} %get-tuple-element.17.own), channel_id=1, source_target_pairs={{0,16},{16,32},{32,48},{48,64},{64,80},{80,96},{96,112},{112,128},... | collective-permute-start | bytes 1966088 | tf_op jit(solution)/shard_map/ppermute | solution.py:29
  8.2 24.4 %collective-permute-start.3 = (f32[5,8,16,256]{3,2,1,0:T(8,128)}, f32[5,8,16,256]{3,2,1,0:T(8,128)S(1)}, u32[]{:S(2)}, u32[]{:S(2)}) collective-permute-start(f32[5,8,16,256]{3,2,1,0:T(8,128)} %get-tuple-element.17.own), channel_id=1, source_target_pairs={{16,0},{32,16},{48,32},{64,48},{80,64},{96,80},{112,96},{128,112},... | collective-permute-start | bytes 1966088 | tf_op jit(solution)/shard_map/ppermute | solution.py:29
  32.6 1.1 copy-start
  33.7 74.5 %copy-start.10 = (f32[8,256]{1,0:T(8,128)S(1)}, f32[8,256]{1,0:T(8,128)}, u32[]{:S(2)}) copy-start(f32[8,256]{1,0:T(8,128)} %get-tuple-element.19) | copy-start | bytes 24580
  33.7 78.9 %copy-start.9 = (f32[16,256]{1,0:T(8,128)S(1)}, f32[16,256]{1,0:T(8,128)}, u32[]{:S(2)}) copy-start(f32[16,256]{1,0:T(8,128)} %get-tuple-element.18) | copy-start | bytes 49156
  33.7 122.7 %copy-start.1 = (f32[5,8,16,256]{3,2,1,0:T(8,128)S(1)}, f32[5,8,16,256]{3,2,1,0:T(8,128)}, u32[]{:S(2)}) copy-start(f32[5,8,16,256]{3,2,1,0:T(8,128)} %get-tuple-element.17.own) | copy-start | bytes 1966084
  35.1 120.4 %collective-permute-start.4 = (f32[5,24,8,256]{3,2,1,0:T(8,128)}, f32[5,24,8,256]{3,2,1,0:T(8,128)S(1)}, u32[]{:S(2)}, u32[]{:S(2)}) collective-permute-start(f32[5,24,8,256]{3,2,1,0:T(8,128)} %get-tuple-element.20), channel_id=1, source_target_pairs={{0,1},{1,2},{2,3},{3,4},{4,5},{5,6},{6,7},{7,8},{8,9},{9,10},{10,1... | collective-permute-start | bytes 2949128 | tf_op jit(solution)/shard_map/ppermute | solution.py:29
  42.1 114.3 %collective-permute-start.5 = (f32[5,24,8,256]{3,2,1,0:T(8,128)}, f32[5,24,8,256]{3,2,1,0:T(8,128)}, u32[]{:S(2)}, u32[]{:S(2)}) collective-permute-start(f32[5,24,8,256]{3,2,1,0:T(8,128)} %get-tuple-element.21), channel_id=1, source_target_pairs={{1,0},{2,1},{3,2},{4,3},{5,4},{6,5},{7,6},{8,7},{9,8},{10,9},{11,1... | collective-permute-start | bytes 2949128 | tf_op jit(solution)/shard_map/ppermute | solution.py:29
  44.0 42.8 %collective-permute-start.6 = (f32[8,16,256]{2,1,0:T(8,128)S(1)}, f32[8,16,256]{2,1,0:T(8,128)S(1)}, u32[]{:S(2)}, u32[]{:S(2)}) collective-permute-start(f32[8,16,256]{2,1,0:T(8,128)S(1)} %copy-done.8), channel_id=1, source_target_pairs={{0,1008},{16,992},{32,976},{48,960},{64,944},{80,928},{96,912},{11... | collective-permute-start | bytes 393224 | tf_op jit(solution)/shard_map/ppermute | solution.py:293
  86.8 7.5 %collective-permute-start.7 = (f32[8,16,256]{2,1,0:T(8,128)S(1)}, f32[8,16,256]{2,1,0:T(8,128)S(1)}, u32[]{:S(2)}, u32[]{:S(2)}) collective-permute-start(f32[8,16,256]{2,1,0:T(8,128)S(1)} %collective-permute-done.6.own), channel_id=1, source_target_pairs={{0,16},{16,32},{32,48},{48,64},{64,80},{80,96},{96,112},{112,128},... | collective-permute-start | bytes 393224 | tf_op jit(solution)/shard_map/ppermute | solution.py:29
  91.6 8.0 %collective-permute-start.8 = (f32[8,16,256]{2,1,0:T(8,128)S(1)}, f32[8,16,256]{2,1,0:T(8,128)S(1)}, u32[]{:S(2)}, u32[]{:S(2)}) collective-permute-start(f32[8,16,256]{2,1,0:T(8,128)S(1)} %collective-permute-done.6.own), channel_id=1, source_target_pairs={{16,0},{32,16},{48,32},{64,48},{80,64},{96,80},{112,96},{128,112},... | collective-permute-start | bytes 393224 | tf_op jit(solution)/shard_map/ppermute | solution.py:29
  100.4 64.6 %collective-permute-start.9 = (f32[24,8,256]{2,1,0:T(8,128)}, f32[24,8,256]{2,1,0:T(8,128)}, u32[]{:S(2)}, u32[]{:S(2)}) collective-permute-start(f32[24,8,256]{2,1,0:T(8,128)} %get-tuple-element.24), channel_id=1, source_target_pairs={{0,1},{1,2},{2,3},{3,4},{4,5},{5,6},{6,7},{7,8},{8,9},{9,10},{10,1... | collective-permute-start | bytes 589832 | tf_op jit(solution)/shard_map/ppermute | solution.py:29
  106.2 58.8 %collective-permute-start.10 = (f32[24,8,256]{2,1,0:T(8,128)}, f32[24,8,256]{2,1,0:T(8,128)}, u32[]{:S(2)}, u32[]{:S(2)}) collective-permute-start(f32[24,8,256]{2,1,0:T(8,128)} %get-tuple-element.25), channel_id=1, source_target_pairs={{1,0},{2,1},{3,2},{4,3},{5,4},{6,5},{7,6},{8,7},{9,8},{10,9},{11,1... | collective-permute-start | bytes 589832 | tf_op jit(solution)/shard_map/ppermute | solution.py:29
  108.2 4.4 %collective-permute-start.1 = (f32[8,256]{1,0:T(8,128)S(1)}, f32[8,256]{1,0:T(8,128)S(1)}, u32[]{:S(2)}, u32[]{:S(2)}) collective-permute-start(f32[8,256]{1,0:T(8,128)S(1)} %copy-done.10), channel_id=1, source_target_pairs={{0,1},{1,2},{2,3},{3,4},{4,5},{5,6},{6,7},{7,8},{8,9},{9,10},{10,1... | collective-permute-start | bytes 24584 | tf_op jit(solution)/shard_map/ppermute | solution.py:291
  112.6 4.0 %collective-permute-start = (f32[16,256]{1,0:T(8,128)S(1)}, f32[16,256]{1,0:T(8,128)S(1)}, u32[]{:S(2)}, u32[]{:S(2)}) collective-permute-start(f32[16,256]{1,0:T(8,128)S(1)} %copy-done.9), channel_id=1, source_target_pairs={{0,16},{16,32},{32,48},{48,64},{64,80},{80,96},{96,112},{112,128},... | collective-permute-start | bytes 49160 | tf_op jit(solution)/shard_map/ppermute | solution.py:290
  135.6 40.9 %all-to-all-start.1 = ((f32[32,1,128]{2,1,0:T(1,128)}), f32[32,1,128]{2,1,0:T(1,128)S(1)}, u32[]{:S(2)}, u32[]{:S(2)}) async-start(f32[32,1,128]{2,1,0:T(1,128)} %shard_map.88), calls=%async_computation.1 | async-start | bytes 32768 | tf_op jit(solution)/shard_map/all_to_all | solution.py:298
  155.4 1.0 copy-start.2
  156.4 1.2 copy-start.3
  165.0 0.6 copy-start.4
  165.6 10.9 %copy-start.6 = (f32[2]{0:T(128)S(1)}, f32[2]{0:T(128)}, u32[]{:S(2)}) copy-start(f32[2]{0:T(128)} %low.1) | copy-start | bytes 28
  165.6 10.9 %copy-start.7 = (f32[2]{0:T(128)S(1)}, f32[2]{0:T(128)}, u32[]{:S(2)}) copy-start(f32[2]{0:T(128)} %high.1) | copy-start | bytes 28
  176.5 0.7 copy-start.5

commit v3 on v2

--- a/solution.py
+++ b/solution.py
@@ -17,6 +17,9 @@
 NEAR = ("gx_1",) + GY
 VMEM = pl.BlockSpec(memory_space=pltpu.VMEM)
 SMEM = pl.BlockSpec(memory_space=pltpu.SMEM)
+STRIDES = (16, 8, 4, 2, 1)
+SHARED = ((7, 1, 1), (6, 2, 2), (5, 3, 3), (16, 22, 1), (17, 21, 2), (18, 20, 3), (4, 19, 4))
+EDGE = BX + len(SHARED)
 
 
 def shift_pairs(n):
@@ -74,30 +77,40 @@
         ref[r, h, PAD + y : PAD + y + value.shape[0], :] = value[:, 128 * h : 128 * h + 128]
 
 
+def place_sides(ref, low, high):
+    for i in range(BX):
+        place(ref, H + i, 0, low[i])
+        place(ref, H + i, H + BY, high[i])
+    for t, (a, b, n) in enumerate(SHARED, BX):
+        for r, by in ((a, 0), (b, n)):
+            at_low, at_high = low[t], high[t]
+            if by:
+                at_low, at_high = pltpu.roll(at_low, 8 - by, 0), pltpu.roll(at_high, by, 0)
+            for row in {1: (0, 1), 22: (22, 23)}.get(r, (r,)):
+                place(ref, row, 0, at_low)
+                place(ref, row, H + BY, at_high)
+
+
 def prepare_kernel(
-    keep, own, x_low, x_high, y_low, y_high, d, cx, cy, ly, cz, lz, top, out, shift, first, second
+    keep, s_own, x_own, y_own, z_own, b_own, x_low, x_high, y_low, y_high, d, cx, cy, ly, cz, lz, top, out, shift, first, second
 ):
     lane = lax.broadcasted_iota(jnp.int32, (8, 128), 1)
     line = lax.broadcasted_iota(jnp.int32, (8, 128), 0)
-    fields = (shift, cx, cy, cz, first)
-    for b, block in enumerate((x_low, own, x_high)):
-
-        def assemble(i, carry, b=b, block=block):
-            for n, ref in enumerate(fields):
-                r = b * BX + i
-                place(ref, r, 0, y_low[n, r])
-                place(ref, r, H, block[n, i])
-                place(ref, r, H + BY, y_high[n, r])
-            return carry
-
-        lax.fori_loop(0, BX, assemble, 0)
+    fields = ((shift, s_own), (cx, x_own), (cy, y_own), (cz, z_own), (first, b_own))
+    for n, (ref, own) in enumerate(fields):
+        for i in range(BX):
+            place(ref, i, H, x_low[n, i])
+            place(ref, H + i, H, own[i])
+            place(ref, H + BX + i, H, x_high[n, i])
+        place_sides(ref, y_low.at[n], y_high.at[n])
     for i in range(BX):
         for h in range(2):
-            out[0, i, h] = own[4, i, :, 128 * h : 128 * h + 128]
+            out[0, i, h] = b_own[i, :, 128 * h : 128 * h + 128]
 
     tiles = [PAD + 8 * t for t in range(EY // 8)]
 
     def diagonal(r, most):
+        away = jnp.maximum(jnp.maximum(H - r, r - (H + BX - 1)), 0)
         for y in tiles:
             z = [cz[r, h, y : y + 8, :] for h in range(2)]
             behind = [turn(v, 1) for v in z]
@@ -112,12 +125,14 @@
                 ly[r, h, y : y + 8, :] = lower
                 lz[r, h, y : y + 8, :] = behind[h]
                 row_bound = diag + total
-                if y == PAD:
-                    row_bound = jnp.where(line > 0, row_bound, 0.0)
+                if y == tiles[0]:
+                    row_bound = jnp.where(line > away, row_bound, 0.0)
+                if y == tiles[-1]:
+                    row_bound = jnp.where(line < 7 - away, row_bound, 0.0)
                 most = jnp.maximum(most, row_bound)
         return most
 
-    most = lax.fori_loop(1, EX, diagonal, jnp.zeros((8, 128), jnp.float32))
+    most = lax.fori_loop(1, EX - 1, diagonal, jnp.zeros((8, 128), jnp.float32))
     bound = jnp.max(jnp.max(most, axis=0, keepdims=True), axis=1, keepdims=True)
     top[...] = jnp.broadcast_to(bound, top.shape)
     scale = jnp.broadcast_to(4.0 / bound, (8, 128))
@@ -145,10 +160,8 @@
 def mirror_kernel(own, x_low, x_high, y_low, y_high, d, cx, cy, ly, cz, lz, out, first, second):
     for b, block in enumerate((x_low, own, x_high)):
         for i in range(BX):
-            r = b * BX + i
-            place(first, r, 0, y_low[b * BX + BX - 1 - i])
-            place(first, r, H, block[BX - 1 - i])
-            place(first, r, H + BY, y_high[b * BX + BX - 1 - i])
+            place(first, b * BX + i, H, block[BX - 1 - i])
+    place_sides(first, y_low, y_high)
     for i in range(BX):
         for h in range(2):
             out[0, i, h] = own[BX - 1 - i, :, 128 * h : 128 * h + 128]
@@ -168,28 +181,40 @@
         copies[n].wait()
 
 
-def edge_kernel(x_low, own, x_high, first_lines, last_lines):
-    for b, block in enumerate((x_low, own, x_high)):
-        rows = pl.ds(b * BX, BX)
-        if len(block.shape) == 3:
-            first_lines[rows] = block[:, :H, :]
-            last_lines[rows] = block[:, BY - H :, :]
-        else:
-            for n in range(block.shape[0]):
-                first_lines[n, rows] = block[n, :, :H, :]
-                last_lines[n, rows] = block[n, :, BY - H :, :]
-
-
-def bound_kernel(own, before_x, before_y, out):
+def edges(row, first_lines, last_lines):
+    line = lax.broadcasted_iota(jnp.int32, (H, NZ), 0)
+    for i in range(BX):
+        first_lines[i] = row(H + i, 0)
+        last_lines[i] = row(H + i, BY - H)
+    for t, (a, b, n) in enumerate(SHARED, BX):
+        last_lines[t] = jnp.where(line >= n, row(a, BY - H), pltpu.roll(row(b, BY - H), n, 0))
+        first_lines[t] = jnp.where(line < H - n, row(a, 0), pltpu.roll(row(b, 0), H - n, 0))
+
+
+def edge_kernel(s_own, x_own, y_own, z_own, b_own, x_low, x_high, first_lines, last_lines):
+    for n, own in enumerate((s_own, x_own, y_own, z_own, b_own)):
+
+        def row(r, y, n=n, own=own):
+            block = (x_low.at[n], own, x_high.at[n])[r // BX]
+            return block[r % BX, y : y + H, :]
+
+        edges(row, first_lines.at[n], last_lines.at[n])
+
+
+def mirror_edge_kernel(own, x_low, x_high, first_lines, last_lines):
+    edges(lambda r, y: (x_low, own, x_high)[r // BX][BX - 1 - r % BX, y : y + H, :], first_lines, last_lines)
+
+
+def bound_kernel(shift, cx, cy, cz, before_x, before_y, out):
     lane = lax.broadcasted_iota(jnp.int32, (BY, NZ), 1)
     line = lax.broadcasted_iota(jnp.int32, (BY, NZ), 0)
     most = jnp.zeros((BY, NZ), jnp.float32)
     for r in range(BX):
-        x, y, z = own[1, r], own[2, r], own[3, r]
-        low_x = before_x[...] if r == 0 else own[1, r - 1]
+        x, y, z = cx[r], cy[r], cz[r]
+        low_x = before_x[...] if r == 0 else cx[r - 1]
         low_y = jnp.where(line == 0, before_y[r : r + 1, :], pltpu.roll(y, 1, 0))
         low_z = jnp.where(lane == 0, 0.0, pltpu.roll(z, 1, 1))
-        most = jnp.maximum(most, own[0, r] + 2.0 * (x + low_x + y + low_y + z + low_z))
+        most = jnp.maximum(most, shift[r] + 2.0 * (x + low_x + y + low_y + z + low_z))
     most = jnp.max(jnp.max(most, axis=0, keepdims=True), axis=1, keepdims=True)
     out[...] = jnp.broadcast_to(most[None], out.shape)
 
@@ -198,7 +223,7 @@
     most = values[0]
     for i in range(1, values.shape[0]):
         most = jnp.maximum(most, values[i])
-    out[...] = jnp.broadcast_to(most[None], out.shape)
+    out[...] = jnp.broadcast_to(most, out.shape)
 
 
 def polynomials(low, high, bound, top):
@@ -226,11 +251,8 @@
     return x, r
 
 
-def combine_kernel(low, high, bounds, top, plain, mirrored, pressure, residual):
-    bound = bounds[0]
-    for i in range(1, bounds.shape[0]):
-        bound = jnp.maximum(bound, bounds[i])
-    bound = jnp.broadcast_to(bound, (8, 128))
+def combine_kernel(low, high, bound, other_bound, top, plain, mirrored, pressure, residual):
+    bound = jnp.maximum(bound[...], other_bound[...])
     found = [polynomials(low[f], high[f], bound, top[...]) for f in range(2)]
     sums, gaps = [], []
     for part in range(2):
@@ -277,28 +299,32 @@
     nx, ny = lax.axis_size(GX), lax.axis_size(GY)
     me_x, me_y = lax.axis_index(GX), lax.axis_index(GY)
     up_x, up_y = shift_pairs(nx)[0], shift_pairs(ny)[0]
-    nz_chips, near = lax.axis_size("gx_0"), lax.axis_size(NEAR)
-
+    near = lax.axis_size(NEAR)
+    given = (shift, coef_x, coef_y, coef_z, right_side)
+
+    mirror = lax.ppermute(right_side, GX, [(i, nx - 1 - i) for i in range(nx)])
     own, plane_x, plane_y = kernel(
         pack_kernel,
         (f32(5, BX, BY, NZ), f32(BY, NZ), f32(BX, NZ)),
-        (shift, coef_x, coef_y, coef_z, right_side),
+        given,
         scratch=[pltpu.SemaphoreType.DMA((5,))],
         where=pl.BlockSpec(memory_space=pl.ANY),
         mib=56,
     )
+    x_low, x_high = both_ways(own, own, GX)
     before_x = lax.ppermute(plane_x, GX, up_x)
     before_y = lax.ppermute(plane_y, GY, up_y)
-    x_low, x_high = both_ways(own, own, GX)
-    mirror = lax.ppermute(right_side, GX, [(i, nx - 1 - i) for i in range(nx)])
-
-    most = kernel(bound_kernel, f32(near, 1, 128), (own, before_x, before_y), mib=4)
+
+    most = kernel(bound_kernel, f32(near, 1, 128), (*given[:4], before_x, before_y), mib=2)
     most = lax.all_to_all(most, NEAR, 0, 0, tiled=True)
-    most = kernel(spread_kernel, f32(nz_chips, 1, 128), (most,), mib=4)
-    bounds = lax.all_to_all(most, "gx_0", 0, 0, tiled=True)
-
-    edge = f32(5, EX, H, NZ)
-    first_lines, last_lines = kernel(edge_kernel, (edge, edge), (x_low, own, x_high))
+    most = kernel(spread_kernel, f32(8, 128), (most,), mib=2)
+    other = most
+    for stride in STRIDES:
+        most = jnp.maximum(most, other)
+        other = lax.ppermute(most, "gx_0", [(i, i ^ stride) for i in range(lax.axis_size("gx_0"))])
+
+    edge = f32(5, EDGE, H, NZ)
+    first_lines, last_lines = kernel(edge_kernel, (edge, edge), (*given, x_low, x_high), mib=2)
     y_low, y_high = both_ways(last_lines, first_lines, GY)
     keep = jnp.stack([me_x < nx - 1, me_y < ny - 1]).astype(jnp.float32)
     wide = f32(EX, 2, EY + 2 * PAD, 128)
@@ -307,15 +333,16 @@
     *operator, top, plain = kernel(
         prepare_kernel,
         (wide,) * 6 + (f32(8, 128), basis_out),
-        (keep, own, x_low, x_high, y_low, y_high),
+        (keep, *given, x_low, x_high, y_low, y_high),
         smem=1,
         scratch=[scratch] * 3,
         flops=30_000_000,
+        mib=6,
     )
 
     m_low, m_high = both_ways(mirror, mirror, GX)
-    edge = f32(EX, H, NZ)
-    first_lines, last_lines = kernel(edge_kernel, (edge, edge), (m_low, mirror, m_high), mib=8)
+    edge = f32(EDGE, H, NZ)
+    first_lines, last_lines = kernel(mirror_edge_kernel, (edge, edge), (mirror, m_low, m_high), mib=2)
     n_low, n_high = both_ways(last_lines, first_lines, GY)
     mirrored = kernel(
         mirror_kernel,
@@ -323,13 +350,14 @@
         (mirror, m_low, m_high, n_low, n_high, *operator),
         scratch=[scratch] * 2,
         flops=20_000_000,
+        mib=4,
     )
     return kernel(
         combine_kernel,
         (f32(BX, BY, NZ), f32(BX, BY, NZ)),
-        (low_frac, high_frac, bounds, top, plain, mirrored),
+        (low_frac, high_frac, most, other, top, plain, mirrored),
         smem=2,
-        mib=8,
+        mib=2,
         flops=3_000_000,
     )
 

time: 180 us -> 198 us (1.10)
  the two profiles are of different devices: /device:TPU:1 before, /device:TPU:8 now
where the time goes in v3:
time: 198 us
  starting transfers between devices  95.2 us (48%)
  waiting for transfers between devices  65.2 us (33%)
  Pallas kernels  16.7 us (8%)
  blocking collectives  14.4 us (7%)
  local copies, waits for them, and re-layouts  5.23 us (3%)
    ppermute x5, starting transfers between devices, shards(): lax.ppermute(most, 'gx_0', [(i, i ^ stride) for i in range(lax.axis_size(...  42.2 us
    ppermute x4, waiting for transfers between devices, both_ways(): lax.ppermute(array_up, axes, up)  27 us
    ppermute x1, waiting for transfers between devices, shards(): mirror = lax.ppermute(right_side, GX, [(i, nx - 1 - i) for i in range(nx)])  22.9 us
    ppermute x1, starting transfers between devices, shards(): mirror = lax.ppermute(right_side, GX, [(i, nx - 1 - i) for i in range(nx)])  19.5 us
    pallas_call x8, Pallas kernels, kernel(): pl.pallas_call(body, out_shape=out, in_specs=[SMEM] * smem + [where] * (l...  16.7 us
    all_to_all x1, blocking collectives, shards(): most = lax.all_to_all(most, NEAR, 0, 0, tiled=True)  14.4 us
    ppermute x4, starting transfers between devices, both_ways(): lax.ppermute(array_up, axes, up)  14 us
    ppermute x4, starting transfers between devices, both_ways(): lax.ppermute(array_down, axes, down)  11.7 us
  transfers between devices with their start and end apart: 16, of which 8 were waited for; matrix products, arithmetic and copies ran while one was open for 0% of the time, Pallas kernels for 6%

profile of v3, /device:TPU:8, one launch (start us, length us, event | category | flops | bytes accessed | tf_op | source)
XLA Modules:
  0.0 197.7 jit_solution(1165849523351597017)
XLA Ops:
  0.6 0.0 copy-start.1
  0.6 0.0 copy-start.3
  0.7 0.0 copy-start.5
  0.7 0.0 copy-start.7
  0.7 0.0 copy-start.9
  0.7 2.1 %shard_map.86 = (f32[5,8,16,256]{3,2,1,0:T(8,128)}, f32[16,256]{1,0:T(8,128)}, f32[8,256]{1,0:T(8,128)}) custom-call(f32[8,16,256]{2,1,0:T(8,128)} %s_own.3, f32[8,16,256]{2,1,0:T(8,128)} %x_own.3, f32[8,16,256]{2,1,0:T(8,128)} %y_own.3, f32[8,16,256]{2,1,0:T(8,128)} %z_own.3, f32[8,16,256]{2,1,0:T(8,128)} %b_own.3), custom_call_target="tpu_custom_call" | custom-call | flops 1000000 | bytes 655360 | tf_op jit(solution)/shard_map/pallas_call | solution.py:287
  2.8 5.0 %collective-permute-start.7 = (f32[5,8,16,256]{3,2,1,0:T(8,128)}, f32[5,8,16,256]{3,2,1,0:T(8,128)S(1)}, u32[]{:S(2)}, u32[]{:S(2)}) collective-permute-start(f32[5,8,16,256]{3,2,1,0:T(8,128)} %get-tuple-element.19), channel_id=1, source_target_pairs={{0,16},{16,32},{32,48},{48,64},{64,80},{80,96},{96,112},{112,128},... | collective-permute-start | bytes 1966088 | tf_op jit(solution)/shard_map/ppermute | solution.py:32
  7.8 1.3 collective-permute-start.8
  9.1 27.0 %collective-permute-done.7.x_low = f32[5,8,16,256]{3,2,1,0:T(8,128)S(1)} collective-permute-done((f32[5,8,16,256]{3,2,1,0:T(8,128)}, f32[5,8,16,256]{3,2,1,0:T(8,128)S(1)}, u32[]{:S(2)}, u32[]{:S(2)}) %collective-permute-start.7) | collective-permute-done | bytes 655392 | tf_op jit(solution)/shard_map/ppermute | solution.py:32
  36.1 0.0 collective-permute-done.8.x_high
  36.1 0.9 copy-done
  37.0 0.9 copy-done.2
  37.9 0.9 copy-done.4
  38.8 0.9 copy-done.6
  39.7 0.9 copy-done.8
  40.6 1.1 shard_map.89
  41.8 1.9 collective-permute-start.9
  43.7 4.5 %collective-permute-start.10 = (f32[5,15,8,256]{3,2,1,0:T(8,128)}, f32[5,15,8,256]{3,2,1,0:T(8,128)S(1)}, u32[]{:S(2)}, u32[]{:S(2)}) collective-permute-start(f32[5,15,8,256]{3,2,1,0:T(8,128)} %get-tuple-element.21), channel_id=1, source_target_pairs={{1,0},{2,1},{3,2},{4,3},{5,4},{6,5},{7,6},{8,7},{9,8},{10,9},{11,1... | collective-permute-start | bytes 1843208 | tf_op jit(solution)/shard_map/ppermute | solution.py:32
  48.2 19.5 %collective-permute-start.11 = (f32[8,16,256]{2,1,0:T(8,128)S(1)}, f32[8,16,256]{2,1,0:T(8,128)S(1)}, u32[]{:S(2)}, u32[]{:S(2)}) collective-permute-start(f32[8,16,256]{2,1,0:T(8,128)S(1)} %copy-done.8), channel_id=1, source_target_pairs={{0,1008},{16,992},{32,976},{48,960},{64,944},{80,928},{96,912},{11... | collective-permute-start | bytes 393224 | tf_op jit(solution)/shard_map/ppermute | solution.py:305
  67.8 22.9 %collective-permute-done.11.own = f32[8,16,256]{2,1,0:T(8,128)S(1)} collective-permute-done((f32[8,16,256]{2,1,0:T(8,128)S(1)}, f32[8,16,256]{2,1,0:T(8,128)S(1)}, u32[]{:S(2)}, u32[]{:S(2)}) %collective-permute-start.11) | collective-permute-done | bytes 131104 | tf_op jit(solution)/shard_map/ppermute | solution.py:305
  90.6 5.2 %collective-permute-start.12 = (f32[8,16,256]{2,1,0:T(8,128)S(1)}, f32[8,16,256]{2,1,0:T(8,128)S(1)}, u32[]{:S(2)}, u32[]{:S(2)}) collective-permute-start(f32[8,16,256]{2,1,0:T(8,128)S(1)} %collective-permute-done.11.own), channel_id=1, source_target_pairs={{0,16},{16,32},{32,48},{48,64},{64,80},{80,96},{96,112},{112,128},... | collective-permute-start | bytes 393224 | tf_op jit(solution)/shard_map/ppermute | solution.py:32
  95.8 1.3 collective-permute-start.13
  97.1 0.0 copy-done.15
  97.1 1.9 collective-permute-start.1
  99.1 4.1 %collective-permute-done.1.before_y = f32[8,256]{1,0:T(8,128)S(1)} collective-permute-done((f32[8,256]{1,0:T(8,128)S(1)}, f32[8,256]{1,0:T(8,128)S(1)}, u32[]{:S(2)}, u32[]{:S(2)}) %collective-permute-start.1) | collective-permute-done | bytes 8224 | tf_op jit(solution)/shard_map/ppermute | solution.py:316
  103.1 0.0 copy-done.14
  103.1 5.9 %collective-permute-start = (f32[16,256]{1,0:T(8,128)S(1)}, f32[16,256]{1,0:T(8,128)S(1)}, u32[]{:S(2)}, u32[]{:S(2)}) collective-permute-start(f32[16,256]{1,0:T(8,128)S(1)} %copy-done.14), channel_id=1, source_target_pairs={{0,16},{16,32},{32,48},{48,64},{64,80},{80,96},{96,112},{112,128},... | collective-permute-start | bytes 49160 | tf_op jit(solution)/shard_map/ppermute | solution.py:315
  109.1 1.4 collective-permute-done.before_x
  110.5 0.2 shard_map.87
  110.7 14.4 %all_to_all.5.values = f32[32,1,128]{2,1,0:T(1,128)S(1)} all-to-all(f32[32,1,128]{2,1,0:T(1,128)S(1)} %shard_map.87), channel_id=1, replica_groups=mesh['gx_0'=32,'gx_1'=2,'gy_0'=4,'gy_1'=2,'gy_2'=2] {'gx_1','gy_0','gy_1..., dimensions={0} | all-to-all | bytes 32768 | tf_op jit(solution)/shard_map/all_to_all | solution.py:319
  125.1 20.6 %collective-permute-start.2 = (f32[8,128]{1,0:T(8,128)S(1)}, f32[8,128]{1,0:T(8,128)S(1)}, u32[]{:S(2)}, u32[]{:S(2)}) collective-permute-start(f32[8,128]{1,0:T(8,128)S(1)} %shard_map.88), channel_id=1, source_target_pairs={{0,512},{32,544},{64,576},{96,608},{128,640},{160,672},{192,704},{... | collective-permute-start | bytes 12296 | tf_op jit(solution)/shard_map/ppermute | solution.py:324
  145.7 3.2 %collective-permute-done.2 = f32[8,128]{1,0:T(8,128)S(1)} collective-permute-done((f32[8,128]{1,0:T(8,128)S(1)}, f32[8,128]{1,0:T(8,128)S(1)}, u32[]{:S(2)}, u32[]{:S(2)}) %collective-permute-start.2) | collective-permute-done | bytes 4128 | tf_op jit(solution)/shard_map/ppermute | solution.py:324
  148.9 3.9 %collective-permute-start.3 = (f32[8,128]{1,0:T(8,128)S(1)}, f32[8,128]{1,0:T(8,128)S(1)}, u32[]{:S(2)}, u32[]{:S(2)}) collective-permute-start(f32[8,128]{1,0:T(8,128)S(1)} %max.13), channel_id=1, source_target_pairs={{0,256},{32,288},{64,320},{96,352},{128,384},{160,416},{192,448},{... | collective-permute-start | bytes 12296 | tf_op jit(solution)/shard_map/ppermute | solution.py:324
  152.8 0.0 collective-permute-done.12.x_low
  152.8 0.0 collective-permute-done.13.x_high
  152.9 0.7 shard_map.91
  153.6 0.7 copy-done.10
  154.2 1.9 collective-permute-start.14
  156.1 4.5 %collective-permute-start.15 = (f32[15,8,256]{2,1,0:T(8,128)}, f32[15,8,256]{2,1,0:T(8,128)}, u32[]{:S(2)}, u32[]{:S(2)}) collective-permute-start(f32[15,8,256]{2,1,0:T(8,128)} %get-tuple-element.25), channel_id=1, source_target_pairs={{1,0},{2,1},{3,2},{4,3},{5,4},{6,5},{7,6},{8,7},{9,8},{10,9},{11,1... | collective-permute-start | bytes 368648 | tf_op jit(solution)/shard_map/ppermute | solution.py:32
  160.7 2.4 %collective-permute-done.3 = f32[8,128]{1,0:T(8,128)S(1)} collective-permute-done((f32[8,128]{1,0:T(8,128)S(1)}, f32[8,128]{1,0:T(8,128)S(1)}, u32[]{:S(2)}, u32[]{:S(2)}) %collective-permute-start.3) | collective-permute-done | bytes 4128 | tf_op jit(solution)/shard_map/ppermute | solution.py:324
  163.1 7.8 %collective-permute-start.4 = (f32[8,128]{1,0:T(8,128)S(1)}, f32[8,128]{1,0:T(8,128)S(1)}, u32[]{:S(2)}, u32[]{:S(2)}) collective-permute-start(f32[8,128]{1,0:T(8,128)S(1)} %max.14), channel_id=1, source_target_pairs={{0,128},{32,160},{64,192},{96,224},{128,0},{160,32},{192,64},{224,... | collective-permute-start | bytes 12296 | tf_op jit(solution)/shard_map/ppermute | solution.py:324
  170.9 1.6 collective-permute-done.4
  172.5 3.7 %collective-permute-start.5 = (f32[8,128]{1,0:T(8,128)S(1)}, f32[8,128]{1,0:T(8,128)S(1)}, u32[]{:S(2)}, u32[]{:S(2)}) collective-permute-start(f32[8,128]{1,0:T(8,128)S(1)} %max.15), channel_id=1, source_target_pairs={{0,64},{32,96},{64,0},{96,32},{128,192},{160,224},{192,128},{224,1... | collective-permute-start | bytes 12296 | tf_op jit(solution)/shard_map/ppermute | solution.py:324
  176.2 0.1 add_convert_fusion.keep
  176.3 2.6 %collective-permute-done.5 = f32[8,128]{1,0:T(8,128)S(1)} collective-permute-done((f32[8,128]{1,0:T(8,128)S(1)}, f32[8,128]{1,0:T(8,128)S(1)}, u32[]{:S(2)}, u32[]{:S(2)}) %collective-permute-start.5) | collective-permute-done | bytes 4128 | tf_op jit(solution)/shard_map/ppermute | solution.py:324
  178.9 6.2 %collective-permute-start.6 = (f32[8,128]{1,0:T(8,128)S(1)}, f32[8,128]{1,0:T(8,128)S(1)}, u32[]{:S(2)}, u32[]{:S(2)}) collective-permute-start(f32[8,128]{1,0:T(8,128)S(1)} %max.16.bound), channel_id=1, source_target_pairs={{0,32},{32,0},{64,96},{96,64},{128,160},{160,128},{192,224},{224,1... | collective-permute-start | bytes 12296 | tf_op jit(solution)/shard_map/ppermute | solution.py:324
  185.1 0.0 collective-permute-done.9.y_low
  185.1 0.0 collective-permute-done.10.y_high
  185.1 0.0 copy-done.1
  185.2 0.0 copy-done.3
  185.2 0.0 copy-done.5
  185.2 0.0 copy-done.7
  185.2 0.0 copy-done.9
  185.2 6.5 %shard_map.90 = (f32[24,2,48,128]{3,2,1,0:T(8,128)S(1)}, f32[24,2,48,128]{3,2,1,0:T(8,128)S(1)}, f32[24,2,48,128]{3,2,1,0:T(8,128)S(1)}, f32[24,2,48,128]{3,2,1,...) custom-call(f32[2]{0:T(128)S(1)} %add_convert_fusion.keep, ...), custom_call_target="tpu_custom_call" | custom-call | flops 30000000 | bytes 3194888 | tf_op jit(solution)/shard_map/pallas_call | solution.py:287
  191.7 0.0 collective-permute-done.14.y_low
  191.7 0.0 collective-permute-done.15.y_high
  191.7 0.0 copy-done.11
  191.7 0.0 copy-start.12
  191.8 0.0 copy-start.13
  191.8 4.1 %shard_map.92.mirrored = f32[9,8,2,16,128]{4,3,2,1,0:T(8,128)S(1)} custom-call(f32[8,16,256]{2,1,0:T(8,128)S(1)} %collective-permute-done.11.own, f32[8,16,256]{2,1,0:T(8,128)S(1)} %collective-permute-done.12.x_low, f32[8,16,256]{2,1,0:T(8,128)S(1)} %copy-done.11, f32[15,8,256]{2,1,0:T(8,128)} %collective-permute-done.14.y_low, ...), custom_call_target="tpu_custom_call" | custom-call | flops 20000000 | bytes 7716864 | tf_op jit(solution)/shard_map/pallas_call | solution.py:287
  195.8 0.0 collective-permute-done.6.other_bound
  195.9 0.0 copy-done.12
  195.9 0.0 copy-done.13
  195.9 1.9 shard_map.93
  (14 shorter events, 0.1 us)
Async XLA Ops:
  0.6 184.5 %copy-start.1 = (f32[8,16,256]{2,1,0:T(8,128)S(1)}, f32[8,16,256]{2,1,0:T(8,128)}, u32[]{:S(2)}) copy-start(f32[8,16,256]{2,1,0:T(8,128)} %s_own.3) | copy-start | bytes 393220
  0.6 184.5 %copy-start.3 = (f32[8,16,256]{2,1,0:T(8,128)S(1)}, f32[8,16,256]{2,1,0:T(8,128)}, u32[]{:S(2)}) copy-start(f32[8,16,256]{2,1,0:T(8,128)} %x_own.3) | copy-start | bytes 393220
  0.7 184.5 %copy-start.5 = (f32[8,16,256]{2,1,0:T(8,128)S(1)}, f32[8,16,256]{2,1,0:T(8,128)}, u32[]{:S(2)}) copy-start(f32[8,16,256]{2,1,0:T(8,128)} %y_own.3) | copy-start | bytes 393220
  0.7 184.5 %copy-start.7 = (f32[8,16,256]{2,1,0:T(8,128)S(1)}, f32[8,16,256]{2,1,0:T(8,128)}, u32[]{:S(2)}) copy-start(f32[8,16,256]{2,1,0:T(8,128)} %z_own.3) | copy-start | bytes 393220
  0.7 184.5 %copy-start.9 = (f32[8,16,256]{2,1,0:T(8,128)S(1)}, f32[8,16,256]{2,1,0:T(8,128)}, u32[]{:S(2)}) copy-start(f32[8,16,256]{2,1,0:T(8,128)} %b_own.3) | copy-start | bytes 393220
  2.8 33.3 %collective-permute-start.7 = (f32[5,8,16,256]{3,2,1,0:T(8,128)}, f32[5,8,16,256]{3,2,1,0:T(8,128)S(1)}, u32[]{:S(2)}, u32[]{:S(2)}) collective-permute-start(f32[5,8,16,256]{3,2,1,0:T(8,128)} %get-tuple-element.19), channel_id=1, source_target_pairs={{0,16},{16,32},{32,48},{48,64},{64,80},{80,96},{96,112},{112,128},... | collective-permute-start | bytes 1966088 | tf_op jit(solution)/shard_map/ppermute | solution.py:32
  7.8 28.3 %collective-permute-start.8 = (f32[5,8,16,256]{3,2,1,0:T(8,128)}, f32[5,8,16,256]{3,2,1,0:T(8,128)S(1)}, u32[]{:S(2)}, u32[]{:S(2)}) collective-permute-start(f32[5,8,16,256]{3,2,1,0:T(8,128)} %get-tuple-element.19), channel_id=1, source_target_pairs={{16,0},{32,16},{48,32},{64,48},{80,64},{96,80},{112,96},{128,112},... | collective-permute-start | bytes 1966088 | tf_op jit(solution)/shard_map/ppermute | solution.py:32
  36.1 0.9 copy-start
  37.0 0.9 copy-start.2
  37.9 0.9 copy-start.4
  38.8 0.9 copy-start.6
  39.7 0.9 copy-start.8
  40.6 56.5 %copy-start.15 = (f32[8,256]{1,0:T(8,128)S(1)}, f32[8,256]{1,0:T(8,128)}, u32[]{:S(2)}) copy-start(f32[8,256]{1,0:T(8,128)} %get-tuple-element.18) | copy-start | bytes 24580
  40.6 62.5 %copy-start.14 = (f32[16,256]{1,0:T(8,128)S(1)}, f32[16,256]{1,0:T(8,128)}, u32[]{:S(2)}) copy-start(f32[16,256]{1,0:T(8,128)} %get-tuple-element.17) | copy-start | bytes 49156
  41.8 143.4 %collective-permute-start.9 = (f32[5,15,8,256]{3,2,1,0:T(8,128)}, f32[5,15,8,256]{3,2,1,0:T(8,128)S(1)}, u32[]{:S(2)}, u32[]{:S(2)}) collective-permute-start(f32[5,15,8,256]{3,2,1,0:T(8,128)} %get-tuple-element.20), channel_id=1, source_target_pairs={{0,1},{1,2},{2,3},{3,4},{4,5},{5,6},{6,7},{7,8},{8,9},{9,10},{10,1... | collective-permute-start | bytes 1843208 | tf_op jit(solution)/shard_map/ppermute | solution.py:32
  43.7 141.5 %collective-permute-start.10 = (f32[5,15,8,256]{3,2,1,0:T(8,128)}, f32[5,15,8,256]{3,2,1,0:T(8,128)S(1)}, u32[]{:S(2)}, u32[]{:S(2)}) collective-permute-start(f32[5,15,8,256]{3,2,1,0:T(8,128)} %get-tuple-element.21), channel_id=1, source_target_pairs={{1,0},{2,1},{3,2},{4,3},{5,4},{6,5},{7,6},{8,7},{9,8},{10,9},{11,1... | collective-permute-start | bytes 1843208 | tf_op jit(solution)/shard_map/ppermute | solution.py:32
  48.2 42.4 %collective-permute-start.11 = (f32[8,16,256]{2,1,0:T(8,128)S(1)}, f32[8,16,256]{2,1,0:T(8,128)S(1)}, u32[]{:S(2)}, u32[]{:S(2)}) collective-permute-start(f32[8,16,256]{2,1,0:T(8,128)S(1)} %copy-done.8), channel_id=1, source_target_pairs={{0,1008},{16,992},{32,976},{48,960},{64,944},{80,928},{96,912},{11... | collective-permute-start | bytes 393224 | tf_op jit(solution)/shard_map/ppermute | solution.py:305
  90.6 62.2 %collective-permute-start.12 = (f32[8,16,256]{2,1,0:T(8,128)S(1)}, f32[8,16,256]{2,1,0:T(8,128)S(1)}, u32[]{:S(2)}, u32[]{:S(2)}) collective-permute-start(f32[8,16,256]{2,1,0:T(8,128)S(1)} %collective-permute-done.11.own), channel_id=1, source_target_pairs={{0,16},{16,32},{32,48},{48,64},{64,80},{80,96},{96,112},{112,128},... | collective-permute-start | bytes 393224 | tf_op jit(solution)/shard_map/ppermute | solution.py:32
  95.8 57.0 %collective-permute-start.13 = (f32[8,16,256]{2,1,0:T(8,128)S(1)}, f32[8,16,256]{2,1,0:T(8,128)S(1)}, u32[]{:S(2)}, u32[]{:S(2)}) collective-permute-start(f32[8,16,256]{2,1,0:T(8,128)S(1)} %collective-permute-done.11.own), channel_id=1, source_target_pairs={{16,0},{32,16},{48,32},{64,48},{80,64},{96,80},{112,96},{128,112},... | collective-permute-start | bytes 393224 | tf_op jit(solution)/shard_map/ppermute | solution.py:32
  97.1 6.0 %collective-permute-start.1 = (f32[8,256]{1,0:T(8,128)S(1)}, f32[8,256]{1,0:T(8,128)S(1)}, u32[]{:S(2)}, u32[]{:S(2)}) collective-permute-start(f32[8,256]{1,0:T(8,128)S(1)} %copy-done.15), channel_id=1, source_target_pairs={{0,1},{1,2},{2,3},{3,4},{4,5},{5,6},{6,7},{7,8},{8,9},{9,10},{10,1... | collective-permute-start | bytes 24584 | tf_op jit(solution)/shard_map/ppermute | solution.py:316
  103.1 7.3 %collective-permute-start = (f32[16,256]{1,0:T(8,128)S(1)}, f32[16,256]{1,0:T(8,128)S(1)}, u32[]{:S(2)}, u32[]{:S(2)}) collective-permute-start(f32[16,256]{1,0:T(8,128)S(1)} %copy-done.14), channel_id=1, source_target_pairs={{0,16},{16,32},{32,48},{48,64},{64,80},{80,96},{96,112},{112,128},... | collective-permute-start | bytes 49160 | tf_op jit(solution)/shard_map/ppermute | solution.py:315
  125.1 23.8 %collective-permute-start.2 = (f32[8,128]{1,0:T(8,128)S(1)}, f32[8,128]{1,0:T(8,128)S(1)}, u32[]{:S(2)}, u32[]{:S(2)}) collective-permute-start(f32[8,128]{1,0:T(8,128)S(1)} %shard_map.88), channel_id=1, source_target_pairs={{0,512},{32,544},{64,576},{96,608},{128,640},{160,672},{192,704},{... | collective-permute-start | bytes 12296 | tf_op jit(solution)/shard_map/ppermute | solution.py:324
  148.9 14.2 %collective-permute-start.3 = (f32[8,128]{1,0:T(8,128)S(1)}, f32[8,128]{1,0:T(8,128)S(1)}, u32[]{:S(2)}, u32[]{:S(2)}) collective-permute-start(f32[8,128]{1,0:T(8,128)S(1)} %max.13), channel_id=1, source_target_pairs={{0,256},{32,288},{64,320},{96,352},{128,384},{160,416},{192,448},{... | collective-permute-start | bytes 12296 | tf_op jit(solution)/shard_map/ppermute | solution.py:324
  153.6 0.7 copy-start.10
  154.2 37.5 %collective-permute-start.14 = (f32[15,8,256]{2,1,0:T(8,128)}, f32[15,8,256]{2,1,0:T(8,128)}, u32[]{:S(2)}, u32[]{:S(2)}) collective-permute-start(f32[15,8,256]{2,1,0:T(8,128)} %get-tuple-element.24), channel_id=1, source_target_pairs={{0,1},{1,2},{2,3},{3,4},{4,5},{5,6},{6,7},{7,8},{8,9},{9,10},{10,1... | collective-permute-start | bytes 368648 | tf_op jit(solution)/shard_map/ppermute | solution.py:32
  156.1 35.6 %collective-permute-start.15 = (f32[15,8,256]{2,1,0:T(8,128)}, f32[15,8,256]{2,1,0:T(8,128)}, u32[]{:S(2)}, u32[]{:S(2)}) collective-permute-start(f32[15,8,256]{2,1,0:T(8,128)} %get-tuple-element.25), channel_id=1, source_target_pairs={{1,0},{2,1},{3,2},{4,3},{5,4},{6,5},{7,6},{8,7},{9,8},{10,9},{11,1... | collective-permute-start | bytes 368648 | tf_op jit(solution)/shard_map/ppermute | solution.py:32
  163.1 9.4 %collective-permute-start.4 = (f32[8,128]{1,0:T(8,128)S(1)}, f32[8,128]{1,0:T(8,128)S(1)}, u32[]{:S(2)}, u32[]{:S(2)}) collective-permute-start(f32[8,128]{1,0:T(8,128)S(1)} %max.14), channel_id=1, source_target_pairs={{0,128},{32,160},{64,192},{96,224},{128,0},{160,32},{192,64},{224,... | collective-permute-start | bytes 12296 | tf_op jit(solution)/shard_map/ppermute | solution.py:324
  172.5 6.4 %collective-permute-start.5 = (f32[8,128]{1,0:T(8,128)S(1)}, f32[8,128]{1,0:T(8,128)S(1)}, u32[]{:S(2)}, u32[]{:S(2)}) collective-permute-start(f32[8,128]{1,0:T(8,128)S(1)} %max.15), channel_id=1, source_target_pairs={{0,64},{32,96},{64,0},{96,32},{128,192},{160,224},{192,128},{224,1... | collective-permute-start | bytes 12296 | tf_op jit(solution)/shard_map/ppermute | solution.py:324
  178.9 12.8 %copy-start.11 = (f32[8,16,256]{2,1,0:T(8,128)S(1)}, f32[8,16,256]{2,1,0:T(8,128)}, u32[]{:S(2)}) copy-start(f32[8,16,256]{2,1,0:T(8,128)} %copy-done.10) | copy-start | bytes 393220
  178.9 16.9 %collective-permute-start.6 = (f32[8,128]{1,0:T(8,128)S(1)}, f32[8,128]{1,0:T(8,128)S(1)}, u32[]{:S(2)}, u32[]{:S(2)}) collective-permute-start(f32[8,128]{1,0:T(8,128)S(1)} %max.16.bound), channel_id=1, source_target_pairs={{0,32},{32,0},{64,96},{96,64},{128,160},{160,128},{192,224},{224,1... | collective-permute-start | bytes 12296 | tf_op jit(solution)/shard_map/ppermute | solution.py:324
  191.7 4.1 %copy-start.12 = (f32[2]{0:T(128)S(1)}, f32[2]{0:T(128)}, u32[]{:S(2)}) copy-start(f32[2]{0:T(128)} %low.1) | copy-start | bytes 28
  191.8 4.1 %copy-start.13 = (f32[2]{0:T(128)S(1)}, f32[2]{0:T(128)}, u32[]{:S(2)}) copy-start(f32[2]{0:T(128)} %high.1) | copy-start | bytes 28

commit v4 on v3

--- a/solution.py
+++ b/solution.py
@@ -17,7 +17,7 @@
 NEAR = ("gx_1",) + GY
 VMEM = pl.BlockSpec(memory_space=pltpu.VMEM)
 SMEM = pl.BlockSpec(memory_space=pltpu.SMEM)
-STRIDES = (16, 8, 4, 2, 1)
+ANY = pl.BlockSpec(memory_space=pl.ANY)
 SHARED = ((7, 1, 1), (6, 2, 2), (5, 3, 3), (16, 22, 1), (17, 21, 2), (18, 20, 3), (4, 19, 4))
 EDGE = BX + len(SHARED)
 
@@ -92,20 +92,26 @@
 
 
 def prepare_kernel(
-    keep, s_own, x_own, y_own, z_own, b_own, x_low, x_high, y_low, y_high, d, cx, cy, ly, cz, lz, top, out, shift, first, second
+    own, x_low, x_high, y_low, y_high, d, cx, cy, ly, cz, lz, top, out, shift, first, second, held, sem
 ):
     lane = lax.broadcasted_iota(jnp.int32, (8, 128), 1)
     line = lax.broadcasted_iota(jnp.int32, (8, 128), 0)
-    fields = ((shift, s_own), (cx, x_own), (cy, y_own), (cz, z_own), (first, b_own))
-    for n, (ref, own) in enumerate(fields):
+    keep = [jnp.where(lax.axis_index(axes) < lax.axis_size(axes) - 1, 1.0, 0.0) for axes in (GX, GY)]
+    copy = pltpu.make_async_copy(own, held, sem)
+    copy.start()
+    fields = (shift, cx, cy, cz, first)
+    for n, ref in enumerate(fields):
         for i in range(BX):
             place(ref, i, H, x_low[n, i])
-            place(ref, H + i, H, own[i])
             place(ref, H + BX + i, H, x_high[n, i])
         place_sides(ref, y_low.at[n], y_high.at[n])
+    copy.wait()
+    for n, ref in enumerate(fields):
+        for i in range(BX):
+            place(ref, H + i, H, held[n, i])
     for i in range(BX):
         for h in range(2):
-            out[0, i, h] = b_own[i, :, 128 * h : 128 * h + 128]
+            out[0, i, h] = held[4, i, :, 128 * h : 128 * h + 128]
 
     tiles = [PAD + 8 * t for t in range(EY // 8)]
 
@@ -168,17 +174,34 @@
     basis(first, second, d, cx, cy, ly, cz, lz, out)
 
 
-def pack_kernel(shift, cx, cy, cz, right_side, own, plane_x, plane_y, sems):
+def pack_kernel(shift, cx, cy, cz, right_side, own, plane_x, plane_y, most, base_x, base_y, sems):
     copies = [pltpu.make_async_copy(a, own.at[n], sems.at[n]) for n, a in enumerate((shift, cx, cy, cz, right_side))]
     for copy in copies:
         copy.start()
+    lane = lax.broadcasted_iota(jnp.int32, (BY, NZ), 1)
+    line = lax.broadcasted_iota(jnp.int32, (BY, NZ), 0)
     copies[1].wait()
     plane_x[...] = own[1, BX - 1]
     copies[2].wait()
     for i in range(BX):
         plane_y[i : i + 1, :] = own[2, i, BY - 1 : BY, :]
-    for n in (0, 3, 4):
-        copies[n].wait()
+    copies[0].wait()
+    copies[3].wait()
+    whole = jnp.zeros((BY, NZ), jnp.float32)
+    for r in range(BX):
+        x, y, z = own[1, r], own[2, r], own[3, r]
+        if r:
+            x = x + own[1, r - 1]
+        y = y + jnp.where(line == 0, 0.0, pltpu.roll(y, 1, 0))
+        z = z + jnp.where(lane == 0, 0.0, pltpu.roll(z, 1, 1))
+        row = own[0, r] + 2.0 * (x + y + z)
+        base_y[r : r + 1, :] = row[0:1, :]
+        if r:
+            whole = jnp.maximum(whole, jnp.where(line == 0, 0.0, row))
+        else:
+            base_x[...] = row
+    most[...] = whole
+    copies[4].wait()
 
 
 def edges(row, first_lines, last_lines):
@@ -191,12 +214,14 @@
         first_lines[t] = jnp.where(line < H - n, row(a, 0), pltpu.roll(row(b, 0), H - n, 0))
 
 
-def edge_kernel(s_own, x_own, y_own, z_own, b_own, x_low, x_high, first_lines, last_lines):
-    for n, own in enumerate((s_own, x_own, y_own, z_own, b_own)):
-
-        def row(r, y, n=n, own=own):
-            block = (x_low.at[n], own, x_high.at[n])[r // BX]
-            return block[r % BX, y : y + H, :]
+def edge_kernel(own, x_low, x_high, first_lines, last_lines, held, sem):
+    copy = pltpu.make_async_copy(own, held, sem)
+    copy.start()
+    copy.wait()
+    for n in range(5):
+
+        def row(r, y, n=n):
+            return (x_low, held, x_high)[r // BX][n, r % BX, y : y + H, :]
 
         edges(row, first_lines.at[n], last_lines.at[n])
 
@@ -205,25 +230,22 @@
     edges(lambda r, y: (x_low, own, x_high)[r // BX][BX - 1 - r % BX, y : y + H, :], first_lines, last_lines)
 
 
-def bound_kernel(shift, cx, cy, cz, before_x, before_y, out):
-    lane = lax.broadcasted_iota(jnp.int32, (BY, NZ), 1)
+def bound_kernel(most, base_x, base_y, before_x, before_y, out):
     line = lax.broadcasted_iota(jnp.int32, (BY, NZ), 0)
-    most = jnp.zeros((BY, NZ), jnp.float32)
-    for r in range(BX):
-        x, y, z = cx[r], cy[r], cz[r]
-        low_x = before_x[...] if r == 0 else cx[r - 1]
-        low_y = jnp.where(line == 0, before_y[r : r + 1, :], pltpu.roll(y, 1, 0))
-        low_z = jnp.where(lane == 0, 0.0, pltpu.roll(z, 1, 1))
-        most = jnp.maximum(most, shift[r] + 2.0 * (x + low_x + y + low_y + z + low_z))
-    most = jnp.max(jnp.max(most, axis=0, keepdims=True), axis=1, keepdims=True)
-    out[...] = jnp.broadcast_to(most[None], out.shape)
+    row = lax.broadcasted_iota(jnp.int32, (BX, NZ), 0)
+    corner = jnp.where(line == 0, before_y[0:1, :], 0.0)
+    largest = jnp.maximum(most[...], base_x[...] + 2.0 * (before_x[...] + corner))
+    first = jnp.where(row == 0, 0.0, base_y[...] + 2.0 * before_y[...])
+    largest = jnp.maximum(jnp.max(largest, axis=0, keepdims=True), jnp.max(first, axis=0, keepdims=True))
+    largest = jnp.max(largest, axis=1, keepdims=True)
+    out[...] = jnp.broadcast_to(largest[None], out.shape)
 
 
 def spread_kernel(values, out):
     most = values[0]
     for i in range(1, values.shape[0]):
         most = jnp.maximum(most, values[i])
-    out[...] = jnp.broadcast_to(most, out.shape)
+    out[...] = jnp.broadcast_to(most[None], out.shape)
 
 
 def polynomials(low, high, bound, top):
@@ -251,8 +273,11 @@
     return x, r
 
 
-def combine_kernel(low, high, bound, other_bound, top, plain, mirrored, pressure, residual):
-    bound = jnp.maximum(bound[...], other_bound[...])
+def combine_kernel(low, high, bounds, top, plain, mirrored, pressure, residual):
+    bound = bounds[0]
+    for i in range(1, bounds.shape[0]):
+        bound = jnp.maximum(bound, bounds[i])
+    bound = jnp.broadcast_to(bound, (8, 128))
     found = [polynomials(low[f], high[f], bound, top[...]) for f in range(2)]
     sums, gaps = [], []
     for part in range(2):
@@ -282,12 +307,12 @@
     return jax.ShapeDtypeStruct(shape, jnp.float32)
 
 
-def kernel(body, out, operands, smem=0, scratch=(), mib=16, flops=1_000_000, where=VMEM):
+def kernel(body, out, operands, smem=0, anywhere=0, scratch=(), mib=16, flops=1_000_000):
     nbytes = sum(a.size * 4 for a in operands)
     return pl.pallas_call(
         body,
         out_shape=out,
-        in_specs=[SMEM] * smem + [where] * (len(operands) - smem),
+        in_specs=[SMEM] * smem + [ANY] * anywhere + [VMEM] * (len(operands) - smem - anywhere),
         out_specs=jax.tree.map(lambda _: VMEM, out),
         scratch_shapes=scratch,
         compiler_params=pltpu.CompilerParams(vmem_limit_bytes=mib << 20),
@@ -297,45 +322,47 @@
 
 def shards(right_side, shift, coef_x, coef_y, coef_z, low_frac, high_frac):
     nx, ny = lax.axis_size(GX), lax.axis_size(GY)
-    me_x, me_y = lax.axis_index(GX), lax.axis_index(GY)
     up_x, up_y = shift_pairs(nx)[0], shift_pairs(ny)[0]
     near = lax.axis_size(NEAR)
     given = (shift, coef_x, coef_y, coef_z, right_side)
 
-    mirror = lax.ppermute(right_side, GX, [(i, nx - 1 - i) for i in range(nx)])
-    own, plane_x, plane_y = kernel(
+    own, plane_x, plane_y, most, base_x, base_y = kernel(
         pack_kernel,
-        (f32(5, BX, BY, NZ), f32(BY, NZ), f32(BX, NZ)),
+        (f32(5, BX, BY, NZ), f32(BY, NZ), f32(BX, NZ), f32(BY, NZ), f32(BY, NZ), f32(BX, NZ)),
         given,
         scratch=[pltpu.SemaphoreType.DMA((5,))],
-        where=pl.BlockSpec(memory_space=pl.ANY),
+        anywhere=5,
         mib=56,
     )
-    x_low, x_high = both_ways(own, own, GX)
     before_x = lax.ppermute(plane_x, GX, up_x)
     before_y = lax.ppermute(plane_y, GY, up_y)
-
-    most = kernel(bound_kernel, f32(near, 1, 128), (*given[:4], before_x, before_y), mib=2)
+    x_low, x_high = both_ways(own, own, GX)
+    mirror = lax.ppermute(right_side, GX, [(i, nx - 1 - i) for i in range(nx)])
+
+    most = kernel(bound_kernel, f32(near, 1, 128), (most, base_x, base_y, before_x, before_y), mib=2)
     most = lax.all_to_all(most, NEAR, 0, 0, tiled=True)
-    most = kernel(spread_kernel, f32(8, 128), (most,), mib=2)
-    other = most
-    for stride in STRIDES:
-        most = jnp.maximum(most, other)
-        other = lax.ppermute(most, "gx_0", [(i, i ^ stride) for i in range(lax.axis_size("gx_0"))])
+    most = kernel(spread_kernel, f32(lax.axis_size("gx_0"), 1, 128), (most,), mib=2)
+    bounds = lax.all_to_all(most, "gx_0", 0, 0, tiled=True)
 
     edge = f32(5, EDGE, H, NZ)
-    first_lines, last_lines = kernel(edge_kernel, (edge, edge), (*given, x_low, x_high), mib=2)
+    first_lines, last_lines = kernel(
+        edge_kernel,
+        (edge, edge),
+        (own, x_low, x_high),
+        anywhere=1,
+        scratch=[pltpu.VMEM((5, BX, BY, NZ), jnp.float32), pltpu.SemaphoreType.DMA(())],
+        mib=4,
+    )
     y_low, y_high = both_ways(last_lines, first_lines, GY)
-    keep = jnp.stack([me_x < nx - 1, me_y < ny - 1]).astype(jnp.float32)
     wide = f32(EX, 2, EY + 2 * PAD, 128)
     scratch = pltpu.VMEM(wide.shape, jnp.float32)
     basis_out = f32(ITERS + 1, BX, 2, BY, 128)
     *operator, top, plain = kernel(
         prepare_kernel,
         (wide,) * 6 + (f32(8, 128), basis_out),
-        (keep, *given, x_low, x_high, y_low, y_high),
-        smem=1,
-        scratch=[scratch] * 3,
+        (own, x_low, x_high, y_low, y_high),
+        anywhere=1,
+        scratch=[scratch] * 3 + [pltpu.VMEM((5, BX, BY, NZ), jnp.float32), pltpu.SemaphoreType.DMA(())],
         flops=30_000_000,
         mib=6,
     )
@@ -355,7 +382,7 @@
     return kernel(
         combine_kernel,
         (f32(BX, BY, NZ), f32(BX, BY, NZ)),
-        (low_frac, high_frac, most, other, top, plain, mirrored),
+        (low_frac, high_frac, bounds, top, plain, mirrored),
         smem=2,
         mib=2,
         flops=3_000_000,

time: 198 us -> 168 us (0.85)
  the two profiles are of different devices: /device:TPU:8 before, /device:TPU:1 now
where the time goes in v4:
time: 168 us; the launch traced here: 167 us
  starting transfers between devices  79.5 us (47%)
  waiting for transfers between devices  48.9 us (29%)
  blocking collectives  16.9 us (10%)
  Pallas kernels  16.2 us (10%)
  local copies, waits for them, and re-layouts  4.97 us (3%)
    ppermute x4, waiting for transfers between devices, both_ways(): lax.ppermute(array_up, axes, up)  23.1 us
    ppermute x1, waiting for transfers between devices, shards(): mirror = lax.ppermute(right_side, GX, [(i, nx - 1 - i) for i in range(nx)])  22 us
    ppermute x1, starting transfers between devices, shards(): mirror = lax.ppermute(right_side, GX, [(i, nx - 1 - i) for i in range(nx)])  20.7 us
    ppermute x4, starting transfers between devices, both_ways(): lax.ppermute(array_up, axes, up)  20.4 us
    all_to_all x1, starting transfers between devices, shards(): bounds = lax.all_to_all(most, 'gx_0', 0, 0, tiled=True)  20.1 us
    all_to_all x1, blocking collectives, shards(): most = lax.all_to_all(most, NEAR, 0, 0, tiled=True)  16.9 us
    pallas_call x8, Pallas kernels, kernel(): pl.pallas_call(body, out_shape=out, in_specs=[SMEM] * smem + [ANY] * anyw...  16.2 us
    ppermute x4, starting transfers between devices, both_ways(): lax.ppermute(array_down, axes, down)  6.42 us
  transfers between devices with their start and end apart: 12, of which 5 were waited for; matrix products, arithmetic and copies ran while one was open for 0% of the time, Pallas kernels for 6%

profile of v4, /device:TPU:1, one launch (start us, length us, event | category | flops | bytes accessed | tf_op | source)
XLA Modules:
  0.0 167.3 jit_solution(2113121307063715945)
XLA Ops:
  0.6 0.0 copy-start.11
  0.6 2.1 %shard_map.86 = (f32[5,8,16,256]{3,2,1,0:T(8,128)}, f32[16,256]{1,0:T(8,128)}, f32[8,256]{1,0:T(8,128)}, f32[16,256]{1,0:T(8,128)}, f32[16,256]{1,0:T(8,128)}, /*index=5*/f32[8,256]{1,0:T(8,128)}) custom-call(f32[8,16,256]{2,1,0:T(8,128)} %shift.1, f32[8,16,256]{2,1,0:T(8,128)} %cx.1, f32[8,16,256]{2,1,0:T(8,128)} %cy.1, f32[8,16,256]{2,1,0:T(8,128)} %cz.1, ...), custom_call_target="tpu_custom_call" | custom-call | flops 1000000 | bytes 655360 | tf_op jit(solution)/shard_map/pallas_call | solution.py:312
  2.8 5.5 %collective-permute-start.2 = (f32[5,8,16,256]{3,2,1,0:T(8,128)}, f32[5,8,16,256]{3,2,1,0:T(8,128)S(1)}, u32[]{:S(2)}, u32[]{:S(2)}) collective-permute-start(f32[5,8,16,256]{3,2,1,0:T(8,128)} %get-tuple-element.25.own), channel_id=1, source_target_pairs={{0,16},{16,32},{32,48},{48,64},{64,80},{80,96},{96,112},{112,128},... | collective-permute-start | bytes 1966088 | tf_op jit(solution)/shard_map/ppermute | solution.py:32
  8.3 1.3 collective-permute-start.3
  9.6 23.1 %collective-permute-done.2.x_low = f32[5,8,16,256]{3,2,1,0:T(8,128)S(1)} collective-permute-done((f32[5,8,16,256]{3,2,1,0:T(8,128)}, f32[5,8,16,256]{3,2,1,0:T(8,128)S(1)}, u32[]{:S(2)}, u32[]{:S(2)}) %collective-permute-start.2) | collective-permute-done | bytes 655392 | tf_op jit(solution)/shard_map/ppermute | solution.py:32
  32.7 0.0 collective-permute-done.3.x_high
  32.7 0.0 copy-start
  32.7 1.1 copy-done
  33.8 0.0 copy-start.13
  33.8 0.0 copy-start.12
  33.8 0.0 copy-start.6
  33.8 0.0 copy-start.7
  33.8 0.0 copy-start.8
  33.8 0.0 copy-start.1
  33.8 1.4 shard_map.89
  35.2 7.0 %collective-permute-start.4 = (f32[5,15,8,256]{3,2,1,0:T(8,128)}, f32[5,15,8,256]{3,2,1,0:T(8,128)S(1)}, u32[]{:S(2)}, u32[]{:S(2)}) collective-permute-start(f32[5,15,8,256]{3,2,1,0:T(8,128)} %get-tuple-element.26), channel_id=1, source_target_pairs={{0,1},{1,2},{2,3},{3,4},{4,5},{5,6},{6,7},{7,8},{8,9},{9,10},{10,1... | collective-permute-start | bytes 1843208 | tf_op jit(solution)/shard_map/ppermute | solution.py:32
  42.2 1.9 %collective-permute-start.5 = (f32[5,15,8,256]{3,2,1,0:T(8,128)}, f32[5,15,8,256]{3,2,1,0:T(8,128)S(1)}, u32[]{:S(2)}, u32[]{:S(2)}) collective-permute-start(f32[5,15,8,256]{3,2,1,0:T(8,128)} %get-tuple-element.27), channel_id=1, source_target_pairs={{1,0},{2,1},{3,2},{4,3},{5,4},{6,5},{7,6},{8,7},{9,8},{10,9},{11,1... | collective-permute-start | bytes 1843208 | tf_op jit(solution)/shard_map/ppermute | solution.py:32
  44.1 0.0 copy-done.11
  44.1 20.7 %collective-permute-start.6 = (f32[8,16,256]{2,1,0:T(8,128)S(1)}, f32[8,16,256]{2,1,0:T(8,128)S(1)}, u32[]{:S(2)}, u32[]{:S(2)}) collective-permute-start(f32[8,16,256]{2,1,0:T(8,128)S(1)} %copy-done.11), channel_id=1, source_target_pairs={{0,1008},{16,992},{32,976},{48,960},{64,944},{80,928},{96,912},{11... | collective-permute-start | bytes 393224 | tf_op jit(solution)/shard_map/ppermute | solution.py:340
  64.9 22.0 %collective-permute-done.6.own = f32[8,16,256]{2,1,0:T(8,128)S(1)} collective-permute-done((f32[8,16,256]{2,1,0:T(8,128)S(1)}, f32[8,16,256]{2,1,0:T(8,128)S(1)}, u32[]{:S(2)}, u32[]{:S(2)}) %collective-permute-start.6) | collective-permute-done | bytes 131104 | tf_op jit(solution)/shard_map/ppermute | solution.py:340
  86.9 4.8 %collective-permute-start.7 = (f32[8,16,256]{2,1,0:T(8,128)S(1)}, f32[8,16,256]{2,1,0:T(8,128)S(1)}, u32[]{:S(2)}, u32[]{:S(2)}) collective-permute-start(f32[8,16,256]{2,1,0:T(8,128)S(1)} %collective-permute-done.6.own), channel_id=1, source_target_pairs={{0,16},{16,32},{32,48},{48,64},{64,80},{80,96},{96,112},{112,128},... | collective-permute-start | bytes 393224 | tf_op jit(solution)/shard_map/ppermute | solution.py:32
  91.7 1.3 collective-permute-start.8
  93.0 0.0 copy-done.13
  93.0 5.5 %collective-permute-start.1 = (f32[8,256]{1,0:T(8,128)S(1)}, f32[8,256]{1,0:T(8,128)S(1)}, u32[]{:S(2)}, u32[]{:S(2)}) collective-permute-start(f32[8,256]{1,0:T(8,128)S(1)} %copy-done.13), channel_id=1, source_target_pairs={{0,1},{1,2},{2,3},{3,4},{4,5},{5,6},{6,7},{7,8},{8,9},{9,10},{10,1... | collective-permute-start | bytes 24584 | tf_op jit(solution)/shard_map/ppermute | solution.py:338
  98.5 0.8 collective-permute-done.1.before_y
  99.3 0.0 copy-done.12
  99.3 6.4 %collective-permute-start = (f32[16,256]{1,0:T(8,128)S(1)}, f32[16,256]{1,0:T(8,128)S(1)}, u32[]{:S(2)}, u32[]{:S(2)}) collective-permute-start(f32[16,256]{1,0:T(8,128)S(1)} %copy-done.12), channel_id=1, source_target_pairs={{0,16},{16,32},{32,48},{48,64},{64,80},{80,96},{96,112},{112,128},... | collective-permute-start | bytes 49160 | tf_op jit(solution)/shard_map/ppermute | solution.py:337
  105.7 0.9 collective-permute-done.before_x
  106.5 0.0 copy-done.6
  106.5 0.0 copy-done.7
  106.6 0.0 copy-done.8
  106.6 0.1 shard_map.87
  106.7 16.9 %all_to_all.10.values = f32[32,1,128]{2,1,0:T(1,128)S(1)} all-to-all(f32[32,1,128]{2,1,0:T(1,128)S(1)} %shard_map.87), channel_id=1, replica_groups=mesh['gx_0'=32,'gx_1'=2,'gy_0'=4,'gy_1'=2,'gy_2'=2] {'gx_1','gy_0','gy_1..., dimensions={0} | all-to-all | bytes 32768 | tf_op jit(solution)/shard_map/all_to_all | solution.py:343
  123.5 0.6 shard_map.88
  124.2 20.1 %all-to-all-start.1 = ((f32[32,1,128]{2,1,0:T(1,128)}), f32[32,1,128]{2,1,0:T(1,128)S(1)}, u32[]{:S(2)}, u32[]{:S(2)}) async-start(f32[32,1,128]{2,1,0:T(1,128)} %shard_map.88), calls=%async_computation.1 | async-start | bytes 32768 | tf_op jit(solution)/shard_map/all_to_all | solution.py:345
  144.2 0.0 collective-permute-done.7.x_low
  144.2 0.0 collective-permute-done.8.x_high
  144.3 0.9 shard_map.91
  145.2 3.1 %collective-permute-start.9 = (f32[15,8,256]{2,1,0:T(8,128)S(1)}, f32[15,8,256]{2,1,0:T(8,128)S(1)}, u32[]{:S(2)}, u32[]{:S(2)}) collective-permute-start(f32[15,8,256]{2,1,0:T(8,128)S(1)} %get-tuple-element.30), channel_id=1, source_target_pairs={{0,1},{1,2},{2,3},{3,4},{4,5},{5,6},{6,7},{7,8},{8,9},{9,10},{10,1... | collective-permute-start | bytes 368648 | tf_op jit(solution)/shard_map/ppermute | solution.py:32
  148.3 1.9 %collective-permute-start.10 = (f32[15,8,256]{2,1,0:T(8,128)S(1)}, f32[15,8,256]{2,1,0:T(8,128)S(1)}, u32[]{:S(2)}, u32[]{:S(2)}) collective-permute-start(f32[15,8,256]{2,1,0:T(8,128)S(1)} %get-tuple-element.31), channel_id=1, source_target_pairs={{1,0},{2,1},{3,2},{4,3},{5,4},{6,5},{7,6},{8,7},{9,8},{10,9},{11,1... | collective-permute-start | bytes 368648 | tf_op jit(solution)/shard_map/ppermute | solution.py:32
  150.3 0.0 collective-permute-done.4.y_low
  150.3 0.0 copy-start.2
  150.3 0.8 copy-done.2
  151.1 0.0 collective-permute-done.5.y_high
  151.1 0.0 copy-start.4
  151.1 0.9 copy-done.4
  152.0 0.0 copy-done.1
  152.0 0.0 copy-start.3
  152.0 1.1 copy-done.3
  153.0 0.0 copy-start.5
  153.0 1.1 copy-done.5
  154.1 5.6 %shard_map.90 = (f32[24,2,48,128]{3,2,1,0:T(8,128)S(1)}, f32[24,2,48,128]{3,2,1,0:T(8,128)S(1)}, f32[24,2,48,128]{3,2,1,0:T(8,128)S(1)}, f32[24,2,48,128]{3,2,1,...) custom-call(f32[5,8,16,256]{3,2,1,0:T(8,128)S(1)} %copy-done.1, ...), custom_call_target="tpu_custom_call" | custom-call | flops 30000000 | bytes 3194880 | tf_op jit(solution)/shard_map/pallas_call | solution.py:312
  159.7 0.0 collective-permute-done.9.y_low
  159.8 0.0 collective-permute-done.10.y_high
  159.8 0.0 copy-start.9
  159.8 0.0 copy-start.10
  159.8 3.5 %shard_map.92.mirrored = f32[9,8,2,16,128]{4,3,2,1,0:T(8,128)S(1)} custom-call(f32[8,16,256]{2,1,0:T(8,128)S(1)} %collective-permute-done.6.own, f32[8,16,256]{2,1,0:T(8,128)S(1)} %collective-permute-done.7.x_low, f32[8,16,256]{2,1,0:T(8,128)} %collective-permute-done.8.x_high, f32[15,8,256]{2,1,0:T(8,128)S(1)} %collective-permute-done.9.y_low, ...), custom_call_target="tpu_custom_call" | custom-call | flops 20000000 | bytes 7716864 | tf_op jit(solution)/shard_map/pallas_call | solution.py:312
  163.3 2.2 %all-to-all-done.1.bounds = f32[32,1,128]{2,1,0:T(1,128)S(1)} async-done(((f32[32,1,128]{2,1,0:T(1,128)}), f32[32,1,128]{2,1,0:T(1,128)S(1)}, u32[]{:S(2)}, u32[]{:S(2)}) %all-to-all-start.1) | async-done | bytes 16416 | tf_op jit(solution)/shard_map/all_to_all | solution.py:345
  165.4 0.0 copy-done.9
  165.4 0.0 copy-done.10
  165.4 1.9 %shard_map.93 = (f32[8,16,256]{2,1,0:T(8,128)}, f32[8,16,256]{2,1,0:T(8,128)}) custom-call(f32[2]{0:T(128)S(1)} %copy-done.9, f32[2]{0:T(128)S(1)} %copy-done.10, f32[32,1,128]{2,1,0:T(1,128)S(1)} %all-to-all-done.1.bounds, f32[8,128]{1,0:T(8,128)S(1)} %get-tuple-element.28.top, f32[9,8,2,16,128]{4,3,2,1,0:T(8,128)S(1)} %get-tuple-element.29.plain, ...), custom_call_target="tpu_custom_call" | custom-call | flops 3000000 | bytes 2379792 | tf_op jit(solution)/shard_map/pallas_call | solution.py:312
Async XLA Ops:
  0.6 43.5 %copy-start.11 = (f32[8,16,256]{2,1,0:T(8,128)S(1)}, f32[8,16,256]{2,1,0:T(8,128)}, u32[]{:S(2)}) copy-start(f32[8,16,256]{2,1,0:T(8,128)} %right_side.1) | copy-start | bytes 393220
  2.8 29.9 %collective-permute-start.2 = (f32[5,8,16,256]{3,2,1,0:T(8,128)}, f32[5,8,16,256]{3,2,1,0:T(8,128)S(1)}, u32[]{:S(2)}, u32[]{:S(2)}) collective-permute-start(f32[5,8,16,256]{3,2,1,0:T(8,128)} %get-tuple-element.25.own), channel_id=1, source_target_pairs={{0,16},{16,32},{32,48},{48,64},{64,80},{80,96},{96,112},{112,128},... | collective-permute-start | bytes 1966088 | tf_op jit(solution)/shard_map/ppermute | solution.py:32
  8.3 24.4 %collective-permute-start.3 = (f32[5,8,16,256]{3,2,1,0:T(8,128)}, f32[5,8,16,256]{3,2,1,0:T(8,128)S(1)}, u32[]{:S(2)}, u32[]{:S(2)}) collective-permute-start(f32[5,8,16,256]{3,2,1,0:T(8,128)} %get-tuple-element.25.own), channel_id=1, source_target_pairs={{16,0},{32,16},{48,32},{64,48},{80,64},{96,80},{112,96},{128,112},... | collective-permute-start | bytes 1966088 | tf_op jit(solution)/shard_map/ppermute | solution.py:32
  32.7 1.1 copy-start
  33.8 59.3 %copy-start.13 = (f32[8,256]{1,0:T(8,128)S(1)}, f32[8,256]{1,0:T(8,128)}, u32[]{:S(2)}) copy-start(f32[8,256]{1,0:T(8,128)} %get-tuple-element.24) | copy-start | bytes 24580
  33.8 65.6 %copy-start.12 = (f32[16,256]{1,0:T(8,128)S(1)}, f32[16,256]{1,0:T(8,128)}, u32[]{:S(2)}) copy-start(f32[16,256]{1,0:T(8,128)} %get-tuple-element.23) | copy-start | bytes 49156
  33.8 72.8 %copy-start.6 = (f32[16,256]{1,0:T(8,128)S(1)}, f32[16,256]{1,0:T(8,128)}, u32[]{:S(2)}) copy-start(f32[16,256]{1,0:T(8,128)} %get-tuple-element.20.most) | copy-start | bytes 49156
  33.8 72.8 %copy-start.7 = (f32[16,256]{1,0:T(8,128)S(1)}, f32[16,256]{1,0:T(8,128)}, u32[]{:S(2)}) copy-start(f32[16,256]{1,0:T(8,128)} %get-tuple-element.21.base_x) | copy-start | bytes 49156
  33.8 72.8 %copy-start.8 = (f32[8,256]{1,0:T(8,128)S(1)}, f32[8,256]{1,0:T(8,128)}, u32[]{:S(2)}) copy-start(f32[8,256]{1,0:T(8,128)} %get-tuple-element.22.base_y) | copy-start | bytes 24580
  33.8 118.2 %copy-start.1 = (f32[5,8,16,256]{3,2,1,0:T(8,128)S(1)}, f32[5,8,16,256]{3,2,1,0:T(8,128)}, u32[]{:S(2)}) copy-start(f32[5,8,16,256]{3,2,1,0:T(8,128)} %get-tuple-element.25.own) | copy-start | bytes 1966084
  35.2 115.1 %collective-permute-start.4 = (f32[5,15,8,256]{3,2,1,0:T(8,128)}, f32[5,15,8,256]{3,2,1,0:T(8,128)S(1)}, u32[]{:S(2)}, u32[]{:S(2)}) collective-permute-start(f32[5,15,8,256]{3,2,1,0:T(8,128)} %get-tuple-element.26), channel_id=1, source_target_pairs={{0,1},{1,2},{2,3},{3,4},{4,5},{5,6},{6,7},{7,8},{8,9},{9,10},{10,1... | collective-permute-start | bytes 1843208 | tf_op jit(solution)/shard_map/ppermute | solution.py:32
  42.2 108.9 %collective-permute-start.5 = (f32[5,15,8,256]{3,2,1,0:T(8,128)}, f32[5,15,8,256]{3,2,1,0:T(8,128)S(1)}, u32[]{:S(2)}, u32[]{:S(2)}) collective-permute-start(f32[5,15,8,256]{3,2,1,0:T(8,128)} %get-tuple-element.27), channel_id=1, source_target_pairs={{1,0},{2,1},{3,2},{4,3},{5,4},{6,5},{7,6},{8,7},{9,8},{10,9},{11,1... | collective-permute-start | bytes 1843208 | tf_op jit(solution)/shard_map/ppermute | solution.py:32
  44.1 42.8 %collective-permute-start.6 = (f32[8,16,256]{2,1,0:T(8,128)S(1)}, f32[8,16,256]{2,1,0:T(8,128)S(1)}, u32[]{:S(2)}, u32[]{:S(2)}) collective-permute-start(f32[8,16,256]{2,1,0:T(8,128)S(1)} %copy-done.11), channel_id=1, source_target_pairs={{0,1008},{16,992},{32,976},{48,960},{64,944},{80,928},{96,912},{11... | collective-permute-start | bytes 393224 | tf_op jit(solution)/shard_map/ppermute | solution.py:340
  86.9 57.3 %collective-permute-start.7 = (f32[8,16,256]{2,1,0:T(8,128)S(1)}, f32[8,16,256]{2,1,0:T(8,128)S(1)}, u32[]{:S(2)}, u32[]{:S(2)}) collective-permute-start(f32[8,16,256]{2,1,0:T(8,128)S(1)} %collective-permute-done.6.own), channel_id=1, source_target_pairs={{0,16},{16,32},{32,48},{48,64},{64,80},{80,96},{96,112},{112,128},... | collective-permute-start | bytes 393224 | tf_op jit(solution)/shard_map/ppermute | solution.py:32
  91.7 52.5 %collective-permute-start.8 = (f32[8,16,256]{2,1,0:T(8,128)S(1)}, f32[8,16,256]{2,1,0:T(8,128)}, u32[]{:S(2)}, u32[]{:S(2)}) collective-permute-start(f32[8,16,256]{2,1,0:T(8,128)S(1)} %collective-permute-done.6.own), channel_id=1, source_target_pairs={{16,0},{32,16},{48,32},{64,48},{80,64},{96,80},{112,96},{128,112},... | collective-permute-start | bytes 393224 | tf_op jit(solution)/shard_map/ppermute | solution.py:32
  93.0 6.3 %collective-permute-start.1 = (f32[8,256]{1,0:T(8,128)S(1)}, f32[8,256]{1,0:T(8,128)S(1)}, u32[]{:S(2)}, u32[]{:S(2)}) collective-permute-start(f32[8,256]{1,0:T(8,128)S(1)} %copy-done.13), channel_id=1, source_target_pairs={{0,1},{1,2},{2,3},{3,4},{4,5},{5,6},{6,7},{7,8},{8,9},{9,10},{10,1... | collective-permute-start | bytes 24584 | tf_op jit(solution)/shard_map/ppermute | solution.py:338
  99.3 7.2 %collective-permute-start = (f32[16,256]{1,0:T(8,128)S(1)}, f32[16,256]{1,0:T(8,128)S(1)}, u32[]{:S(2)}, u32[]{:S(2)}) collective-permute-start(f32[16,256]{1,0:T(8,128)S(1)} %copy-done.12), channel_id=1, source_target_pairs={{0,16},{16,32},{32,48},{48,64},{64,80},{80,96},{96,112},{112,128},... | collective-permute-start | bytes 49160 | tf_op jit(solution)/shard_map/ppermute | solution.py:337
  124.2 41.2 %all-to-all-start.1 = ((f32[32,1,128]{2,1,0:T(1,128)}), f32[32,1,128]{2,1,0:T(1,128)S(1)}, u32[]{:S(2)}, u32[]{:S(2)}) async-start(f32[32,1,128]{2,1,0:T(1,128)} %shard_map.88), calls=%async_computation.1 | async-start | bytes 32768 | tf_op jit(solution)/shard_map/all_to_all | solution.py:345
  145.2 14.6 %collective-permute-start.9 = (f32[15,8,256]{2,1,0:T(8,128)S(1)}, f32[15,8,256]{2,1,0:T(8,128)S(1)}, u32[]{:S(2)}, u32[]{:S(2)}) collective-permute-start(f32[15,8,256]{2,1,0:T(8,128)S(1)} %get-tuple-element.30), channel_id=1, source_target_pairs={{0,1},{1,2},{2,3},{3,4},{4,5},{5,6},{6,7},{7,8},{8,9},{9,10},{10,1... | collective-permute-start | bytes 368648 | tf_op jit(solution)/shard_map/ppermute | solution.py:32
  148.3 11.4 %collective-permute-start.10 = (f32[15,8,256]{2,1,0:T(8,128)S(1)}, f32[15,8,256]{2,1,0:T(8,128)S(1)}, u32[]{:S(2)}, u32[]{:S(2)}) collective-permute-start(f32[15,8,256]{2,1,0:T(8,128)S(1)} %get-tuple-element.31), channel_id=1, source_target_pairs={{1,0},{2,1},{3,2},{4,3},{5,4},{6,5},{7,6},{8,7},{9,8},{10,9},{11,1... | collective-permute-start | bytes 368648 | tf_op jit(solution)/shard_map/ppermute | solution.py:32
  150.3 0.8 copy-start.2
  151.1 0.9 copy-start.4
  152.0 1.1 copy-start.3
  153.0 1.1 copy-start.5
  159.8 5.7 %copy-start.9 = (f32[2]{0:T(128)S(1)}, f32[2]{0:T(128)}, u32[]{:S(2)}) copy-start(f32[2]{0:T(128)} %low.1) | copy-start | bytes 28
  159.8 5.6 %copy-start.10 = (f32[2]{0:T(128)S(1)}, f32[2]{0:T(128)}, u32[]{:S(2)}) copy-start(f32[2]{0:T(128)} %high.1) | copy-start | bytes 28

commit v5 on v4

--- a/solution.py
+++ b/solution.py
@@ -174,7 +174,7 @@
     basis(first, second, d, cx, cy, ly, cz, lz, out)
 
 
-def pack_kernel(shift, cx, cy, cz, right_side, own, plane_x, plane_y, most, base_x, base_y, sems):
+def pack_kernel(shift, cx, cy, cz, right_side, own, plane_x, plane_y, base, sems):
     copies = [pltpu.make_async_copy(a, own.at[n], sems.at[n]) for n, a in enumerate((shift, cx, cy, cz, right_side))]
     for copy in copies:
         copy.start()
@@ -195,12 +195,12 @@
         y = y + jnp.where(line == 0, 0.0, pltpu.roll(y, 1, 0))
         z = z + jnp.where(lane == 0, 0.0, pltpu.roll(z, 1, 1))
         row = own[0, r] + 2.0 * (x + y + z)
-        base_y[r : r + 1, :] = row[0:1, :]
+        base[2 * BY + r : 2 * BY + r + 1, :] = row[0:1, :]
         if r:
             whole = jnp.maximum(whole, jnp.where(line == 0, 0.0, row))
         else:
-            base_x[...] = row
-    most[...] = whole
+            base[BY : 2 * BY, :] = row
+    base[0:BY, :] = whole
     copies[4].wait()
 
 
@@ -230,12 +230,12 @@
     edges(lambda r, y: (x_low, own, x_high)[r // BX][BX - 1 - r % BX, y : y + H, :], first_lines, last_lines)
 
 
-def bound_kernel(most, base_x, base_y, before_x, before_y, out):
+def bound_kernel(base, before_x, before_y, out):
     line = lax.broadcasted_iota(jnp.int32, (BY, NZ), 0)
     row = lax.broadcasted_iota(jnp.int32, (BX, NZ), 0)
     corner = jnp.where(line == 0, before_y[0:1, :], 0.0)
-    largest = jnp.maximum(most[...], base_x[...] + 2.0 * (before_x[...] + corner))
-    first = jnp.where(row == 0, 0.0, base_y[...] + 2.0 * before_y[...])
+    largest = jnp.maximum(base[0:BY, :], base[BY : 2 * BY, :] + 2.0 * (before_x[...] + corner))
+    first = jnp.where(row == 0, 0.0, base[2 * BY :, :] + 2.0 * before_y[...])
     largest = jnp.maximum(jnp.max(largest, axis=0, keepdims=True), jnp.max(first, axis=0, keepdims=True))
     largest = jnp.max(largest, axis=1, keepdims=True)
     out[...] = jnp.broadcast_to(largest[None], out.shape)
@@ -323,12 +323,12 @@
 def shards(right_side, shift, coef_x, coef_y, coef_z, low_frac, high_frac):
     nx, ny = lax.axis_size(GX), lax.axis_size(GY)
     up_x, up_y = shift_pairs(nx)[0], shift_pairs(ny)[0]
-    near = lax.axis_size(NEAR)
     given = (shift, coef_x, coef_y, coef_z, right_side)
 
-    own, plane_x, plane_y, most, base_x, base_y = kernel(
+    mirror = lax.ppermute(right_side, GX, [(i, nx - 1 - i) for i in range(nx)])
+    own, plane_x, plane_y, base = kernel(
         pack_kernel,
-        (f32(5, BX, BY, NZ), f32(BY, NZ), f32(BX, NZ), f32(BY, NZ), f32(BY, NZ), f32(BX, NZ)),
+        (f32(5, BX, BY, NZ), f32(BY, NZ), f32(BX, NZ), f32(2 * BY + BX, NZ)),
         given,
         scratch=[pltpu.SemaphoreType.DMA((5,))],
         anywhere=5,
@@ -337,12 +337,12 @@
     before_x = lax.ppermute(plane_x, GX, up_x)
     before_y = lax.ppermute(plane_y, GY, up_y)
     x_low, x_high = both_ways(own, own, GX)
-    mirror = lax.ppermute(right_side, GX, [(i, nx - 1 - i) for i in range(nx)])
-
-    most = kernel(bound_kernel, f32(near, 1, 128), (most, base_x, base_y, before_x, before_y), mib=2)
-    most = lax.all_to_all(most, NEAR, 0, 0, tiled=True)
-    most = kernel(spread_kernel, f32(lax.axis_size("gx_0"), 1, 128), (most,), mib=2)
-    bounds = lax.all_to_all(most, "gx_0", 0, 0, tiled=True)
+
+    chips_z, near = lax.axis_size("gx_0"), lax.axis_size(NEAR)
+    most = kernel(bound_kernel, f32(chips_z, 1, 128), (base, before_x, before_y), mib=2)
+    most = lax.all_to_all(most, "gx_0", 0, 0, tiled=True)
+    most = kernel(spread_kernel, f32(near, 1, 128), (most,), mib=2)
+    bounds = lax.all_to_all(most, NEAR, 0, 0, tiled=True)
 
     edge = f32(5, EDGE, H, NZ)
     first_lines, last_lines = kernel(

time: 168 us -> 176 us (1.048)
  blocking collectives: 16.9 us -> 0 us
  starting transfers between devices: 79.5 us -> 93.7 us
  waiting for transfers between devices: 48.9 us -> 58.7 us
    all_to_all x1 -> x0, blocking collectives: 16.9 us -> none  [shards(): most = lax.all_to_all(most, NEAR, 0, 0, tiled=True)]
    all_to_all x1 -> x2, starting transfers between devices: 20.1 us -> 31.7 us  [the longest x1 22.4 us: shards(): most = lax.all_to_all(most, 'gx_0', 0, 0, tiled=True)]
    all_to_all x1 -> x2, waiting for transfers between devices: 2.16 us -> 12 us  [the longest x1 12 us: shards(): most = lax.all_to_all(most, 'gx_0', 0, 0, tiled=True)]
    ppermute x4, starting transfers between devices: 20.4 us -> 22.9 us  [both_ways(): lax.ppermute(array_up, axes, up)]
    unnamed x28 -> x24, local copies, waits for them, and re-layouts: 4.97 us -> 4.91 us
  transfers between devices with their start and end apart: 12 -> 13, of which waited for: 5 -> 5; matrix products, arithmetic and copies ran while one was open for 0% -> 0% of each run, Pallas kernels for 6% -> 7%
where the time goes in v5:
time: 176 us
  starting transfers between devices  93.7 us (53%)
  waiting for transfers between devices  58.7 us (33%)
  Pallas kernels  17.5 us (10%)
  local copies, waits for them, and re-layouts  4.91 us (3%)
    ppermute x4, waiting for transfers between devices, both_ways(): lax.ppermute(array_up, axes, up)  23.1 us
    ppermute x4, starting transfers between devices, both_ways(): lax.ppermute(array_up, axes, up)  22.9 us
    all_to_all x1, starting transfers between devices, shards(): most = lax.all_to_all(most, 'gx_0', 0, 0, tiled=True)  22.4 us
    ppermute x1, waiting for transfers between devices, shards(): mirror = lax.ppermute(right_side, GX, [(i, nx - 1 - i) for i in range(nx)])  22 us
    ppermute x1, starting transfers between devices, shards(): mirror = lax.ppermute(right_side, GX, [(i, nx - 1 - i) for i in range(nx)])  20.7 us
    pallas_call x8, Pallas kernels, kernel(): pl.pallas_call(body, out_shape=out, in_specs=[SMEM] * smem + [ANY] * anyw...  17.5 us
    all_to_all x1, waiting for transfers between devices, shards(): most = lax.all_to_all(most, 'gx_0', 0, 0, tiled=True)  12 us
    all_to_all x1, starting transfers between devices, shards(): bounds = lax.all_to_all(most, NEAR, 0, 0, tiled=True)  9.33 us
  transfers between devices with their start and end apart: 13, of which 5 were waited for; matrix products, arithmetic and copies ran while one was open for 0% of the time, Pallas kernels for 7%

profile of v5, /device:TPU:1, one launch (start us, length us, event | category | flops | bytes accessed | tf_op | source)
XLA Modules:
  0.0 175.7 jit_solution(3365224654670264986)
XLA Ops:
  0.6 0.0 copy-start.9
  0.6 2.1 %shard_map.86 = (f32[5,8,16,256]{3,2,1,0:T(8,128)}, f32[16,256]{1,0:T(8,128)}, f32[8,256]{1,0:T(8,128)}, f32[40,256]{1,0:T(8,128)}) custom-call(f32[8,16,256]{2,1,0:T(8,128)} %shift.1, f32[8,16,256]{2,1,0:T(8,128)} %cx.1, f32[8,16,256]{2,1,0:T(8,128)} %cy.1, f32[8,16,256]{2,1,0:T(8,128)} %cz.1, f32[8,16,256]{2,1,0:T(8,128)} %right_side.1), custom_call_target="tpu_custom_call" | custom-call | flops 1000000 | bytes 655360 | tf_op jit(solution)/shard_map/pallas_call | solution.py:312
  2.8 5.5 %collective-permute-start.2 = (f32[5,8,16,256]{3,2,1,0:T(8,128)}, f32[5,8,16,256]{3,2,1,0:T(8,128)S(1)}, u32[]{:S(2)}, u32[]{:S(2)}) collective-permute-start(f32[5,8,16,256]{3,2,1,0:T(8,128)} %get-tuple-element.21.own), channel_id=1, source_target_pairs={{0,16},{16,32},{32,48},{48,64},{64,80},{80,96},{96,112},{112,128},... | collective-permute-start | bytes 1966088 | tf_op jit(solution)/shard_map/ppermute | solution.py:32
  8.3 1.3 collective-permute-start.3
  9.6 23.1 %collective-permute-done.2.x_low = f32[5,8,16,256]{3,2,1,0:T(8,128)S(1)} collective-permute-done((f32[5,8,16,256]{3,2,1,0:T(8,128)}, f32[5,8,16,256]{3,2,1,0:T(8,128)S(1)}, u32[]{:S(2)}, u32[]{:S(2)}) %collective-permute-start.2) | collective-permute-done | bytes 655392 | tf_op jit(solution)/shard_map/ppermute | solution.py:32
  32.6 0.0 collective-permute-done.3.x_high
  32.7 0.0 copy-start
  32.7 1.1 copy-done
  33.7 0.0 copy-start.11
  33.7 0.0 copy-start.10
  33.7 0.0 copy-start.6
  33.7 0.0 copy-start.1
  33.8 1.4 shard_map.89
  35.1 7.0 %collective-permute-start.4 = (f32[5,15,8,256]{3,2,1,0:T(8,128)}, f32[5,15,8,256]{3,2,1,0:T(8,128)S(1)}, u32[]{:S(2)}, u32[]{:S(2)}) collective-permute-start(f32[5,15,8,256]{3,2,1,0:T(8,128)} %get-tuple-element.22), channel_id=1, source_target_pairs={{0,1},{1,2},{2,3},{3,4},{4,5},{5,6},{6,7},{7,8},{8,9},{9,10},{10,1... | collective-permute-start | bytes 1843208 | tf_op jit(solution)/shard_map/ppermute | solution.py:32
  42.1 1.9 %collective-permute-start.5 = (f32[5,15,8,256]{3,2,1,0:T(8,128)}, f32[5,15,8,256]{3,2,1,0:T(8,128)S(1)}, u32[]{:S(2)}, u32[]{:S(2)}) collective-permute-start(f32[5,15,8,256]{3,2,1,0:T(8,128)} %get-tuple-element.23), channel_id=1, source_target_pairs={{1,0},{2,1},{3,2},{4,3},{5,4},{6,5},{7,6},{8,7},{9,8},{10,9},{11,1... | collective-permute-start | bytes 1843208 | tf_op jit(solution)/shard_map/ppermute | solution.py:32
  44.0 0.0 copy-done.9
  44.1 20.7 %collective-permute-start.6 = (f32[8,16,256]{2,1,0:T(8,128)S(1)}, f32[8,16,256]{2,1,0:T(8,128)S(1)}, u32[]{:S(2)}, u32[]{:S(2)}) collective-permute-start(f32[8,16,256]{2,1,0:T(8,128)S(1)} %copy-done.9), channel_id=1, source_target_pairs={{0,1008},{16,992},{32,976},{48,960},{64,944},{80,928},{96,912},{11... | collective-permute-start | bytes 393224 | tf_op jit(solution)/shard_map/ppermute | solution.py:328
  64.8 22.0 %collective-permute-done.6.own = f32[8,16,256]{2,1,0:T(8,128)S(1)} collective-permute-done((f32[8,16,256]{2,1,0:T(8,128)S(1)}, f32[8,16,256]{2,1,0:T(8,128)S(1)}, u32[]{:S(2)}, u32[]{:S(2)}) %collective-permute-start.6) | collective-permute-done | bytes 131104 | tf_op jit(solution)/shard_map/ppermute | solution.py:328
  86.8 4.8 %collective-permute-start.7 = (f32[8,16,256]{2,1,0:T(8,128)S(1)}, f32[8,16,256]{2,1,0:T(8,128)S(1)}, u32[]{:S(2)}, u32[]{:S(2)}) collective-permute-start(f32[8,16,256]{2,1,0:T(8,128)S(1)} %collective-permute-done.6.own), channel_id=1, source_target_pairs={{0,16},{16,32},{32,48},{48,64},{64,80},{80,96},{96,112},{112,128},... | collective-permute-start | bytes 393224 | tf_op jit(solution)/shard_map/ppermute | solution.py:32
  91.6 1.3 collective-permute-start.8
  92.9 0.0 copy-done.11
  92.9 5.5 %collective-permute-start.1 = (f32[8,256]{1,0:T(8,128)S(1)}, f32[8,256]{1,0:T(8,128)S(1)}, u32[]{:S(2)}, u32[]{:S(2)}) collective-permute-start(f32[8,256]{1,0:T(8,128)S(1)} %copy-done.11), channel_id=1, source_target_pairs={{0,1},{1,2},{2,3},{3,4},{4,5},{5,6},{6,7},{7,8},{8,9},{9,10},{10,1... | collective-permute-start | bytes 24584 | tf_op jit(solution)/shard_map/ppermute | solution.py:338
  98.5 0.8 collective-permute-done.1.before_y
  99.2 0.0 copy-done.10
  99.2 6.4 %collective-permute-start = (f32[16,256]{1,0:T(8,128)S(1)}, f32[16,256]{1,0:T(8,128)S(1)}, u32[]{:S(2)}, u32[]{:S(2)}) collective-permute-start(f32[16,256]{1,0:T(8,128)S(1)} %copy-done.10), channel_id=1, source_target_pairs={{0,16},{16,32},{32,48},{48,64},{64,80},{80,96},{96,112},{112,128},... | collective-permute-start | bytes 49160 | tf_op jit(solution)/shard_map/ppermute | solution.py:337
  105.6 0.9 collective-permute-done.before_x
  106.5 0.0 copy-done.6
  106.5 0.7 shard_map.87
  107.2 22.4 %all-to-all-start = ((f32[32,1,128]{2,1,0:T(1,128)}), f32[32,1,128]{2,1,0:T(1,128)S(1)}, u32[]{:S(2)}, u32[]{:S(2)}) async-start(f32[32,1,128]{2,1,0:T(1,128)} %shard_map.87), calls=%async_computation | async-start | bytes 32768 | tf_op jit(solution)/shard_map/all_to_all | solution.py:343
  129.6 0.0 collective-permute-done.7.x_low
  129.6 0.0 collective-permute-done.8.x_high
  129.6 1.6 shard_map.91
  131.2 5.6 %collective-permute-start.9 = (f32[15,8,256]{2,1,0:T(8,128)}, f32[15,8,256]{2,1,0:T(8,128)}, u32[]{:S(2)}, u32[]{:S(2)}) collective-permute-start(f32[15,8,256]{2,1,0:T(8,128)} %get-tuple-element.26), channel_id=1, source_target_pairs={{0,1},{1,2},{2,3},{3,4},{4,5},{5,6},{6,7},{7,8},{8,9},{9,10},{10,1... | collective-permute-start | bytes 368648 | tf_op jit(solution)/shard_map/ppermute | solution.py:32
  136.8 1.9 %collective-permute-start.10 = (f32[15,8,256]{2,1,0:T(8,128)}, f32[15,8,256]{2,1,0:T(8,128)}, u32[]{:S(2)}, u32[]{:S(2)}) collective-permute-start(f32[15,8,256]{2,1,0:T(8,128)} %get-tuple-element.27), channel_id=1, source_target_pairs={{1,0},{2,1},{3,2},{4,3},{5,4},{6,5},{7,6},{8,7},{9,8},{10,9},{11,1... | collective-permute-start | bytes 368648 | tf_op jit(solution)/shard_map/ppermute | solution.py:32
  138.8 12.0 %all-to-all-done.values = f32[32,1,128]{2,1,0:T(1,128)S(1)} async-done(((f32[32,1,128]{2,1,0:T(1,128)}), f32[32,1,128]{2,1,0:T(1,128)S(1)}, u32[]{:S(2)}, u32[]{:S(2)}) %all-to-all-start) | async-done | bytes 16416 | tf_op jit(solution)/shard_map/all_to_all | solution.py:343
  150.7 0.6 shard_map.88
  151.4 9.3 %all-to-all-start.1 = ((f32[32,1,128]{2,1,0:T(1,128)}), f32[32,1,128]{2,1,0:T(1,128)S(1)}, u32[]{:S(2)}, u32[]{:S(2)}) async-start(f32[32,1,128]{2,1,0:T(1,128)} %shard_map.88), calls=%async_computation.1 | async-start | bytes 32768 | tf_op jit(solution)/shard_map/all_to_all | solution.py:345
  160.7 0.0 collective-permute-done.4.y_low
  160.7 0.0 copy-start.2
  160.7 0.8 copy-done.2
  161.6 0.0 collective-permute-done.5.y_high
  161.6 0.0 copy-start.4
  161.6 0.8 copy-done.4
  162.4 0.0 copy-done.1
  162.4 0.0 copy-start.3
  162.4 1.1 copy-done.3
  163.5 0.0 copy-start.5
  163.5 1.1 copy-done.5
  164.5 5.6 %shard_map.90 = (f32[24,2,48,128]{3,2,1,0:T(8,128)S(1)}, f32[24,2,48,128]{3,2,1,0:T(8,128)S(1)}, f32[24,2,48,128]{3,2,1,0:T(8,128)S(1)}, f32[24,2,48,128]{3,2,1,...) custom-call(f32[5,8,16,256]{3,2,1,0:T(8,128)S(1)} %copy-done.1, ...), custom_call_target="tpu_custom_call" | custom-call | flops 30000000 | bytes 3194880 | tf_op jit(solution)/shard_map/pallas_call | solution.py:312
  170.2 0.0 collective-permute-done.9.y_low
  170.2 0.0 collective-permute-done.10.y_high
  170.2 0.0 copy-start.7
  170.2 0.0 copy-start.8
  170.2 3.6 %shard_map.92.mirrored = f32[9,8,2,16,128]{4,3,2,1,0:T(8,128)S(1)} custom-call(f32[8,16,256]{2,1,0:T(8,128)S(1)} %collective-permute-done.6.own, f32[8,16,256]{2,1,0:T(8,128)S(1)} %collective-permute-done.7.x_low, f32[8,16,256]{2,1,0:T(8,128)} %collective-permute-done.8.x_high, f32[15,8,256]{2,1,0:T(8,128)} %collective-permute-done.9.y_low, ...), custom_call_target="tpu_custom_call" | custom-call | flops 20000000 | bytes 7716864 | tf_op jit(solution)/shard_map/pallas_call | solution.py:312
  173.8 0.0 all-to-all-done.1.bounds
  173.8 0.0 copy-done.7
  173.8 0.0 copy-done.8
  173.8 1.9 %shard_map.93 = (f32[8,16,256]{2,1,0:T(8,128)}, f32[8,16,256]{2,1,0:T(8,128)}) custom-call(f32[2]{0:T(128)S(1)} %copy-done.7, f32[2]{0:T(128)S(1)} %copy-done.8, f32[32,1,128]{2,1,0:T(1,128)S(1)} %all-to-all-done.1.bounds, f32[8,128]{1,0:T(8,128)S(1)} %get-tuple-element.24.top, f32[9,8,2,16,128]{4,3,2,1,0:T(8,128)S(1)} %get-tuple-element.25.plain, ...), custom_call_target="tpu_custom_call" | custom-call | flops 3000000 | bytes 2379792 | tf_op jit(solution)/shard_map/pallas_call | solution.py:312
Async XLA Ops:
  0.6 43.4 %copy-start.9 = (f32[8,16,256]{2,1,0:T(8,128)S(1)}, f32[8,16,256]{2,1,0:T(8,128)}, u32[]{:S(2)}) copy-start(f32[8,16,256]{2,1,0:T(8,128)} %right_side.1) | copy-start | bytes 393220
  2.8 29.9 %collective-permute-start.2 = (f32[5,8,16,256]{3,2,1,0:T(8,128)}, f32[5,8,16,256]{3,2,1,0:T(8,128)S(1)}, u32[]{:S(2)}, u32[]{:S(2)}) collective-permute-start(f32[5,8,16,256]{3,2,1,0:T(8,128)} %get-tuple-element.21.own), channel_id=1, source_target_pairs={{0,16},{16,32},{32,48},{48,64},{64,80},{80,96},{96,112},{112,128},... | collective-permute-start | bytes 1966088 | tf_op jit(solution)/shard_map/ppermute | solution.py:32
  8.3 24.4 %collective-permute-start.3 = (f32[5,8,16,256]{3,2,1,0:T(8,128)}, f32[5,8,16,256]{3,2,1,0:T(8,128)S(1)}, u32[]{:S(2)}, u32[]{:S(2)}) collective-permute-start(f32[5,8,16,256]{3,2,1,0:T(8,128)} %get-tuple-element.21.own), channel_id=1, source_target_pairs={{16,0},{32,16},{48,32},{64,48},{80,64},{96,80},{112,96},{128,112},... | collective-permute-start | bytes 1966088 | tf_op jit(solution)/shard_map/ppermute | solution.py:32
  32.7 1.1 copy-start
  33.7 59.2 %copy-start.11 = (f32[8,256]{1,0:T(8,128)S(1)}, f32[8,256]{1,0:T(8,128)}, u32[]{:S(2)}) copy-start(f32[8,256]{1,0:T(8,128)} %get-tuple-element.20) | copy-start | bytes 24580
  33.7 65.5 %copy-start.10 = (f32[16,256]{1,0:T(8,128)S(1)}, f32[16,256]{1,0:T(8,128)}, u32[]{:S(2)}) copy-start(f32[16,256]{1,0:T(8,128)} %get-tuple-element.19) | copy-start | bytes 49156
  33.7 72.7 %copy-start.6 = (f32[40,256]{1,0:T(8,128)S(1)}, f32[40,256]{1,0:T(8,128)}, u32[]{:S(2)}) copy-start(f32[40,256]{1,0:T(8,128)} %get-tuple-element.18.base) | copy-start | bytes 122884
  33.7 128.6 %copy-start.1 = (f32[5,8,16,256]{3,2,1,0:T(8,128)S(1)}, f32[5,8,16,256]{3,2,1,0:T(8,128)}, u32[]{:S(2)}) copy-start(f32[5,8,16,256]{3,2,1,0:T(8,128)} %get-tuple-element.21.own) | copy-start | bytes 1966084
  35.1 125.6 %collective-permute-start.4 = (f32[5,15,8,256]{3,2,1,0:T(8,128)}, f32[5,15,8,256]{3,2,1,0:T(8,128)S(1)}, u32[]{:S(2)}, u32[]{:S(2)}) collective-permute-start(f32[5,15,8,256]{3,2,1,0:T(8,128)} %get-tuple-element.22), channel_id=1, source_target_pairs={{0,1},{1,2},{2,3},{3,4},{4,5},{5,6},{6,7},{7,8},{8,9},{9,10},{10,1... | collective-permute-start | bytes 1843208 | tf_op jit(solution)/shard_map/ppermute | solution.py:32
  42.1 119.4 %collective-permute-start.5 = (f32[5,15,8,256]{3,2,1,0:T(8,128)}, f32[5,15,8,256]{3,2,1,0:T(8,128)S(1)}, u32[]{:S(2)}, u32[]{:S(2)}) collective-permute-start(f32[5,15,8,256]{3,2,1,0:T(8,128)} %get-tuple-element.23), channel_id=1, source_target_pairs={{1,0},{2,1},{3,2},{4,3},{5,4},{6,5},{7,6},{8,7},{9,8},{10,9},{11,1... | collective-permute-start | bytes 1843208 | tf_op jit(solution)/shard_map/ppermute | solution.py:32
  44.1 42.8 %collective-permute-start.6 = (f32[8,16,256]{2,1,0:T(8,128)S(1)}, f32[8,16,256]{2,1,0:T(8,128)S(1)}, u32[]{:S(2)}, u32[]{:S(2)}) collective-permute-start(f32[8,16,256]{2,1,0:T(8,128)S(1)} %copy-done.9), channel_id=1, source_target_pairs={{0,1008},{16,992},{32,976},{48,960},{64,944},{80,928},{96,912},{11... | collective-permute-start | bytes 393224 | tf_op jit(solution)/shard_map/ppermute | solution.py:328
  86.8 42.8 %collective-permute-start.7 = (f32[8,16,256]{2,1,0:T(8,128)S(1)}, f32[8,16,256]{2,1,0:T(8,128)S(1)}, u32[]{:S(2)}, u32[]{:S(2)}) collective-permute-start(f32[8,16,256]{2,1,0:T(8,128)S(1)} %collective-permute-done.6.own), channel_id=1, source_target_pairs={{0,16},{16,32},{32,48},{48,64},{64,80},{80,96},{96,112},{112,128},... | collective-permute-start | bytes 393224 | tf_op jit(solution)/shard_map/ppermute | solution.py:32
  91.6 38.0 %collective-permute-start.8 = (f32[8,16,256]{2,1,0:T(8,128)S(1)}, f32[8,16,256]{2,1,0:T(8,128)}, u32[]{:S(2)}, u32[]{:S(2)}) collective-permute-start(f32[8,16,256]{2,1,0:T(8,128)S(1)} %collective-permute-done.6.own), channel_id=1, source_target_pairs={{16,0},{32,16},{48,32},{64,48},{80,64},{96,80},{112,96},{128,112},... | collective-permute-start | bytes 393224 | tf_op jit(solution)/shard_map/ppermute | solution.py:32
  92.9 6.3 %collective-permute-start.1 = (f32[8,256]{1,0:T(8,128)S(1)}, f32[8,256]{1,0:T(8,128)S(1)}, u32[]{:S(2)}, u32[]{:S(2)}) collective-permute-start(f32[8,256]{1,0:T(8,128)S(1)} %copy-done.11), channel_id=1, source_target_pairs={{0,1},{1,2},{2,3},{3,4},{4,5},{5,6},{6,7},{7,8},{8,9},{9,10},{10,1... | collective-permute-start | bytes 24584 | tf_op jit(solution)/shard_map/ppermute | solution.py:338
  99.2 7.2 %collective-permute-start = (f32[16,256]{1,0:T(8,128)S(1)}, f32[16,256]{1,0:T(8,128)S(1)}, u32[]{:S(2)}, u32[]{:S(2)}) collective-permute-start(f32[16,256]{1,0:T(8,128)S(1)} %copy-done.10), channel_id=1, source_target_pairs={{0,16},{16,32},{32,48},{48,64},{64,80},{80,96},{96,112},{112,128},... | collective-permute-start | bytes 49160 | tf_op jit(solution)/shard_map/ppermute | solution.py:337
  107.2 43.6 %all-to-all-start = ((f32[32,1,128]{2,1,0:T(1,128)}), f32[32,1,128]{2,1,0:T(1,128)S(1)}, u32[]{:S(2)}, u32[]{:S(2)}) async-start(f32[32,1,128]{2,1,0:T(1,128)} %shard_map.87), calls=%async_computation | async-start | bytes 32768 | tf_op jit(solution)/shard_map/all_to_all | solution.py:343
  131.2 39.0 %collective-permute-start.9 = (f32[15,8,256]{2,1,0:T(8,128)}, f32[15,8,256]{2,1,0:T(8,128)}, u32[]{:S(2)}, u32[]{:S(2)}) collective-permute-start(f32[15,8,256]{2,1,0:T(8,128)} %get-tuple-element.26), channel_id=1, source_target_pairs={{0,1},{1,2},{2,3},{3,4},{4,5},{5,6},{6,7},{7,8},{8,9},{9,10},{10,1... | collective-permute-start | bytes 368648 | tf_op jit(solution)/shard_map/ppermute | solution.py:32
  136.8 33.3 %collective-permute-start.10 = (f32[15,8,256]{2,1,0:T(8,128)}, f32[15,8,256]{2,1,0:T(8,128)}, u32[]{:S(2)}, u32[]{:S(2)}) collective-permute-start(f32[15,8,256]{2,1,0:T(8,128)} %get-tuple-element.27), channel_id=1, source_target_pairs={{1,0},{2,1},{3,2},{4,3},{5,4},{6,5},{7,6},{8,7},{9,8},{10,9},{11,1... | collective-permute-start | bytes 368648 | tf_op jit(solution)/shard_map/ppermute | solution.py:32
  151.4 22.4 %all-to-all-start.1 = ((f32[32,1,128]{2,1,0:T(1,128)}), f32[32,1,128]{2,1,0:T(1,128)S(1)}, u32[]{:S(2)}, u32[]{:S(2)}) async-start(f32[32,1,128]{2,1,0:T(1,128)} %shard_map.88), calls=%async_computation.1 | async-start | bytes 32768 | tf_op jit(solution)/shard_map/all_to_all | solution.py:345
  160.7 0.8 copy-start.2
  161.6 0.8 copy-start.4
  162.4 1.1 copy-start.3
  163.5 1.1 copy-start.5
  170.2 3.6 %copy-start.7 = (f32[2]{0:T(128)S(1)}, f32[2]{0:T(128)}, u32[]{:S(2)}) copy-start(f32[2]{0:T(128)} %low.1) | copy-start | bytes 28
  170.2 3.6 %copy-start.8 = (f32[2]{0:T(128)S(1)}, f32[2]{0:T(128)}, u32[]{:S(2)}) copy-start(f32[2]{0:T(128)} %high.1) | copy-start | bytes 28

commit v6 on v5

--- a/solution.py
+++ b/solution.py
@@ -339,10 +339,10 @@
     x_low, x_high = both_ways(own, own, GX)
 
     chips_z, near = lax.axis_size("gx_0"), lax.axis_size(NEAR)
-    most = kernel(bound_kernel, f32(chips_z, 1, 128), (base, before_x, before_y), mib=2)
-    most = lax.all_to_all(most, "gx_0", 0, 0, tiled=True)
-    most = kernel(spread_kernel, f32(near, 1, 128), (most,), mib=2)
-    bounds = lax.all_to_all(most, NEAR, 0, 0, tiled=True)
+    most = kernel(bound_kernel, f32(near, 1, 128), (base, before_x, before_y), mib=2)
+    most = lax.all_to_all(most, NEAR, 0, 0, tiled=True)
+    most = kernel(spread_kernel, f32(chips_z, 1, 128), (most,), mib=2)
+    bounds = lax.all_to_all(most, "gx_0", 0, 0, tiled=True)
 
     edge = f32(5, EDGE, H, NZ)
     first_lines, last_lines = kernel(

time: 176 us -> 168 us (0.955)
  blocking collectives: 0 us -> 16.9 us
  starting transfers between devices: 93.7 us -> 79.5 us
  waiting for transfers between devices: 58.7 us -> 48.9 us
    all_to_all x0 -> x1, blocking collectives: none -> 16.9 us  [shards(): most = lax.all_to_all(most, NEAR, 0, 0, tiled=True)]
    all_to_all x2 -> x1, starting transfers between devices: 31.7 us -> 20.1 us  [shards(): bounds = lax.all_to_all(most, 'gx_0', 0, 0, tiled=True)]
    all_to_all x2 -> x1, waiting for transfers between devices: 12 us -> 2.16 us  [shards(): bounds = lax.all_to_all(most, 'gx_0', 0, 0, tiled=True)]
    ppermute x4, starting transfers between devices: 22.9 us -> 20.4 us  [both_ways(): lax.ppermute(array_up, axes, up)]
  transfers between devices with their start and end apart: 13 -> 12, of which waited for: 5 -> 5; matrix products, arithmetic and copies ran while one was open for 0% -> 0% of each run, Pallas kernels for 7% -> 6%
where the time goes in v6:
time: 168 us; the launch traced here: 167 us
  starting transfers between devices  79.5 us (47%)
  waiting for transfers between devices  48.9 us (29%)
  blocking collectives  16.9 us (10%)
  Pallas kernels  16.1 us (10%)
  local copies, waits for them, and re-layouts  4.96 us (3%)
    ppermute x4, waiting for transfers between devices, both_ways(): lax.ppermute(array_up, axes, up)  23.1 us
    ppermute x1, waiting for transfers between devices, shards(): mirror = lax.ppermute(right_side, GX, [(i, nx - 1 - i) for i in range(nx)])  22 us
    ppermute x1, starting transfers between devices, shards(): mirror = lax.ppermute(right_side, GX, [(i, nx - 1 - i) for i in range(nx)])  20.7 us
    ppermute x4, starting transfers between devices, both_ways(): lax.ppermute(array_up, axes, up)  20.4 us
    all_to_all x1, starting transfers between devices, shards(): bounds = lax.all_to_all(most, 'gx_0', 0, 0, tiled=True)  20.1 us
    all_to_all x1, blocking collectives, shards(): most = lax.all_to_all(most, NEAR, 0, 0, tiled=True)  16.9 us
    pallas_call x8, Pallas kernels, kernel(): pl.pallas_call(body, out_shape=out, in_specs=[SMEM] * smem + [ANY] * anyw...  16.1 us
    ppermute x4, starting transfers between devices, both_ways(): lax.ppermute(array_down, axes, down)  6.42 us
  transfers between devices with their start and end apart: 12, of which 5 were waited for; matrix products, arithmetic and copies ran while one was open for 0% of the time, Pallas kernels for 6%

profile of v6, /device:TPU:1, one launch (start us, length us, event | category | flops | bytes accessed | tf_op | source)
XLA Modules:
  0.0 167.2 jit_solution(10044115877490825088)
XLA Ops:
  0.6 0.0 copy-start.9
  0.6 2.1 %shard_map.86 = (f32[5,8,16,256]{3,2,1,0:T(8,128)}, f32[16,256]{1,0:T(8,128)}, f32[8,256]{1,0:T(8,128)}, f32[40,256]{1,0:T(8,128)}) custom-call(f32[8,16,256]{2,1,0:T(8,128)} %shift.1, f32[8,16,256]{2,1,0:T(8,128)} %cx.1, f32[8,16,256]{2,1,0:T(8,128)} %cy.1, f32[8,16,256]{2,1,0:T(8,128)} %cz.1, f32[8,16,256]{2,1,0:T(8,128)} %right_side.1), custom_call_target="tpu_custom_call" | custom-call | flops 1000000 | bytes 655360 | tf_op jit(solution)/shard_map/pallas_call | solution.py:312
  2.8 5.5 %collective-permute-start.2 = (f32[5,8,16,256]{3,2,1,0:T(8,128)}, f32[5,8,16,256]{3,2,1,0:T(8,128)S(1)}, u32[]{:S(2)}, u32[]{:S(2)}) collective-permute-start(f32[5,8,16,256]{3,2,1,0:T(8,128)} %get-tuple-element.21.own), channel_id=1, source_target_pairs={{0,16},{16,32},{32,48},{48,64},{64,80},{80,96},{96,112},{112,128},... | collective-permute-start | bytes 1966088 | tf_op jit(solution)/shard_map/ppermute | solution.py:32
  8.3 1.3 collective-permute-start.3
  9.6 23.1 %collective-permute-done.2.x_low = f32[5,8,16,256]{3,2,1,0:T(8,128)S(1)} collective-permute-done((f32[5,8,16,256]{3,2,1,0:T(8,128)}, f32[5,8,16,256]{3,2,1,0:T(8,128)S(1)}, u32[]{:S(2)}, u32[]{:S(2)}) %collective-permute-start.2) | collective-permute-done | bytes 655392 | tf_op jit(solution)/shard_map/ppermute | solution.py:32
  32.7 0.0 collective-permute-done.3.x_high
  32.7 0.0 copy-start
  32.7 1.1 copy-done
  33.7 0.0 copy-start.11
  33.7 0.0 copy-start.10
  33.8 0.0 copy-start.6
  33.8 0.0 copy-start.1
  33.8 1.4 shard_map.89
  35.2 7.0 %collective-permute-start.4 = (f32[5,15,8,256]{3,2,1,0:T(8,128)}, f32[5,15,8,256]{3,2,1,0:T(8,128)S(1)}, u32[]{:S(2)}, u32[]{:S(2)}) collective-permute-start(f32[5,15,8,256]{3,2,1,0:T(8,128)} %get-tuple-element.22), channel_id=1, source_target_pairs={{0,1},{1,2},{2,3},{3,4},{4,5},{5,6},{6,7},{7,8},{8,9},{9,10},{10,1... | collective-permute-start | bytes 1843208 | tf_op jit(solution)/shard_map/ppermute | solution.py:32
  42.2 1.9 %collective-permute-start.5 = (f32[5,15,8,256]{3,2,1,0:T(8,128)}, f32[5,15,8,256]{3,2,1,0:T(8,128)S(1)}, u32[]{:S(2)}, u32[]{:S(2)}) collective-permute-start(f32[5,15,8,256]{3,2,1,0:T(8,128)} %get-tuple-element.23), channel_id=1, source_target_pairs={{1,0},{2,1},{3,2},{4,3},{5,4},{6,5},{7,6},{8,7},{9,8},{10,9},{11,1... | collective-permute-start | bytes 1843208 | tf_op jit(solution)/shard_map/ppermute | solution.py:32
  44.1 0.0 copy-done.9
  44.1 20.7 %collective-permute-start.6 = (f32[8,16,256]{2,1,0:T(8,128)S(1)}, f32[8,16,256]{2,1,0:T(8,128)S(1)}, u32[]{:S(2)}, u32[]{:S(2)}) collective-permute-start(f32[8,16,256]{2,1,0:T(8,128)S(1)} %copy-done.9), channel_id=1, source_target_pairs={{0,1008},{16,992},{32,976},{48,960},{64,944},{80,928},{96,912},{11... | collective-permute-start | bytes 393224 | tf_op jit(solution)/shard_map/ppermute | solution.py:328
  64.8 22.0 %collective-permute-done.6.own = f32[8,16,256]{2,1,0:T(8,128)S(1)} collective-permute-done((f32[8,16,256]{2,1,0:T(8,128)S(1)}, f32[8,16,256]{2,1,0:T(8,128)S(1)}, u32[]{:S(2)}, u32[]{:S(2)}) %collective-permute-start.6) | collective-permute-done | bytes 131104 | tf_op jit(solution)/shard_map/ppermute | solution.py:328
  86.9 4.8 %collective-permute-start.7 = (f32[8,16,256]{2,1,0:T(8,128)S(1)}, f32[8,16,256]{2,1,0:T(8,128)S(1)}, u32[]{:S(2)}, u32[]{:S(2)}) collective-permute-start(f32[8,16,256]{2,1,0:T(8,128)S(1)} %collective-permute-done.6.own), channel_id=1, source_target_pairs={{0,16},{16,32},{32,48},{48,64},{64,80},{80,96},{96,112},{112,128},... | collective-permute-start | bytes 393224 | tf_op jit(solution)/shard_map/ppermute | solution.py:32
  91.7 1.3 collective-permute-start.8
  93.0 0.0 copy-done.11
  93.0 5.5 %collective-permute-start.1 = (f32[8,256]{1,0:T(8,128)S(1)}, f32[8,256]{1,0:T(8,128)S(1)}, u32[]{:S(2)}, u32[]{:S(2)}) collective-permute-start(f32[8,256]{1,0:T(8,128)S(1)} %copy-done.11), channel_id=1, source_target_pairs={{0,1},{1,2},{2,3},{3,4},{4,5},{5,6},{6,7},{7,8},{8,9},{9,10},{10,1... | collective-permute-start | bytes 24584 | tf_op jit(solution)/shard_map/ppermute | solution.py:338
  98.5 0.8 collective-permute-done.1.before_y
  99.3 0.0 copy-done.10
  99.3 6.4 %collective-permute-start = (f32[16,256]{1,0:T(8,128)S(1)}, f32[16,256]{1,0:T(8,128)S(1)}, u32[]{:S(2)}, u32[]{:S(2)}) collective-permute-start(f32[16,256]{1,0:T(8,128)S(1)} %copy-done.10), channel_id=1, source_target_pairs={{0,16},{16,32},{32,48},{48,64},{64,80},{80,96},{96,112},{112,128},... | collective-permute-start | bytes 49160 | tf_op jit(solution)/shard_map/ppermute | solution.py:337
  105.7 0.9 collective-permute-done.before_x
  106.5 0.0 copy-done.6
  106.5 0.1 shard_map.87
  106.6 16.9 %all_to_all.10.values = f32[32,1,128]{2,1,0:T(1,128)S(1)} all-to-all(f32[32,1,128]{2,1,0:T(1,128)S(1)} %shard_map.87), channel_id=1, replica_groups=mesh['gx_0'=32,'gx_1'=2,'gy_0'=4,'gy_1'=2,'gy_2'=2] {'gx_1','gy_0','gy_1..., dimensions={0} | all-to-all | bytes 32768 | tf_op jit(solution)/shard_map/all_to_all | solution.py:343
  123.5 0.6 shard_map.88
  124.1 20.1 %all-to-all-start.1 = ((f32[32,1,128]{2,1,0:T(1,128)}), f32[32,1,128]{2,1,0:T(1,128)S(1)}, u32[]{:S(2)}, u32[]{:S(2)}) async-start(f32[32,1,128]{2,1,0:T(1,128)} %shard_map.88), calls=%async_computation.1 | async-start | bytes 32768 | tf_op jit(solution)/shard_map/all_to_all | solution.py:345
  144.2 0.0 collective-permute-done.7.x_low
  144.2 0.0 collective-permute-done.8.x_high
  144.2 0.9 shard_map.91
  145.1 3.1 %collective-permute-start.9 = (f32[15,8,256]{2,1,0:T(8,128)S(1)}, f32[15,8,256]{2,1,0:T(8,128)S(1)}, u32[]{:S(2)}, u32[]{:S(2)}) collective-permute-start(f32[15,8,256]{2,1,0:T(8,128)S(1)} %get-tuple-element.26), channel_id=1, source_target_pairs={{0,1},{1,2},{2,3},{3,4},{4,5},{5,6},{6,7},{7,8},{8,9},{9,10},{10,1... | collective-permute-start | bytes 368648 | tf_op jit(solution)/shard_map/ppermute | solution.py:32
  148.3 1.9 %collective-permute-start.10 = (f32[15,8,256]{2,1,0:T(8,128)S(1)}, f32[15,8,256]{2,1,0:T(8,128)S(1)}, u32[]{:S(2)}, u32[]{:S(2)}) collective-permute-start(f32[15,8,256]{2,1,0:T(8,128)S(1)} %get-tuple-element.27), channel_id=1, source_target_pairs={{1,0},{2,1},{3,2},{4,3},{5,4},{6,5},{7,6},{8,7},{9,8},{10,9},{11,1... | collective-permute-start | bytes 368648 | tf_op jit(solution)/shard_map/ppermute | solution.py:32
  150.2 0.0 collective-permute-done.4.y_low
  150.2 0.0 copy-start.2
  150.2 0.8 copy-done.2
  151.1 0.0 collective-permute-done.5.y_high
  151.1 0.0 copy-start.4
  151.1 0.8 copy-done.4
  151.9 0.0 copy-done.1
  151.9 0.0 copy-start.3
  151.9 1.1 copy-done.3
  153.0 0.0 copy-start.5
  153.0 1.1 copy-done.5
  154.1 5.6 %shard_map.90 = (f32[24,2,48,128]{3,2,1,0:T(8,128)S(1)}, f32[24,2,48,128]{3,2,1,0:T(8,128)S(1)}, f32[24,2,48,128]{3,2,1,0:T(8,128)S(1)}, f32[24,2,48,128]{3,2,1,...) custom-call(f32[5,8,16,256]{3,2,1,0:T(8,128)S(1)} %copy-done.1, ...), custom_call_target="tpu_custom_call" | custom-call | flops 30000000 | bytes 3194880 | tf_op jit(solution)/shard_map/pallas_call | solution.py:312
  159.7 0.0 collective-permute-done.9.y_low
  159.7 0.0 collective-permute-done.10.y_high
  159.7 0.0 copy-start.7
  159.7 0.0 copy-start.8
  159.7 3.5 %shard_map.92.mirrored = f32[9,8,2,16,128]{4,3,2,1,0:T(8,128)S(1)} custom-call(f32[8,16,256]{2,1,0:T(8,128)S(1)} %collective-permute-done.6.own, f32[8,16,256]{2,1,0:T(8,128)S(1)} %collective-permute-done.7.x_low, f32[8,16,256]{2,1,0:T(8,128)} %collective-permute-done.8.x_high, f32[15,8,256]{2,1,0:T(8,128)S(1)} %collective-permute-done.9.y_low, ...), custom_call_target="tpu_custom_call" | custom-call | flops 20000000 | bytes 7716864 | tf_op jit(solution)/shard_map/pallas_call | solution.py:312
  163.2 2.2 %all-to-all-done.1.bounds = f32[32,1,128]{2,1,0:T(1,128)S(1)} async-done(((f32[32,1,128]{2,1,0:T(1,128)}), f32[32,1,128]{2,1,0:T(1,128)S(1)}, u32[]{:S(2)}, u32[]{:S(2)}) %all-to-all-start.1) | async-done | bytes 16416 | tf_op jit(solution)/shard_map/all_to_all | solution.py:345
  165.4 0.0 copy-done.7
  165.4 0.0 copy-done.8
  165.4 1.9 %shard_map.93 = (f32[8,16,256]{2,1,0:T(8,128)}, f32[8,16,256]{2,1,0:T(8,128)}) custom-call(f32[2]{0:T(128)S(1)} %copy-done.7, f32[2]{0:T(128)S(1)} %copy-done.8, f32[32,1,128]{2,1,0:T(1,128)S(1)} %all-to-all-done.1.bounds, f32[8,128]{1,0:T(8,128)S(1)} %get-tuple-element.24.top, f32[9,8,2,16,128]{4,3,2,1,0:T(8,128)S(1)} %get-tuple-element.25.plain, ...), custom_call_target="tpu_custom_call" | custom-call | flops 3000000 | bytes 2379792 | tf_op jit(solution)/shard_map/pallas_call | solution.py:312
Async XLA Ops:
  0.6 43.5 %copy-start.9 = (f32[8,16,256]{2,1,0:T(8,128)S(1)}, f32[8,16,256]{2,1,0:T(8,128)}, u32[]{:S(2)}) copy-start(f32[8,16,256]{2,1,0:T(8,128)} %right_side.1) | copy-start | bytes 393220
  2.8 29.9 %collective-permute-start.2 = (f32[5,8,16,256]{3,2,1,0:T(8,128)}, f32[5,8,16,256]{3,2,1,0:T(8,128)S(1)}, u32[]{:S(2)}, u32[]{:S(2)}) collective-permute-start(f32[5,8,16,256]{3,2,1,0:T(8,128)} %get-tuple-element.21.own), channel_id=1, source_target_pairs={{0,16},{16,32},{32,48},{48,64},{64,80},{80,96},{96,112},{112,128},... | collective-permute-start | bytes 1966088 | tf_op jit(solution)/shard_map/ppermute | solution.py:32
  8.3 24.4 %collective-permute-start.3 = (f32[5,8,16,256]{3,2,1,0:T(8,128)}, f32[5,8,16,256]{3,2,1,0:T(8,128)S(1)}, u32[]{:S(2)}, u32[]{:S(2)}) collective-permute-start(f32[5,8,16,256]{3,2,1,0:T(8,128)} %get-tuple-element.21.own), channel_id=1, source_target_pairs={{16,0},{32,16},{48,32},{64,48},{80,64},{96,80},{112,96},{128,112},... | collective-permute-start | bytes 1966088 | tf_op jit(solution)/shard_map/ppermute | solution.py:32
  32.7 1.1 copy-start
  33.7 59.2 %copy-start.11 = (f32[8,256]{1,0:T(8,128)S(1)}, f32[8,256]{1,0:T(8,128)}, u32[]{:S(2)}) copy-start(f32[8,256]{1,0:T(8,128)} %get-tuple-element.20) | copy-start | bytes 24580
  33.7 65.5 %copy-start.10 = (f32[16,256]{1,0:T(8,128)S(1)}, f32[16,256]{1,0:T(8,128)}, u32[]{:S(2)}) copy-start(f32[16,256]{1,0:T(8,128)} %get-tuple-element.19) | copy-start | bytes 49156
  33.8 72.8 %copy-start.6 = (f32[40,256]{1,0:T(8,128)S(1)}, f32[40,256]{1,0:T(8,128)}, u32[]{:S(2)}) copy-start(f32[40,256]{1,0:T(8,128)} %get-tuple-element.18.base) | copy-start | bytes 122884
  33.8 118.2 %copy-start.1 = (f32[5,8,16,256]{3,2,1,0:T(8,128)S(1)}, f32[5,8,16,256]{3,2,1,0:T(8,128)}, u32[]{:S(2)}) copy-start(f32[5,8,16,256]{3,2,1,0:T(8,128)} %get-tuple-element.21.own) | copy-start | bytes 1966084
  35.2 115.1 %collective-permute-start.4 = (f32[5,15,8,256]{3,2,1,0:T(8,128)}, f32[5,15,8,256]{3,2,1,0:T(8,128)S(1)}, u32[]{:S(2)}, u32[]{:S(2)}) collective-permute-start(f32[5,15,8,256]{3,2,1,0:T(8,128)} %get-tuple-element.22), channel_id=1, source_target_pairs={{0,1},{1,2},{2,3},{3,4},{4,5},{5,6},{6,7},{7,8},{8,9},{9,10},{10,1... | collective-permute-start | bytes 1843208 | tf_op jit(solution)/shard_map/ppermute | solution.py:32
  42.2 108.9 %collective-permute-start.5 = (f32[5,15,8,256]{3,2,1,0:T(8,128)}, f32[5,15,8,256]{3,2,1,0:T(8,128)S(1)}, u32[]{:S(2)}, u32[]{:S(2)}) collective-permute-start(f32[5,15,8,256]{3,2,1,0:T(8,128)} %get-tuple-element.23), channel_id=1, source_target_pairs={{1,0},{2,1},{3,2},{4,3},{5,4},{6,5},{7,6},{8,7},{9,8},{10,9},{11,1... | collective-permute-start | bytes 1843208 | tf_op jit(solution)/shard_map/ppermute | solution.py:32
  44.1 42.8 %collective-permute-start.6 = (f32[8,16,256]{2,1,0:T(8,128)S(1)}, f32[8,16,256]{2,1,0:T(8,128)S(1)}, u32[]{:S(2)}, u32[]{:S(2)}) collective-permute-start(f32[8,16,256]{2,1,0:T(8,128)S(1)} %copy-done.9), channel_id=1, source_target_pairs={{0,1008},{16,992},{32,976},{48,960},{64,944},{80,928},{96,912},{11... | collective-permute-start | bytes 393224 | tf_op jit(solution)/shard_map/ppermute | solution.py:328
  86.9 57.3 %collective-permute-start.7 = (f32[8,16,256]{2,1,0:T(8,128)S(1)}, f32[8,16,256]{2,1,0:T(8,128)S(1)}, u32[]{:S(2)}, u32[]{:S(2)}) collective-permute-start(f32[8,16,256]{2,1,0:T(8,128)S(1)} %collective-permute-done.6.own), channel_id=1, source_target_pairs={{0,16},{16,32},{32,48},{48,64},{64,80},{80,96},{96,112},{112,128},... | collective-permute-start | bytes 393224 | tf_op jit(solution)/shard_map/ppermute | solution.py:32
  91.7 52.5 %collective-permute-start.8 = (f32[8,16,256]{2,1,0:T(8,128)S(1)}, f32[8,16,256]{2,1,0:T(8,128)}, u32[]{:S(2)}, u32[]{:S(2)}) collective-permute-start(f32[8,16,256]{2,1,0:T(8,128)S(1)} %collective-permute-done.6.own), channel_id=1, source_target_pairs={{16,0},{32,16},{48,32},{64,48},{80,64},{96,80},{112,96},{128,112},... | collective-permute-start | bytes 393224 | tf_op jit(solution)/shard_map/ppermute | solution.py:32
  93.0 6.3 %collective-permute-start.1 = (f32[8,256]{1,0:T(8,128)S(1)}, f32[8,256]{1,0:T(8,128)S(1)}, u32[]{:S(2)}, u32[]{:S(2)}) collective-permute-start(f32[8,256]{1,0:T(8,128)S(1)} %copy-done.11), channel_id=1, source_target_pairs={{0,1},{1,2},{2,3},{3,4},{4,5},{5,6},{6,7},{7,8},{8,9},{9,10},{10,1... | collective-permute-start | bytes 24584 | tf_op jit(solution)/shard_map/ppermute | solution.py:338
  99.3 7.2 %collective-permute-start = (f32[16,256]{1,0:T(8,128)S(1)}, f32[16,256]{1,0:T(8,128)S(1)}, u32[]{:S(2)}, u32[]{:S(2)}) collective-permute-start(f32[16,256]{1,0:T(8,128)S(1)} %copy-done.10), channel_id=1, source_target_pairs={{0,16},{16,32},{32,48},{48,64},{64,80},{80,96},{96,112},{112,128},... | collective-permute-start | bytes 49160 | tf_op jit(solution)/shard_map/ppermute | solution.py:337
  124.1 41.2 %all-to-all-start.1 = ((f32[32,1,128]{2,1,0:T(1,128)}), f32[32,1,128]{2,1,0:T(1,128)S(1)}, u32[]{:S(2)}, u32[]{:S(2)}) async-start(f32[32,1,128]{2,1,0:T(1,128)} %shard_map.88), calls=%async_computation.1 | async-start | bytes 32768 | tf_op jit(solution)/shard_map/all_to_all | solution.py:345
  145.1 14.6 %collective-permute-start.9 = (f32[15,8,256]{2,1,0:T(8,128)S(1)}, f32[15,8,256]{2,1,0:T(8,128)S(1)}, u32[]{:S(2)}, u32[]{:S(2)}) collective-permute-start(f32[15,8,256]{2,1,0:T(8,128)S(1)} %get-tuple-element.26), channel_id=1, source_target_pairs={{0,1},{1,2},{2,3},{3,4},{4,5},{5,6},{6,7},{7,8},{8,9},{9,10},{10,1... | collective-permute-start | bytes 368648 | tf_op jit(solution)/shard_map/ppermute | solution.py:32
  148.3 11.4 %collective-permute-start.10 = (f32[15,8,256]{2,1,0:T(8,128)S(1)}, f32[15,8,256]{2,1,0:T(8,128)S(1)}, u32[]{:S(2)}, u32[]{:S(2)}) collective-permute-start(f32[15,8,256]{2,1,0:T(8,128)S(1)} %get-tuple-element.27), channel_id=1, source_target_pairs={{1,0},{2,1},{3,2},{4,3},{5,4},{6,5},{7,6},{8,7},{9,8},{10,9},{11,1... | collective-permute-start | bytes 368648 | tf_op jit(solution)/shard_map/ppermute | solution.py:32
  150.2 0.9 copy-start.2
  151.1 0.8 copy-start.4
  151.9 1.1 copy-start.3
  153.0 1.1 copy-start.5
  159.7 5.7 %copy-start.7 = (f32[2]{0:T(128)S(1)}, f32[2]{0:T(128)}, u32[]{:S(2)}) copy-start(f32[2]{0:T(128)} %low.1) | copy-start | bytes 28
  159.7 5.6 %copy-start.8 = (f32[2]{0:T(128)S(1)}, f32[2]{0:T(128)}, u32[]{:S(2)}) copy-start(f32[2]{0:T(128)} %high.1) | copy-start | bytes 28
